TPU v7x, 128 devices: a whole 4x4x4 slice. The times are simulated.
128 devices in a mesh: grp: 8 (over y, core), mem: 16 (over z, x).
Axes of the slice: x: 4, y: 4, z: 4, core: 2. Of those that a mesh axis runs over, the one named last changes fastest.
Arguments:
- coefficients: float32 [8, 240, 16384], P(None, None, ('grp', 'mem')), may hold values from -6 to 6
- incident: float32 [8, 240, 16384], P(None, None, ('grp', 'mem')), may hold values from -6 to 6
- mie_coeffs: float32 [2, 240], replicated, may hold values from -0.8 to 0.8
- rot_table: bfloat16 [8, 240, 240], replicated, may hold values from -0.375 to 0.375
- axial_shells: bfloat16 [3, 2, 240, 240], replicated, may hold values from -0.1875 to 0.1875
- up_axial: bfloat16 [2, 240, 240], replicated, may hold values from -0.1875 to 0.1875
- far_axial: bfloat16 [2, 240, 240], replicated, may hold values from -0.0625 to 0.0625
- coupling: float32 [256, 256], replicated, may hold values from 0.01 to 0.1
- cluster_ids: int32 [16384], P(('grp', 'mem')), may hold values from 0 to 31
- center_rot: int32 [16384], P(('grp', 'mem')), may hold values from 0 to 7
- pair_col: int32 [24, 16384], P(None, ('grp', 'mem')), may hold values from -1 to 1407, as said below
- pair_rot: int32 [24, 16384], P(None, ('grp', 'mem')), may hold values from -1 to 7, as said below
- send_col: int32 [768, 64], P(('grp', 'mem')), may hold values from 0 to 1023, as said below
Outputs:
- updated: float32 [8, 240, 16384], P(None, None, ('grp', 'mem'))
Inputs may be any that keep to these rules, and one draw needn't show every extreme that they name: `pair_col`: -1 marks an empty slot; a value below 1024 is r * 128 + j for the own device's sphere j rotated by entry r; a larger one is 1024 + p * 64 + c for the c-th column sent to this device by its neighbour p; every such received column is named by some slot of the receiving device. `pair_rot`: -1 exactly in empty slots; otherwise the table entry with which the slot's column was rotated. `send_col`: row d * 6 + p lists the pool columns r * 128 + j that device d provides to the device whose neighbour p it is.
All inputs are finite; a program needn't handle non-finite values.
Results may differ from a plain program's by a relative error of at most 0.0038.
The roundings to bfloat16 on the way count: a program that leaves them out, or rounds other values in their place, can miss the bound.
Values may be sent and summed in bfloat16 or wider, within the bound.
No kernel may reach another device: no remote copies, remote signals or barrier semaphores. Data moves between devices by JAX's collectives and lax.ppermute only.
A program may use at most 128 MiB of HBM per device.

v0:
```python
import jax
import jax.numpy as jnp
from jax import lax
from jax.experimental import pallas as pl
from jax.experimental.pallas import tpu as pltpu
from jax.sharding import PartitionSpec as P

BF = jnp.bfloat16
F32 = jnp.float32
I32 = jnp.int32
VM = pl.BlockSpec(memory_space=pltpu.VMEM)


def nn_dot(a, b):
    return lax.dot_general(a, b, (((1,), (0,)), ((), ())), preferred_element_type=F32)


def iota(shape, dim):
    return lax.broadcasted_iota(I32, shape, dim)


def shifted(value, axis, by):
    length = lax.axis_size(axis)
    return lax.ppermute(value, axis, [(i, (i + by) % length) for i in range(length)])


def packed_complex(mat, cols):
    k = mat.shape[0] // 2
    both = nn_dot(mat, cols)
    sign = jnp.where(iota((k, 128), 1) < 64, -1.0, 1.0).astype(F32)
    return both[:k] + pltpu.roll(both[k:], 64, 1) * sign


def send_kernel(n_mem, coef, rot, send, crot, cid, up, pool, *rest):
    outs = rest[:6]
    far, xs, sel = rest[6:]
    n_x, n_k, n_i = coef.shape
    n_r = rot.shape[0]
    for x in range(n_x):
        xs[:, x * n_i : (x + 1) * n_i] = coef[x].astype(BF)
    x_all = xs[...]
    for r in range(n_r):
        turned = nn_dot(rot[r], x_all).astype(BF)
        for x in range(n_x):
            pool[x * n_k : (x + 1) * n_k, r * n_i : (r + 1) * n_i] = turned[
                :, x * n_i : (x + 1) * n_i
            ]
    rows = iota((n_r * n_i, 128), 0)
    for q in range(3):
        ids = jnp.concatenate([send[2 * q : 2 * q + 1, :], send[2 * q + 1 : 2 * q + 2, :]], axis=1)
        sel[:, q * 128 : (q + 1) * 128] = jnp.where(rows == ids, 1.0, 0.0).astype(BF)
    key = (crot[...] * 32 + cid[...]).astype(F32)
    key_t = jnp.transpose(jnp.broadcast_to(key, (n_i, n_i)))
    lanes = iota((n_i, n_i), 1)
    for r in range(n_r):
        hit = (key_t == (lanes + r * 32).astype(F32)) & (lanes < 32)
        sel[r * n_i : (r + 1) * n_i, 384:512] = jnp.where(hit, 1.0, 0.0).astype(BF)
    half = n_x // 2 * n_k
    real = nn_dot(pool[:half, :], sel[...])
    imag = nn_dot(pool[half:, :], sel[...])
    low = iota((half, 128), 1) < 64
    for q in range(3):
        re = real[:, q * 128 : (q + 1) * 128]
        im = imag[:, q * 128 : (q + 1) * 128]
        outs[2 * q][...] = jnp.where(low, re, pltpu.roll(im, 64, 1)).astype(BF)
        outs[2 * q + 1][...] = jnp.where(low, pltpu.roll(re, 64, 1), im).astype(BF)
    me = lax.axis_index("mem")
    chunk = 32
    far[lax.rem(2 * n_mem - 1 - me, n_mem)] = jnp.zeros((chunk, 128), F32)
    mat = up[...].reshape(2 * n_k, n_k)
    packed = []
    for xh in range(2):
        total = None
        for q in range(4):
            x = 2 * q + xh
            src = real if x < 4 else imag
            part = src[(x % 4) * n_k : (x % 4 + 1) * n_k, 384:512]
            part = pltpu.roll(part, 32 * q, 1) if q else part
            total = part if total is None else total + part
        hi = total.astype(BF)
        rem = total - hi.astype(F32)
        mid = rem.astype(BF)
        lo = (rem - mid.astype(F32)).astype(BF)
        packed.append(
            packed_complex(mat, lo) + packed_complex(mat, mid) + packed_complex(mat, hi)
        )
    whole = jnp.concatenate(packed, axis=0)
    for c in range(2 * n_k // chunk):
        far[lax.rem(n_mem + c - me, n_mem)] = whole[c * chunk : (c + 1) * chunk]


def own_kernel(pool, pcol, prot, axial, rot, g_out, sel_out, late_out, rt_out, mats, stack):
    r = pl.program_id(0)
    n_k = 240
    n_i = pcol.shape[1]

    @pl.when(r == 0)
    def _():
        mats[...] = jnp.zeros_like(mats)
        stack[...] = jnp.zeros_like(stack)
        for s in range(3):
            mats[:, s * 256 : s * 256 + n_k] = axial[s].reshape(2 * n_k, n_k)

    rt_out[...] = jnp.zeros_like(rt_out)
    rt_out[:, :n_k] = jnp.transpose(rot[0].astype(F32)).astype(BF)
    js = iota((n_i, n_i), 0)
    target = js + r * n_i
    counts = []
    for s in range(3):
        total = jnp.zeros((n_i, n_i), F32)
        for t in range(8):
            row = pcol[s * 8 + t : s * 8 + t + 1, :]
            total = total + jnp.where(row == target, 1.0, 0.0)
        counts.append(total.astype(BF))
    taken = nn_dot(pool[...], jnp.concatenate(counts, axis=1)).astype(BF)
    for s in range(3):
        for x in range(8):
            stack[s * 256 : s * 256 + n_k, x * n_i : (x + 1) * n_i] = taken[
                x * n_k : (x + 1) * n_k, s * n_i : (s + 1) * n_i
            ]
    both = nn_dot(mats[...], stack[...])
    half = 4 * n_i
    g_out[0, :, :half] = both[:n_k, :half] - both[n_k:, half:]
    g_out[0, :, half:] = both[n_k:, :half] + both[:n_k, half:]
    keys = jnp.where(pcol[...] >= 1024, pcol[...] - 1024 + prot[...] * 384, -1)
    for pb, pair in enumerate((0, 2, 1)):
        target = js + pair * 128 + r * 384
        for s in range(3):
            total = jnp.zeros((n_i, n_i), F32)
            for t in range(8):
                row = keys[s * 8 + t : s * 8 + t + 1, :]
                total = total + jnp.where(row == target, 1.0, 0.0)
            if pb < 2:
                at = (pb * 3 + s) * 128
                sel_out[at : at + 128, :] = total.astype(BF)
            else:
                late_out[s * 128 : (s + 1) * 128, :] = total.astype(BF)


def lift_pairs(pairs, axial, xs, moved):
    n_k = 240
    low = iota((n_k, 128), 1) < 64
    count = len(pairs)
    half = count * 512
    for j, (first, second) in enumerate(pairs):
        for d in range(4):
            a = first[d * n_k : (d + 1) * n_k, :].astype(F32)
            b = second[d * n_k : (d + 1) * n_k, :].astype(F32)
            at = (j * 4 + d) * 128
            xs[:, at : at + 128] = jnp.where(low, a, pltpu.roll(b, 64, 1)).astype(BF)
            xs[:, half + at : half + at + 128] = jnp.where(low, pltpu.roll(a, 64, 1), b).astype(BF)
    for s in range(3):
        both = nn_dot(axial[s].reshape(2 * n_k, n_k), xs[...])
        real = (both[:n_k, :half] - both[n_k:, half:]).astype(BF)
        imag = (both[n_k:, :half] + both[:n_k, half:]).astype(BF)
        for j in range(count):
            lane = (j * 3 + s) * 128
            for d in range(4):
                at = (j * 4 + d) * 128
                moved[d * n_k : (d + 1) * n_k, lane : lane + 128] = real[:, at : at + 128]
                moved[(4 + d) * n_k : (5 + d) * n_k, lane : lane + 128] = imag[:, at : at + 128]


def early_kernel(p0, p1, p4, p5, axial, sel, g_in, g_out, xs, moved):
    n_k = 240
    lift_pairs(((p0, p1), (p4, p5)), axial, xs, moved)
    for step in range(4):
        res = nn_dot(moved[...], sel[:, step * 256 : (step + 1) * 256])
        for rr in range(2):
            r = step * 2 + rr
            for x in range(8):
                g_out[r, :, x * 128 : (x + 1) * 128] = (
                    g_in[r, :, x * 128 : (x + 1) * 128]
                    + res[x * n_k : (x + 1) * n_k, rr * 128 : (rr + 1) * 128]
                )


def reach_kernel(blocks, coupling, out):
    me = lax.axis_index("grp")
    n_g = blocks.shape[0]
    rows = coupling[pl.ds(pl.multiple_of(me * 32, 32), 32), :]
    diag = iota((32, 256), 1) == iota((32, 256), 0) + me * 32
    rows = jnp.where(diag, 0.0, rows)
    lanes = iota((32, 128), 1)
    total = jnp.zeros((32, 128), F32)
    for gs in range(n_g):
        window = rows[:, gs // 4 * 128 : gs // 4 * 128 + 128]
        parts = []
        for q in range(4):
            by = (q * 32 - gs % 4 * 32) % 128
            moved = pltpu.roll(window, by, 1) if by else window
            parts.append(jnp.where((lanes >= q * 32) & (lanes < q * 32 + 32), moved, 0.0))
        mat = jnp.concatenate(parts, axis=0)
        block = blocks[lax.rem(n_g + me - gs, n_g)]
        total = total + lax.dot_general(
            block,
            mat,
            (((1,), (1,)), ((), ())),
            preferred_element_type=F32,
            precision=lax.Precision.HIGHEST,
        )
    out[...] = total.astype(BF)


def final_kernel(
    p2, p3, axial, sel, g_in, far_in, far_axial, cid, crot, rt, incident, mie, out,
    xs, moved, gb, fin, fsum
):
    n_k = 240
    n_mem = far_in.shape[0]
    lift_pairs(((p2, p3),), axial, xs, moved)
    me = lax.axis_index("mem")
    for c in range(n_mem):
        fin[c * 32 : (c + 1) * 32, :] = far_in[lax.rem(n_mem + me - c, n_mem)]
    mat = far_axial[...].reshape(2 * n_k, n_k)
    ids = jnp.broadcast_to(cid[...], (n_k, 128))
    for xh in range(2):
        cluster = packed_complex(mat, fin[xh * n_k : (xh + 1) * n_k, :])
        for q in range(4):
            fsum[2 * q + xh] = jnp.take_along_axis(cluster, ids + q * 32, axis=1)
    turn = jnp.broadcast_to(crot[...], (n_k, 128))
    pad = jnp.zeros((16, 1024), BF)
    for step in range(4):
        res = nn_dot(moved[...], sel[:, step * 256 : (step + 1) * 256])
        for rr in range(2):
            r = step * 2 + rr
            mine = turn == r
            for x in range(8):
                total = (
                    g_in[r, :, x * 128 : (x + 1) * 128]
                    + res[x * n_k : (x + 1) * n_k, rr * 128 : (rr + 1) * 128]
                    + jnp.where(mine, fsum[x], 0.0)
                )
                gb[r * 256 : r * 256 + n_k, x * 128 : (x + 1) * 128] = total.astype(BF)
            gb[r * 256 + n_k : (r + 1) * 256, :] = pad
    field = nn_dot(rt[...], gb[...])
    mie_re = jnp.transpose(jnp.broadcast_to(mie[0:1, :], (128, n_k)))
    mie_im = jnp.transpose(jnp.broadcast_to(mie[1:2, :], (128, n_k)))
    for d in range(4):
        re = incident[d] + field[:, d * 128 : (d + 1) * 128]
        im = incident[4 + d] + field[:, (4 + d) * 128 : (5 + d) * 128]
        out[d] = mie_re * re - mie_im * im
        out[4 + d] = mie_re * im + mie_im * re


def params(mib):
    return pltpu.CompilerParams(vmem_limit_bytes=mib << 20)


def on_device(
    coefficients,
    incident,
    mie_coeffs,
    rot_table,
    axial_shells,
    up_axial,
    far_axial,
    coupling,
    cluster_ids,
    center_rot,
    pair_col,
    pair_rot,
    send_col,
):
    sds = jax.ShapeDtypeStruct
    n_mem = lax.axis_size("mem")
    cid = cluster_ids.reshape(1, 128)
    crot = center_rot.reshape(1, 128)
    first = pl.pallas_call(
        lambda *refs: send_kernel(n_mem, *refs),
        out_shape=[sds((1920, 1024), BF)] + [sds((960, 128), BF)] * 6 + [sds((n_mem, 32, 128), F32)],
        in_specs=[VM] * 6,
        out_specs=[VM] * 8,
        scratch_shapes=[pltpu.VMEM((240, 1024), BF), pltpu.VMEM((1024, 512), BF)],
        compiler_params=params(40),
        name="send",
    )(coefficients, rot_table, send_col, crot, cid, up_axial)
    pool = first[0]
    sends = first[1:7]
    acc = first[7]
    moves = (("mem", 1), ("mem", -1), ("mem", 2), ("mem", -2), ("grp", 1), ("grp", -1))
    got = [None] * 6
    for p in (2, 3, 0, 1, 4, 5):
        got[p] = shifted(sends[p], *moves[p])
    size = n_mem // 2
    while size:
        acc = acc[:size] + shifted(acc[size:], "mem", size)
        size //= 2
    step = 1
    while step < lax.axis_size("grp"):
        acc = jnp.concatenate([acc, shifted(acc, "grp", step)], axis=0)
        step *= 2
    reached = pl.pallas_call(
        reach_kernel,
        out_shape=sds((32, 128), BF),
        in_specs=[VM] * 2,
        out_specs=VM,
        name="reach",
    )(acc, coupling)[None]
    step = 1
    while step < n_mem:
        reached = jnp.concatenate([reached, shifted(reached, "mem", step)], axis=0)
        step *= 2
    g_own, sel, sel_late, rt = pl.pallas_call(
        own_kernel,
        grid=(8,),
        out_shape=[sds((8, 240, 1024), F32), sds((768, 1024), BF), sds((384, 1024), BF), sds((240, 2048), BF)],
        in_specs=[
            pl.BlockSpec((1920, 128), lambda r: (0, r)),
            pl.BlockSpec((24, 128), lambda r: (0, 0)),
            pl.BlockSpec((24, 128), lambda r: (0, 0)),
            pl.BlockSpec((3, 2, 240, 240), lambda r: (0, 0, 0, 0)),
            pl.BlockSpec((1, 240, 240), lambda r: (r, 0, 0)),
        ],
        out_specs=[
            pl.BlockSpec((1, 240, 1024), lambda r: (r, 0, 0)),
            pl.BlockSpec((768, 128), lambda r: (0, r)),
            pl.BlockSpec((384, 128), lambda r: (0, r)),
            pl.BlockSpec((240, 256), lambda r: (0, r)),
        ],
        scratch_shapes=[pltpu.VMEM((480, 768), BF), pltpu.VMEM((768, 1024), BF)],
        compiler_params=params(40),
        name="own",
    )(pool, pair_col, pair_rot, axial_shells, rot_table)
    g_early = pl.pallas_call(
        early_kernel,
        out_shape=sds((8, 240, 1024), F32),
        in_specs=[VM] * 7,
        out_specs=VM,
        scratch_shapes=[pltpu.VMEM((240, 2048), BF), pltpu.VMEM((1920, 768), BF)],
        compiler_params=params(48),
        name="early",
    )(got[0], got[1], got[4], got[5], axial_shells, sel, g_own)
    return pl.pallas_call(
        final_kernel,
        out_shape=sds((8, 240, 128), F32),
        in_specs=[VM] * 12,
        out_specs=VM,
        scratch_shapes=[
            pltpu.VMEM((240, 1024), BF),
            pltpu.VMEM((1920, 384), BF),
            pltpu.VMEM((2048, 1024), BF),
            pltpu.VMEM((512, 128), BF),
            pltpu.VMEM((8, 240, 128), F32),
        ],
        compiler_params=params(48),
        name="final",
    )(
        got[2], got[3], axial_shells, sel_late, g_early, reached, far_axial, cid, crot, rt,
        incident, mie_coeffs,
    )


def solution(mesh):
    in_specs = (
        P(None, None, ("grp", "mem")),
        P(None, None, ("grp", "mem")),
        P(),
        P(),
        P(),
        P(),
        P(),
        P(),
        P(("grp", "mem")),
        P(("grp", "mem")),
        P(None, ("grp", "mem")),
        P(None, ("grp", "mem")),
        P(("grp", "mem"), None),
    )
    out_specs = P(None, None, ("grp", "mem"))
    return jax.shard_map(
        on_device, mesh=mesh, in_specs=in_specs, out_specs=out_specs, check_vma=False
    )
```

profile of v0, /device:TPU:0, one launch (start us, length us, event | category | flops | bytes accessed | tf_op | source)
XLA Modules:
  0.0 133.5 jit_solution(13751989216863006407)
XLA Ops:
  0.0 1.3 copy-done.2
  1.3 1.2 copy-done.3
  5.4 4.9 %send.1 = (bf16[1920,1024]{1,0:T(8,128)(2,1)S(1)}, bf16[960,128]{1,0:T(8,128)(2,1)S(1)}, bf16[960,128]{1,0:T(8,128)(2,1)S(1)}, bf16[960,128]{1,0:T(8,128)(2,1)},...) custom-call(f32[8,240,128]{2,1,0:T(8,128)S(1)} %copy-done.3, ...), custom_call_target="tpu_custom_call" | custom-call | tf_op jit(solution)/shard_map/send/pallas_call | solution.py:269
  10.4 4.1 %collective-permute-start.6 = (f32[8,32,128]{2,1,0:T(8,128)S(1)}, f32[8,32,128]{2,1,0:T(8,128)S(1)}, u32[]{:S(2)}, u32[]{:S(2)}) collective-permute-start(f32[8,32,128]{2,1,0:T(8,128)S(1)} %slice.25), channel_id=1, source_target_pairs={{0,8},{1,9},{2,10},{3,11},{4,12},{5,13},{6,14},{7,15},{8,0},{9,1},... | collective-permute-start | bytes 393224 | tf_op jit(solution)/shard_map/ppermute | solution.py:24
  14.4 3.5 %collective-permute-done.6 = f32[8,32,128]{2,1,0:T(8,128)S(1)} collective-permute-done((f32[8,32,128]{2,1,0:T(8,128)S(1)}, f32[8,32,128]{2,1,0:T(8,128)S(1)}, u32[]{:S(2)}, u32[]{:S(2)}) %collective-permute-start.6) | collective-permute-done | bytes 131104 | tf_op jit(solution)/shard_map/ppermute | solution.py:24
  18.0 1.4 %collective-permute-start.7 = (f32[4,32,128]{2,1,0:T(8,128)S(1)}, f32[4,32,128]{2,1,0:T(8,128)S(1)}, u32[]{:S(2)}, u32[]{:S(2)}) collective-permute-start(f32[4,32,128]{2,1,0:T(8,128)S(1)} %slice.33), channel_id=1, source_target_pairs={{0,4},{1,5},{2,6},{3,7},{4,8},{5,9},{6,10},{7,11},{8,12},{9,13},{1... | collective-permute-start | bytes 196616 | tf_op jit(solution)/shard_map/ppermute | solution.py:24
  19.3 4.4 %collective-permute-done.7 = f32[4,32,128]{2,1,0:T(8,128)S(1)} collective-permute-done((f32[4,32,128]{2,1,0:T(8,128)S(1)}, f32[4,32,128]{2,1,0:T(8,128)S(1)}, u32[]{:S(2)}, u32[]{:S(2)}) %collective-permute-start.7) | collective-permute-done | bytes 65568 | tf_op jit(solution)/shard_map/ppermute | solution.py:24
  23.7 3.1 %collective-permute-start.8 = (f32[2,32,128]{2,1,0:T(8,128)S(1)}, f32[2,32,128]{2,1,0:T(8,128)S(1)}, u32[]{:S(2)}, u32[]{:S(2)}) collective-permute-start(f32[2,32,128]{2,1,0:T(8,128)S(1)} %slice.35), channel_id=1, source_target_pairs={{0,2},{1,3},{2,4},{3,5},{4,6},{5,7},{6,8},{7,9},{8,10},{9,11},{10,... | collective-permute-start | bytes 98312 | tf_op jit(solution)/shard_map/ppermute | solution.py:24
  26.8 4.5 %collective-permute-done.8 = f32[2,32,128]{2,1,0:T(8,128)S(1)} collective-permute-done((f32[2,32,128]{2,1,0:T(8,128)S(1)}, f32[2,32,128]{2,1,0:T(8,128)S(1)}, u32[]{:S(2)}, u32[]{:S(2)}) %collective-permute-start.8) | collective-permute-done | bytes 32800 | tf_op jit(solution)/shard_map/ppermute | solution.py:24
  31.3 1.6 %collective-permute-start.9 = (f32[1,32,128]{2,1,0:T(8,128)S(1)}, f32[1,32,128]{2,1,0:T(8,128)S(1)}, u32[]{:S(2)}, u32[]{:S(2)}) collective-permute-start(f32[1,32,128]{2,1,0:T(8,128)S(1)} %slice.37), channel_id=1, source_target_pairs={{0,1},{1,2},{2,3},{3,4},{4,5},{5,6},{6,7},{7,8},{8,9},{9,10},{10,1... | collective-permute-start | bytes 49160 | tf_op jit(solution)/shard_map/ppermute | solution.py:24
  32.9 5.6 %collective-permute-done.9 = f32[1,32,128]{2,1,0:T(8,128)S(1)} collective-permute-done((f32[1,32,128]{2,1,0:T(8,128)S(1)}, f32[1,32,128]{2,1,0:T(8,128)S(1)}, u32[]{:S(2)}, u32[]{:S(2)}) %collective-permute-start.9) | collective-permute-done | bytes 16416 | tf_op jit(solution)/shard_map/ppermute | solution.py:24
  38.5 5.3 %collective-permute-start.3 = (bf16[960,128]{1,0:T(8,128)(2,1)S(1)}, bf16[960,128]{1,0:T(8,128)(2,1)S(1)}, u32[]{:S(2)}, u32[]{:S(2)}) collective-permute-start(bf16[960,128]{1,0:T(8,128)(2,1)S(1)} %get-tuple-element.22), channel_id=1, source_target_pairs={{0,15},{1,0},{2,1},{3,2},{4,3},{5,4},{6,5},{7,6},{8,7},{9,8},{10,9... | collective-permute-start | bytes 737288 | tf_op jit(solution)/shard_map/ppermute | solution.py:24
  44.9 1.9 %collective-permute-start.5 = (bf16[960,128]{1,0:T(8,128)(2,1)S(1)}, bf16[960,128]{1,0:T(8,128)(2,1)S(1)}, u32[]{:S(2)}, u32[]{:S(2)}) collective-permute-start(bf16[960,128]{1,0:T(8,128)(2,1)S(1)} %get-tuple-element.24), channel_id=1, source_target_pairs={{0,112},{16,0},{32,16},{48,32},{64,48},{80,64},{96,80},{112,96},{1... | collective-permute-start | bytes 737288 | tf_op jit(solution)/shard_map/ppermute | solution.py:24
  47.2 4.8 %collective-permute-done.11 = f32[2,32,128]{2,1,0:T(8,128)S(1)} collective-permute-done((f32[2,32,128]{2,1,0:T(8,128)S(1)}, f32[2,32,128]{2,1,0:T(8,128)S(1)}, u32[]{:S(2)}, u32[]{:S(2)}) %collective-permute-start.11) | collective-permute-done | bytes 32800 | tf_op jit(solution)/shard_map/ppermute | solution.py:24
  52.0 1.1 collective-permute-start.12
  55.6 18.3 %own.1 = (f32[8,240,1024]{2,1,0:T(8,128)}, bf16[768,1024]{1,0:T(8,128)(2,1)S(1)}, bf16[384,1024]{1,0:T(8,128)(2,1)S(1)}, bf16[240,2048]{1,0:T(8,128)(2,1)S(1)}) custom-call(bf16[1920,1024]{1,0:T(8,128)(2,1)S(1)} %get-tuple-element.19.pool, s32[24,128]{1,0:T(8,128)S(1)} %copy-done.7, s32[24,128]{1,0:T(8,128)S(1)} %copy-done.8, ...), custom_call_target="tpu_custom_call" | custom-call | tf_op jit(solution)/shard_map/own/pallas_call | solution.py:304
  74.0 5.6 %collective-permute-start.1 = (bf16[960,128]{1,0:T(8,128)(2,1)}, bf16[960,128]{1,0:T(8,128)(2,1)}, u32[]{:S(2)}, u32[]{:S(2)}) collective-permute-start(bf16[960,128]{1,0:T(8,128)(2,1)} %get-tuple-element.18), channel_id=1, source_target_pairs={{0,14},{1,15},{2,0},{3,1},{4,2},{5,3},{6,4},{7,5},{8,6},{9,7},{10,... | collective-permute-start | bytes 737288 | tf_op jit(solution)/shard_map/ppermute | solution.py:24
  79.7 12.4 %early.1.g_in = f32[8,240,1024]{2,1,0:T(8,128)} custom-call(bf16[960,128]{1,0:T(8,128)(2,1)S(1)} %collective-permute-done.2.p0, bf16[960,128]{1,0:T(8,128)(2,1)S(1)} %collective-permute-done.3.p1, bf16[960,128]{1,0:T(8,128)(2,1)S(1)} %collective-permute-done.4.p4, bf16[960,128]{1,0:T(8,128)(2,1)S(1)} %collective-permute-done.5.p5, ...), custom_call_target="tpu_custom_call" | custom-call | tf_op jit(solution)/shard_map/early/pallas_call | solution.py:325
  92.7 2.6 %reach.1 = bf16[32,128]{1,0:T(8,128)(2,1)} custom-call(f32[8,32,128]{2,1,0:T(8,128)} %pad_maximum_fusion.blocks, f32[256,256]{1,0:T(8,128)} %coupling.1), custom_call_target="tpu_custom_call" | custom-call | tf_op jit(solution)/shard_map/reach/pallas_call | solution.py:293
  96.1 6.4 %collective-permute-done.13 = bf16[1,32,128]{2,1,0:T(8,128)(2,1)S(1)} collective-permute-done((bf16[1,32,128]{2,1,0:T(8,128)(2,1)}, bf16[1,32,128]{2,1,0:T(8,128)(2,1)S(1)}, u32[]{:S(2)}, u32[]{:S(2)}) %collective-permute-start.13) | collective-permute-done | bytes 8224 | tf_op jit(solution)/shard_map/ppermute | solution.py:24
  103.2 7.3 %collective-permute-done.14 = bf16[2,32,128]{2,1,0:T(8,128)(2,1)S(1)} collective-permute-done((bf16[2,32,128]{2,1,0:T(8,128)(2,1)S(1)}, bf16[2,32,128]{2,1,0:T(8,128)(2,1)S(1)}, u32[]{:S(2)}, u32[]{:S(2)}) %collective-permute-start.14) | collective-permute-done | bytes 16416 | tf_op jit(solution)/shard_map/ppermute | solution.py:24
  111.3 5.1 %collective-permute-done.15 = bf16[4,32,128]{2,1,0:T(8,128)(2,1)S(1)} collective-permute-done((bf16[4,32,128]{2,1,0:T(8,128)(2,1)S(1)}, bf16[4,32,128]{2,1,0:T(8,128)(2,1)S(1)}, u32[]{:S(2)}, u32[]{:S(2)}) %collective-permute-start.15) | collective-permute-done | bytes 32800 | tf_op jit(solution)/shard_map/ppermute | solution.py:24
  117.2 5.7 %collective-permute-done.16 = bf16[8,32,128]{2,1,0:T(8,128)(2,1)S(1)} collective-permute-done((bf16[8,32,128]{2,1,0:T(8,128)(2,1)S(1)}, bf16[8,32,128]{2,1,0:T(8,128)(2,1)S(1)}, u32[]{:S(2)}, u32[]{:S(2)}) %collective-permute-start.16) | collective-permute-done | bytes 65568 | tf_op jit(solution)/shard_map/ppermute | solution.py:24
  124.0 9.5 %final.1 = f32[8,240,128]{2,1,0:T(8,128)} custom-call(bf16[960,128]{1,0:T(8,128)(2,1)} %collective-permute-done.p2, bf16[960,128]{1,0:T(8,128)(2,1)} %collective-permute-done.1.p3, bf16[3,2,240,240]{3,2,1,0:T(8,128)(2,1)S(1)} %copy-done.1, bf16[384,1024]{1,0:T(8,128)(2,1)S(1)} %get-tuple-element.20.sel, f32[8,240,1024]{2,1,0:T(8,128)} %early.1.g_in, ...), custom_call_target="tpu_custom_call" | custom-call | tf_op jit(solution)/shard_map/final/pallas_call | solution.py:334
  (64 shorter events, 11.7 us)
Async XLA Ops:
  0.0 79.6 %copy-start.1 = (bf16[3,2,240,240]{3,2,1,0:T(8,128)(2,1)S(1)}, bf16[3,2,240,240]{3,2,1,0:T(8,128)(2,1)}, u32[]{:S(2)}) copy-start(bf16[3,2,240,240]{3,2,1,0:T(8,128)(2,1)} %axial.5) | copy-start | bytes 2073604
  0.0 1.3 copy-start.2
  1.3 1.2 copy-start.3
  10.4 7.6 %collective-permute-start.6 = (f32[8,32,128]{2,1,0:T(8,128)S(1)}, f32[8,32,128]{2,1,0:T(8,128)S(1)}, u32[]{:S(2)}, u32[]{:S(2)}) collective-permute-start(f32[8,32,128]{2,1,0:T(8,128)S(1)} %slice.25), channel_id=1, source_target_pairs={{0,8},{1,9},{2,10},{3,11},{4,12},{5,13},{6,14},{7,15},{8,0},{9,1},... | collective-permute-start | bytes 393224 | tf_op jit(solution)/shard_map/ppermute | solution.py:24
  18.0 5.7 %collective-permute-start.7 = (f32[4,32,128]{2,1,0:T(8,128)S(1)}, f32[4,32,128]{2,1,0:T(8,128)S(1)}, u32[]{:S(2)}, u32[]{:S(2)}) collective-permute-start(f32[4,32,128]{2,1,0:T(8,128)S(1)} %slice.33), channel_id=1, source_target_pairs={{0,4},{1,5},{2,6},{3,7},{4,8},{5,9},{6,10},{7,11},{8,12},{9,13},{1... | collective-permute-start | bytes 196616 | tf_op jit(solution)/shard_map/ppermute | solution.py:24
  23.7 7.6 %collective-permute-start.8 = (f32[2,32,128]{2,1,0:T(8,128)S(1)}, f32[2,32,128]{2,1,0:T(8,128)S(1)}, u32[]{:S(2)}, u32[]{:S(2)}) collective-permute-start(f32[2,32,128]{2,1,0:T(8,128)S(1)} %slice.35), channel_id=1, source_target_pairs={{0,2},{1,3},{2,4},{3,5},{4,6},{5,7},{6,8},{7,9},{8,10},{9,11},{10,... | collective-permute-start | bytes 98312 | tf_op jit(solution)/shard_map/ppermute | solution.py:24
  31.3 7.1 %collective-permute-start.9 = (f32[1,32,128]{2,1,0:T(8,128)S(1)}, f32[1,32,128]{2,1,0:T(8,128)S(1)}, u32[]{:S(2)}, u32[]{:S(2)}) collective-permute-start(f32[1,32,128]{2,1,0:T(8,128)S(1)} %slice.37), channel_id=1, source_target_pairs={{0,1},{1,2},{2,3},{3,4},{4,5},{5,6},{6,7},{7,8},{8,9},{9,10},{10,1... | collective-permute-start | bytes 49160 | tf_op jit(solution)/shard_map/ppermute | solution.py:24
  38.4 8.4 %collective-permute-start.10 = (f32[1,32,128]{2,1,0:T(8,128)S(1)}, f32[1,32,128]{2,1,0:T(8,128)S(1)}, u32[]{:S(2)}, u32[]{:S(2)}) collective-permute-start(f32[1,32,128]{2,1,0:T(8,128)S(1)} %slice_add_fusion.3), channel_id=1, source_target_pairs={{0,16},{16,32},{32,48},{48,64},{64,80},{80,96},{96,112},{112,0},{1... | collective-permute-start | bytes 49160 | tf_op jit(solution)/shard_map/ppermute | solution.py:24
  38.5 35.5 %collective-permute-start.2 = (bf16[960,128]{1,0:T(8,128)(2,1)S(1)}, bf16[960,128]{1,0:T(8,128)(2,1)S(1)}, u32[]{:S(2)}, u32[]{:S(2)}) collective-permute-start(bf16[960,128]{1,0:T(8,128)(2,1)S(1)} %get-tuple-element.21), channel_id=1, source_target_pairs={{0,1},{1,2},{2,3},{3,4},{4,5},{5,6},{6,7},{7,8},{8,9},{9,10},{10,1... | collective-permute-start | bytes 737288 | tf_op jit(solution)/shard_map/ppermute | solution.py:24
  38.5 35.4 %collective-permute-start.3 = (bf16[960,128]{1,0:T(8,128)(2,1)S(1)}, bf16[960,128]{1,0:T(8,128)(2,1)S(1)}, u32[]{:S(2)}, u32[]{:S(2)}) collective-permute-start(bf16[960,128]{1,0:T(8,128)(2,1)S(1)} %get-tuple-element.22), channel_id=1, source_target_pairs={{0,15},{1,0},{2,1},{3,2},{4,3},{5,4},{6,5},{7,6},{8,7},{9,8},{10,9... | collective-permute-start | bytes 737288 | tf_op jit(solution)/shard_map/ppermute | solution.py:24
  43.9 35.7 %collective-permute-start.4 = (bf16[960,128]{1,0:T(8,128)(2,1)S(1)}, bf16[960,128]{1,0:T(8,128)(2,1)S(1)}, u32[]{:S(2)}, u32[]{:S(2)}) collective-permute-start(bf16[960,128]{1,0:T(8,128)(2,1)S(1)} %get-tuple-element.23), channel_id=1, source_target_pairs={{0,16},{16,32},{32,48},{48,64},{64,80},{80,96},{96,112},{112,0},{1... | collective-permute-start | bytes 737288 | tf_op jit(solution)/shard_map/ppermute | solution.py:24
  44.9 34.7 %collective-permute-start.5 = (bf16[960,128]{1,0:T(8,128)(2,1)S(1)}, bf16[960,128]{1,0:T(8,128)(2,1)S(1)}, u32[]{:S(2)}, u32[]{:S(2)}) collective-permute-start(bf16[960,128]{1,0:T(8,128)(2,1)S(1)} %get-tuple-element.24), channel_id=1, source_target_pairs={{0,112},{16,0},{32,16},{48,32},{64,48},{80,64},{96,80},{112,96},{1... | collective-permute-start | bytes 737288 | tf_op jit(solution)/shard_map/ppermute | solution.py:24
  46.8 5.1 %collective-permute-start.11 = (f32[2,32,128]{2,1,0:T(8,128)S(1)}, f32[2,32,128]{2,1,0:T(8,128)S(1)}, u32[]{:S(2)}, u32[]{:S(2)}) collective-permute-start(f32[2,32,128]{2,1,0:T(8,128)S(1)} %pad_maximum_fusion.3), channel_id=1, source_target_pairs={{0,32},{16,48},{32,64},{48,80},{64,96},{80,112},{96,0},{112,16},{1... | collective-permute-start | bytes 98312 | tf_op jit(solution)/shard_map/ppermute | solution.py:24
  52.0 40.1 %collective-permute-start.12 = (f32[4,32,128]{2,1,0:T(8,128)S(1)}, f32[4,32,128]{2,1,0:T(8,128)S(1)}, u32[]{:S(2)}, u32[]{:S(2)}) collective-permute-start(f32[4,32,128]{2,1,0:T(8,128)S(1)} %pad_maximum_fusion.1), channel_id=1, source_target_pairs={{0,64},{16,80},{32,96},{48,112},{64,0},{80,16},{96,32},{112,48},{1... | collective-permute-start | bytes 196616 | tf_op jit(solution)/shard_map/ppermute | solution.py:24
  74.0 49.0 %collective-permute-start = (bf16[960,128]{1,0:T(8,128)(2,1)}, bf16[960,128]{1,0:T(8,128)(2,1)}, u32[]{:S(2)}, u32[]{:S(2)}) collective-permute-start(bf16[960,128]{1,0:T(8,128)(2,1)} %get-tuple-element.17), channel_id=1, source_target_pairs={{0,2},{1,3},{2,4},{3,5},{4,6},{5,7},{6,8},{7,9},{8,10},{9,11},{10,... | collective-permute-start | bytes 737288 | tf_op jit(solution)/shard_map/ppermute | solution.py:24
  74.0 49.0 %collective-permute-start.1 = (bf16[960,128]{1,0:T(8,128)(2,1)}, bf16[960,128]{1,0:T(8,128)(2,1)}, u32[]{:S(2)}, u32[]{:S(2)}) collective-permute-start(bf16[960,128]{1,0:T(8,128)(2,1)} %get-tuple-element.18), channel_id=1, source_target_pairs={{0,14},{1,15},{2,0},{3,1},{4,2},{5,3},{6,4},{7,5},{8,6},{9,7},{10,... | collective-permute-start | bytes 737288 | tf_op jit(solution)/shard_map/ppermute | solution.py:24
  79.6 43.4 %copy-start.4 = (f32[8,240,128]{2,1,0:T(8,128)S(1)}, f32[8,240,128]{2,1,0:T(8,128)}, u32[]{:S(2)}) copy-start(f32[8,240,128]{2,1,0:T(8,128)} %incident.1) | copy-start | bytes 2949124
  79.6 43.4 %copy-start.10 = (f32[2,240]{1,0:T(2,128)S(1)}, f32[2,240]{1,0:T(2,128)}, u32[]{:S(2)}) copy-start(f32[2,240]{1,0:T(2,128)} %mie.1) | copy-start | bytes 5764
  79.6 43.4 %copy-start.12 = (s32[128]{0:T(128)S(1)}, s32[128]{0:T(128)}, u32[]{:S(2)}) copy-start(s32[128]{0:T(128)} %param.22) | copy-start | bytes 1540
  79.7 43.4 %copy-start.14 = (s32[128]{0:T(128)S(1)}, s32[128]{0:T(128)}, u32[]{:S(2)}) copy-start(s32[128]{0:T(128)} %param.21) | copy-start | bytes 1540
  95.3 7.2 %collective-permute-start.13 = (bf16[1,32,128]{2,1,0:T(8,128)(2,1)}, bf16[1,32,128]{2,1,0:T(8,128)(2,1)S(1)}, u32[]{:S(2)}, u32[]{:S(2)}) collective-permute-start(bf16[1,32,128]{2,1,0:T(8,128)(2,1)} %bitcast.8), channel_id=1, source_target_pairs={{0,1},{1,2},{2,3},{3,4},{4,5},{5,6},{6,7},{7,8},{8,9},{9,10},{10,1... | collective-permute-start | bytes 24584 | tf_op jit(solution)/shard_map/ppermute | solution.py:24
  103.2 7.4 %collective-permute-start.14 = (bf16[2,32,128]{2,1,0:T(8,128)(2,1)S(1)}, bf16[2,32,128]{2,1,0:T(8,128)(2,1)S(1)}, u32[]{:S(2)}, u32[]{:S(2)}) collective-permute-start(bf16[2,32,128]{2,1,0:T(8,128)(2,1)S(1)} %pad_maximum_fusion.5), channel_id=1, source_target_pairs={{0,2},{1,3},{2,4},{3,5},{4,6},{5,7},{6,8},{7,9},{8,10},{9,11},{10,... | collective-permute-start | bytes 49160 | tf_op jit(solution)/shard_map/ppermute | solution.py:24
  111.3 5.1 %collective-permute-start.15 = (bf16[4,32,128]{2,1,0:T(8,128)(2,1)S(1)}, bf16[4,32,128]{2,1,0:T(8,128)(2,1)S(1)}, u32[]{:S(2)}, u32[]{:S(2)}) collective-permute-start(bf16[4,32,128]{2,1,0:T(8,128)(2,1)S(1)} %pad_maximum_fusion.4), channel_id=1, source_target_pairs={{0,4},{1,5},{2,6},{3,7},{4,8},{5,9},{6,10},{7,11},{8,12},{9,13},{1... | collective-permute-start | bytes 98312 | tf_op jit(solution)/shard_map/ppermute | solution.py:24
  117.1 5.8 %collective-permute-start.16 = (bf16[8,32,128]{2,1,0:T(8,128)(2,1)S(1)}, bf16[8,32,128]{2,1,0:T(8,128)(2,1)S(1)}, u32[]{:S(2)}, u32[]{:S(2)}) collective-permute-start(bf16[8,32,128]{2,1,0:T(8,128)(2,1)S(1)} %pad_maximum_fusion.2), channel_id=1, source_target_pairs={{0,8},{1,9},{2,10},{3,11},{4,12},{5,13},{6,14},{7,15},{8,0},{9,1},... | collective-permute-start | bytes 196616 | tf_op jit(solution)/shard_map/ppermute | solution.py:24
  (8 other events, 6.4 us)
where the time goes:
time: 134 us
  Pallas kernels  47.8 us (36%)
  waiting for transfers between devices  47.4 us (35%)
  starting transfers between devices  25.7 us (19%)
  local copies, waits for them, and re-layouts  9.7 us (7%)
  other arithmetic  2.82 us (2%)
    ppermute x17, waiting for transfers between devices, shifted(): lax.ppermute(value, axis, [(i, (i + by) % length) for i in range(length)])  47.4 us
    ppermute x17, starting transfers between devices, shifted(): lax.ppermute(value, axis, [(i, (i + by) % length) for i in range(length)])  25.7 us
    pallas_call x1, Pallas kernels, on_device(): pl.pallas_call(own_kernel, grid=(8,), out_shape=[sds((8, 240, 1024), F32)...  18.3 us
    pallas_call x1, Pallas kernels, on_device(): pl.pallas_call(early_kernel, out_shape=sds((8, 240, 1024), F32), in_specs...  12.4 us
    unnamed x34, local copies, waits for them, and re-layouts  9.67 us
    pallas_call x1, Pallas kernels, on_device(): pl.pallas_call(final_kernel, out_shape=sds((8, 240, 128), F32), in_specs=...  9.54 us
    pallas_call x1, Pallas kernels, on_device(): pl.pallas_call(lambda *refs: send_kernel(n_mem, *refs), out_shape=[sds((1...  4.92 us
  transfers between devices with their start and end apart: 17, of which 9 were waited for; matrix products, arithmetic and copies ran while one was open for 3% of the time, Pallas kernels for 25%

commit v1 on v0

v1 whole, which is shorter than its diff:
```python
import jax
import jax.numpy as jnp
from jax import lax
from jax.experimental import pallas as pl
from jax.experimental.pallas import tpu as pltpu
from jax.sharding import PartitionSpec as P


BF = jnp.bfloat16
F32 = jnp.float32
I32 = jnp.int32
VM = pl.BlockSpec(memory_space=pltpu.VMEM)


def nn_dot(a, b):
    return lax.dot_general(a, b, (((1,), (0,)), ((), ())), preferred_element_type=F32)


def iota(shape, dim):
    return lax.broadcasted_iota(I32, shape, dim)


def shifted(value, axis, by):
    length = lax.axis_size(axis)
    return lax.ppermute(value, axis, [(i, (i + by) % length) for i in range(length)])


def packed_complex(mat, cols):
    k = mat.shape[0] // 2
    both = nn_dot(mat, cols)
    sign = jnp.where(iota((k, 128), 1) < 64, -1.0, 1.0).astype(F32)
    return both[:k] + pltpu.roll(both[k:], 64, 1) * sign


def send_kernel(n_mem, coef_h, rot_h, send_h, crot_h, cid_h, up_h, *rest):
    pools = rest[:8]
    outs = rest[8:14]
    far, coef, rot, send, crot, cid, up, xs, sel, sems = rest[14:]
    pairs = ((coef_h, coef), (rot_h, rot), (send_h, send), (crot_h, crot), (cid_h, cid), (up_h, up))
    copies = [pltpu.make_async_copy(src, dst, sems.at[i]) for i, (src, dst) in enumerate(pairs)]
    for copy in copies:
        copy.start()
    n_x, n_k, n_i = coef.shape
    n_r = rot.shape[0]
    for i in (2, 3, 4):
        copies[i].wait()
    rows = iota((n_r * n_i, 128), 0)
    for q in range(3):
        ids = jnp.concatenate([send[2 * q : 2 * q + 1, :], send[2 * q + 1 : 2 * q + 2, :]], axis=1)
        sel[:, q * 128 : (q + 1) * 128] = jnp.where(rows == ids, 1.0, 0.0).astype(BF)
    key = (crot[...] * 32 + cid[...]).astype(F32)
    key_t = jnp.transpose(jnp.broadcast_to(key, (n_i, n_i)))
    lanes = iota((n_i, n_i), 1)
    for r in range(n_r):
        hit = (key_t == (lanes + r * 32).astype(F32)) & (lanes < 32)
        sel[r * n_i : (r + 1) * n_i, 384:512] = jnp.where(hit, 1.0, 0.0).astype(BF)
    for i in (0, 1, 5):
        copies[i].wait()
    for x in range(n_x):
        xs[:, x * n_i : (x + 1) * n_i] = coef[x].astype(BF)
    x_all = xs[...]
    for r in range(n_r):
        turned = nn_dot(rot[r], x_all).astype(BF)
        for x in range(n_x):
            pools[r][x * n_k : (x + 1) * n_k, :] = turned[:, x * n_i : (x + 1) * n_i]
    half = n_x // 2 * n_k
    real = nn_dot(jnp.concatenate([p[:half, :] for p in pools], axis=1), sel[...])
    imag = nn_dot(jnp.concatenate([p[half:, :] for p in pools], axis=1), sel[...])
    low = iota((half, 128), 1) < 64
    for q in range(3):
        re = real[:, q * 128 : (q + 1) * 128]
        im = imag[:, q * 128 : (q + 1) * 128]
        outs[2 * q][...] = jnp.where(low, re, pltpu.roll(im, 64, 1)).astype(BF)
        outs[2 * q + 1][...] = jnp.where(low, pltpu.roll(re, 64, 1), im).astype(BF)
    me = lax.axis_index("mem")
    chunk = 32
    far[lax.rem(2 * n_mem - 1 - me, n_mem)] = jnp.zeros((chunk, 128), F32)
    mat = up[...].reshape(2 * n_k, n_k)
    packed = []
    for xh in range(2):
        total = None
        for q in range(4):
            x = 2 * q + xh
            src = real if x < 4 else imag
            part = src[(x % 4) * n_k : (x % 4 + 1) * n_k, 384:512]
            part = pltpu.roll(part, 32 * q, 1) if q else part
            total = part if total is None else total + part
        hi = total.astype(BF)
        rem = total - hi.astype(F32)
        mid = rem.astype(BF)
        lo = (rem - mid.astype(F32)).astype(BF)
        packed.append(
            packed_complex(mat, lo) + packed_complex(mat, mid) + packed_complex(mat, hi)
        )
    whole = jnp.concatenate(packed, axis=0)
    for c in range(2 * n_k // chunk):
        far[lax.rem(n_mem + c - me, n_mem)] = whole[c * chunk : (c + 1) * chunk]


def own_kernel(r, *refs):
    if r == 0:
        pool, pcol, prot, rot, axial, g_out, sel_out, rt_out, mats, stack = refs
    else:
        pool, pcol, prot, rot, mats, g_out, sel_out, rt_out, stack = refs
    n_k = 240
    n_i = pcol.shape[1]
    if r == 0:
        mats[...] = jnp.zeros_like(mats)
        for s in range(3):
            mats[:, s * 256 : s * 256 + n_k] = axial[s].reshape(2 * n_k, n_k)
    for s in range(3):
        stack[s * 256 + n_k : (s + 1) * 256, :] = jnp.zeros((16, 8 * n_i), BF)
    rt_out[...] = jnp.zeros_like(rt_out)
    rt_out[:, :n_k] = jnp.transpose(rot[r].astype(F32)).astype(BF)
    js = iota((n_i, n_i), 0)
    counts = []
    for s in range(3):
        total = jnp.zeros((n_i, n_i), F32)
        for t in range(8):
            row = pcol[s * 8 + t : s * 8 + t + 1, :]
            total = total + jnp.where(row == js + r * n_i, 1.0, 0.0)
        counts.append(total.astype(BF))
    taken = nn_dot(pool[...], jnp.concatenate(counts, axis=1)).astype(BF)
    for s in range(3):
        for x in range(8):
            stack[s * 256 : s * 256 + n_k, x * n_i : (x + 1) * n_i] = taken[
                x * n_k : (x + 1) * n_k, s * n_i : (s + 1) * n_i
            ]
    both = nn_dot(mats[...], stack[...])
    half = 4 * n_i
    g_out[:, :half] = both[:n_k, :half] - both[n_k:, half:]
    g_out[:, half:] = both[n_k:, :half] + both[:n_k, half:]
    keys = jnp.where(pcol[...] >= 1024, pcol[...] - 1024 + prot[...] * 384, -1)
    for pair in range(3):
        for s in range(3):
            total = jnp.zeros((n_i, n_i), F32)
            for t in range(8):
                row = keys[s * 8 + t : s * 8 + t + 1, :]
                total = total + jnp.where(row == js + pair * 128 + r * 384, 1.0, 0.0)
            at = (pair * 3 + s) * 128
            sel_out[at : at + 128, :] = total.astype(BF)


def lift_kernel(first, second, axial, moved, xs):
    n_k = 240
    low = iota((n_k, 128), 1) < 64
    for d in range(4):
        a = first[d * n_k : (d + 1) * n_k, :].astype(F32)
        b = second[d * n_k : (d + 1) * n_k, :].astype(F32)
        at = d * 128
        xs[:, at : at + 128] = jnp.where(low, a, pltpu.roll(b, 64, 1)).astype(BF)
        xs[:, 512 + at : 512 + at + 128] = jnp.where(low, pltpu.roll(a, 64, 1), b).astype(BF)
    for s in range(3):
        both = nn_dot(axial[s].reshape(2 * n_k, n_k), xs[...])
        real = (both[:n_k, :512] - both[n_k:, 512:]).astype(BF)
        imag = (both[n_k:, :512] + both[:n_k, 512:]).astype(BF)
        lane = s * 128
        for d in range(4):
            at = d * 128
            moved[d * n_k : (d + 1) * n_k, lane : lane + 128] = real[:, at : at + 128]
            moved[(4 + d) * n_k : (5 + d) * n_k, lane : lane + 128] = imag[:, at : at + 128]


def recv_kernel(m0, m1, m2, sel_a, sel_b, g_a, g_b, g_out):
    n_k = 240
    moved = jnp.concatenate([m0[...], m1[...], m2[...]], axis=1)
    res = nn_dot(moved, jnp.concatenate([sel_a[...], sel_b[...]], axis=1))
    for rr, g_in in enumerate((g_a, g_b)):
        for x in range(8):
            g_out[rr, :, x * 128 : (x + 1) * 128] = (
                g_in[:, x * 128 : (x + 1) * 128]
                + res[x * n_k : (x + 1) * n_k, rr * 128 : (rr + 1) * 128]
            )


def reach_kernel(blocks, coupling, out):
    me = lax.axis_index("grp")
    n_g = blocks.shape[0]
    rows = coupling[pl.ds(pl.multiple_of(me * 32, 32), 32), :]
    diag = iota((32, 256), 1) == iota((32, 256), 0) + me * 32
    rows = jnp.where(diag, 0.0, rows)
    lanes = iota((32, 128), 1)
    total = jnp.zeros((32, 128), F32)
    for gs in range(n_g):
        window = rows[:, gs // 4 * 128 : gs // 4 * 128 + 128]
        parts = []
        for q in range(4):
            by = (q * 32 - gs % 4 * 32) % 128
            moved = pltpu.roll(window, by, 1) if by else window
            parts.append(jnp.where((lanes >= q * 32) & (lanes < q * 32 + 32), moved, 0.0))
        mat = jnp.concatenate(parts, axis=0)
        block = blocks[lax.rem(n_g + me - gs, n_g)]
        total = total + lax.dot_general(
            block,
            mat,
            (((1,), (1,)), ((), ())),
            preferred_element_type=F32,
            precision=lax.Precision.HIGHEST,
        )
    out[...] = total.astype(BF)


def final_kernel(*refs):
    gs = refs[:4]
    rts = refs[4:12]
    far_in, far_axial, cid, crot, incident, mie, out, gb, fin, fsum = refs[12:]
    n_k = 240
    n_mem = far_in.shape[0]
    me = lax.axis_index("mem")
    for c in range(n_mem):
        fin[c * 32 : (c + 1) * 32, :] = far_in[lax.rem(n_mem + me - c, n_mem)]
    mat = far_axial[...].reshape(2 * n_k, n_k)
    ids = jnp.broadcast_to(cid[...], (n_k, 128))
    for xh in range(2):
        cluster = packed_complex(mat, fin[xh * n_k : (xh + 1) * n_k, :])
        for q in range(4):
            fsum[2 * q + xh] = jnp.take_along_axis(cluster, ids + q * 32, axis=1)
    turn = jnp.broadcast_to(crot[...], (n_k, 128))
    pad = jnp.zeros((16, 1024), BF)
    for r in range(8):
        mine = turn == r
        for x in range(8):
            total = gs[r // 2][r % 2, :, x * 128 : (x + 1) * 128] + jnp.where(mine, fsum[x], 0.0)
            gb[r * 256 : r * 256 + n_k, x * 128 : (x + 1) * 128] = total.astype(BF)
        gb[r * 256 + n_k : (r + 1) * 256, :] = pad
    field = nn_dot(jnp.concatenate([t[...] for t in rts], axis=1), gb[...])
    mie_re = jnp.transpose(jnp.broadcast_to(mie[0:1, :], (128, n_k)))
    mie_im = jnp.transpose(jnp.broadcast_to(mie[1:2, :], (128, n_k)))
    for d in range(4):
        re = incident[d] + field[:, d * 128 : (d + 1) * 128]
        im = incident[4 + d] + field[:, (4 + d) * 128 : (5 + d) * 128]
        out[d] = mie_re * re - mie_im * im
        out[4 + d] = mie_re * im + mie_im * re


def params(mib):
    return pltpu.CompilerParams(vmem_limit_bytes=mib << 20)


def cost(flops, bytes_accessed):
    return pl.CostEstimate(flops=int(flops), transcendentals=0, bytes_accessed=int(bytes_accessed))


def on_device(
    coefficients,
    incident,
    mie_coeffs,
    rot_table,
    axial_shells,
    up_axial,
    far_axial,
    coupling,
    cluster_ids,
    center_rot,
    pair_col,
    pair_rot,
    send_col,
):
    sds = jax.ShapeDtypeStruct
    n_mem = lax.axis_size("mem")
    cid = cluster_ids.reshape(1, 128)
    crot = center_rot.reshape(1, 128)
    first = pl.pallas_call(
        lambda *refs: send_kernel(n_mem, *refs),
        out_shape=[sds((1920, 128), BF)] * 8 + [sds((960, 128), BF)] * 6 + [sds((n_mem, 32, 128), F32)],
        in_specs=[pl.BlockSpec(memory_space=pltpu.MemorySpace.HBM)] * 6,
        out_specs=[VM] * 15,
        scratch_shapes=[
            pltpu.VMEM((8, 240, 128), F32),
            pltpu.VMEM((8, 240, 240), BF),
            pltpu.VMEM((6, 64), I32),
            pltpu.VMEM((1, 128), I32),
            pltpu.VMEM((1, 128), I32),
            pltpu.VMEM((2, 240, 240), BF),
            pltpu.VMEM((240, 1024), BF),
            pltpu.VMEM((1024, 512), BF),
            pltpu.SemaphoreType.DMA((6,)),
        ],
        compiler_params=params(24),
        name="send",
    )(*[pltpu.with_memory_space_constraint(v, pltpu.HBM) for v in (coefficients, rot_table, send_col, crot, cid, up_axial)])
    pools = first[:8]
    sends = first[8:14]
    acc = first[14]
    moves = (("mem", 1), ("mem", -1), ("mem", 2), ("mem", -2), ("grp", 1), ("grp", -1))
    got = []
    for p in range(6):
        got.append(shifted(sends[p], *moves[p]))
    size = n_mem // 2
    while size:
        come = shifted(acc[size:], "mem", size)
        acc = acc[:size] + come
        size //= 2
    step = 1
    while step < lax.axis_size("grp"):
        come = shifted(acc, "grp", step)
        acc = jnp.concatenate([acc, come], axis=0)
        step *= 2
    reached = pl.pallas_call(
        reach_kernel,
        out_shape=sds((32, 128), BF),
        in_specs=[VM] * 2,
        out_specs=VM,
        compiler_params=params(2),
        name="reach",
    )(acc, coupling)[None]
    step = 1
    while step < n_mem:
        come = shifted(reached, "mem", step)
        reached = jnp.concatenate([reached, come], axis=0)
        step *= 2
    g_own, sels, rts = [], [], []
    mats = None
    for r in range(8):
        res = pl.pallas_call(
            lambda *refs, r=r: own_kernel(r, *refs),
            out_shape=[sds((240, 1024), F32), sds((1152, 128), BF), sds((240, 256), BF)]
            + ([sds((480, 768), BF)] if r == 0 else []),
            in_specs=[VM] * 5,
            out_specs=[VM] * (4 if r == 0 else 3),
            scratch_shapes=[pltpu.VMEM((768, 1024), BF)],
            compiler_params=params(20),
            cost_estimate=cost(1.26e9, 3e6),
        )(pools[r], pair_col, pair_rot, rot_table, axial_shells if r == 0 else mats)
        if r == 0:
            mats = res[3]
        g_own.append(res[0])
        sels.append(res[1])
        rts.append(res[2])
    lifted = []
    for j in range(3):
        lifted.append(
            pl.pallas_call(
                lift_kernel,
                out_shape=sds((1920, 384), BF),
                in_specs=[VM] * 3,
                out_specs=VM,
                scratch_shapes=[pltpu.VMEM((240, 1024), BF)],
                compiler_params=params(20),
                cost_estimate=cost(0.7e9, 3e6),
            )(got[2 * j], got[2 * j + 1], axial_shells)
        )
    totals = []
    for q in range(4):
        totals.append(
            pl.pallas_call(
                recv_kernel,
                out_shape=sds((2, 240, 1024), F32),
                in_specs=[VM] * 7,
                out_specs=VM,
                compiler_params=params(20),
                cost_estimate=cost(1.2e9, 8e6),
            )(*lifted, sels[2 * q], sels[2 * q + 1], g_own[2 * q], g_own[2 * q + 1])
        )
    return pl.pallas_call(
        final_kernel,
        out_shape=sds((8, 240, 128), F32),
        in_specs=[VM] * 18,
        out_specs=VM,
        scratch_shapes=[
            pltpu.VMEM((2048, 1024), BF),
            pltpu.VMEM((512, 128), BF),
            pltpu.VMEM((8, 240, 128), F32),
        ],
        compiler_params=params(20),
        name="final",
    )(*totals, *rts, reached, far_axial, cid, crot, incident, mie_coeffs)


def solution(mesh):
    in_specs = (
        P(None, None, ("grp", "mem")),
        P(None, None, ("grp", "mem")),
        P(),
        P(),
        P(),
        P(),
        P(),
        P(),
        P(("grp", "mem")),
        P(("grp", "mem")),
        P(None, ("grp", "mem")),
        P(None, ("grp", "mem")),
        P(("grp", "mem"), None),
    )
    out_specs = P(None, None, ("grp", "mem"))

    return jax.shard_map(
        on_device, mesh=mesh, in_specs=in_specs, out_specs=out_specs, check_vma=False
    )
```

time: 134 us -> 101 us (0.75)
  Pallas kernels: 47.8 us -> 34.8 us
  local copies, waits for them, and re-layouts: 9.7 us -> 0.12 us
  starting transfers between devices: 25.7 us -> 18.8 us
  other arithmetic: 2.82 us -> 0.08 us
    unnamed x34 -> x24, local copies, waits for them, and re-layouts: 9.67 us -> 0.08 us
    ppermute x17, starting transfers between devices: 25.7 us -> 18.8 us  [shifted(): lax.ppermute(value, axis, [(i, (i + by) % length) for i in range(length)])]
    pallas_call x1, Pallas kernels: 9.54 us -> 3.22 us  [on_device(): pl.pallas_call(final_kernel, out_shape=sds((8, 240, 128), F32), in_specs=...]
    pallas_call x2 -> x15, Pallas kernels: 30.7 us -> 24.6 us  [the longest x8 15.4 us: on_device(): pl.pallas_call(lambda *refs, r=r: own_kernel(r, *refs), out_shape=[sds((2...]
    concatenate x6, other arithmetic: 2.78 us -> 0.04 us  [the longest x3 0.02 us: on_device(): acc = jnp.concatenate([acc, come], axis=0)]
    pallas_call x1, Pallas kernels: 2.63 us -> 1.01 us  [on_device(): pl.pallas_call(reach_kernel, out_shape=sds((32, 128), BF), in_specs=[VM]...]
  transfers between devices with their start and end apart: 17 -> 17, of which waited for: 9 -> 10; matrix products, arithmetic and copies ran while one was open for 3% -> 0% of each run, Pallas kernels for 25% -> 24%
where the time goes in v1:
time: 101 us
  waiting for transfers between devices  47 us (47%)
  Pallas kernels  34.8 us (34%)
  starting transfers between devices  18.8 us (19%)
    ppermute x17, waiting for transfers between devices, shifted(): lax.ppermute(value, axis, [(i, (i + by) % length) for i in range(length)])  47 us
    ppermute x17, starting transfers between devices, shifted(): lax.ppermute(value, axis, [(i, (i + by) % length) for i in range(length)])  18.8 us
    pallas_call x8, Pallas kernels, on_device(): pl.pallas_call(lambda *refs, r=r: own_kernel(r, *refs), out_shape=[sds((2...  15.4 us
    pallas_call x1, Pallas kernels, on_device(): pl.pallas_call(lambda *refs: send_kernel(n_mem, *refs), out_shape=[sds((1...  5.9 us
    pallas_call x4, Pallas kernels, on_device(): pl.pallas_call(recv_kernel, out_shape=sds((2, 240, 1024), F32), in_specs=...  5.89 us
    pallas_call x3, Pallas kernels, on_device(): pl.pallas_call(lift_kernel, out_shape=sds((1920, 384), BF), in_specs=[VM]...  3.31 us
    pallas_call x1, Pallas kernels, on_device(): pl.pallas_call(final_kernel, out_shape=sds((8, 240, 128), F32), in_specs=...  3.22 us
  transfers between devices with their start and end apart: 17, of which 10 were waited for; matrix products, arithmetic and copies ran while one was open for 0% of the time, Pallas kernels for 24%

profile of v1, /device:TPU:0, one launch (start us, length us, event | category | flops | bytes accessed | tf_op | source)
XLA Modules:
  0.0 101.1 jit_solution(3022316593531650151)
XLA Ops:
  0.0 5.9 %send.1 = (bf16[1920,128]{1,0:T(8,128)(2,1)S(1)}, bf16[1920,128]{1,0:T(8,128)(2,1)S(1)}, bf16[1920,128]{1,0:T(8,128)(2,1)S(1)}, bf16[1920,128]{1,0:T(8,128)(2,1)...) custom-call(f32[8,240,128]{2,1,0:T(8,128)} %refs_0_.1, ...), custom_call_target="tpu_custom_call" | custom-call | tf_op jit(solution)/shard_map/send/pallas_call | solution.py:263
  5.9 1.7 %collective-permute-start = (bf16[960,128]{1,0:T(8,128)(2,1)S(1)}, bf16[960,128]{1,0:T(8,128)(2,1)S(1)}, u32[]{:S(2)}, u32[]{:S(2)}) collective-permute-start(bf16[960,128]{1,0:T(8,128)(2,1)S(1)} %get-tuple-element.45), channel_id=1, source_target_pairs={{0,1},{1,2},{2,3},{3,4},{4,5},{5,6},{6,7},{7,8},{8,9},{9,10},{10,1... | collective-permute-start | bytes 737288 | tf_op jit(solution)/shard_map/ppermute | solution.py:25
  7.6 4.8 %collective-permute-start.1 = (bf16[960,128]{1,0:T(8,128)(2,1)S(1)}, bf16[960,128]{1,0:T(8,128)(2,1)S(1)}, u32[]{:S(2)}, u32[]{:S(2)}) collective-permute-start(bf16[960,128]{1,0:T(8,128)(2,1)S(1)} %get-tuple-element.46), channel_id=1, source_target_pairs={{0,15},{1,0},{2,1},{3,2},{4,3},{5,4},{6,5},{7,6},{8,7},{9,8},{10,9... | collective-permute-start | bytes 737288 | tf_op jit(solution)/shard_map/ppermute | solution.py:25
  12.4 5.6 %collective-permute-start.3 = (bf16[960,128]{1,0:T(8,128)(2,1)S(1)}, bf16[960,128]{1,0:T(8,128)(2,1)S(1)}, u32[]{:S(2)}, u32[]{:S(2)}) collective-permute-start(bf16[960,128]{1,0:T(8,128)(2,1)S(1)} %get-tuple-element.48), channel_id=1, source_target_pairs={{0,14},{1,15},{2,0},{3,1},{4,2},{5,3},{6,4},{7,5},{8,6},{9,7},{10,... | collective-permute-start | bytes 737288 | tf_op jit(solution)/shard_map/ppermute | solution.py:25
  18.8 2.0 %shard_map.130 = (f32[240,1024]{1,0:T(8,128)S(1)}, bf16[1152,128]{1,0:T(8,128)(2,1)S(1)}, bf16[240,256]{1,0:T(8,128)(2,1)S(1)}, bf16[480,768]{1,0:T(8,128)(2,1)S(1)}) custom-call(bf16[1920,128]{1,0:T(8,128)(2,1)S(1)} %get-tuple-element.51.refs_0_, s32[24,128]{1,0:T(8,128)S(1)} %copy-done.8, s32[24,128]{1,0:T(8,128)S(1)} %copy-done.9, ...), custom_call_target="tpu_custom_call" | custom-call | flops 1260000000 | bytes 3000000 | tf_op jit(solution)/shard_map/pallas_call | solution.py:315
  20.8 1.9 %shard_map.131 = (f32[240,1024]{1,0:T(8,128)S(1)}, bf16[1152,128]{1,0:T(8,128)(2,1)S(1)}, bf16[240,256]{1,0:T(8,128)(2,1)S(1)}) custom-call(bf16[1920,128]{1,0:T(8,128)(2,1)S(1)} %get-tuple-element.53.refs_0_, s32[24,128]{1,0:T(8,128)S(1)} %copy-done.8, s32[24,128]{1,0:T(8,128)S(1)} %copy-done.9, bf16[8,240,240]{2,1,0:T(8,128)(2,1)S(1)} %copy-done.1, ...), custom_call_target="tpu_custom_call" | custom-call | flops 1260000000 | bytes 3000000 | tf_op jit(solution)/shard_map/pallas_call | solution.py:315
  22.7 1.9 %shard_map.133 = (f32[240,1024]{1,0:T(8,128)S(1)}, bf16[1152,128]{1,0:T(8,128)(2,1)S(1)}, bf16[240,256]{1,0:T(8,128)(2,1)S(1)}) custom-call(bf16[1920,128]{1,0:T(8,128)(2,1)S(1)} %get-tuple-element.58.refs_0_, s32[24,128]{1,0:T(8,128)S(1)} %copy-done.8, s32[24,128]{1,0:T(8,128)S(1)} %copy-done.9, bf16[8,240,240]{2,1,0:T(8,128)(2,1)S(1)} %copy-done.1, ...), custom_call_target="tpu_custom_call" | custom-call | flops 1260000000 | bytes 3000000 | tf_op jit(solution)/shard_map/pallas_call | solution.py:315
  24.7 1.9 %shard_map.134 = (f32[240,1024]{1,0:T(8,128)S(1)}, bf16[1152,128]{1,0:T(8,128)(2,1)S(1)}, bf16[240,256]{1,0:T(8,128)(2,1)S(1)}) custom-call(bf16[1920,128]{1,0:T(8,128)(2,1)S(1)} %get-tuple-element.60.refs_0_, s32[24,128]{1,0:T(8,128)S(1)} %copy-done.8, s32[24,128]{1,0:T(8,128)S(1)} %copy-done.9, bf16[8,240,240]{2,1,0:T(8,128)(2,1)S(1)} %copy-done.1, ...), custom_call_target="tpu_custom_call" | custom-call | flops 1260000000 | bytes 3000000 | tf_op jit(solution)/shard_map/pallas_call | solution.py:315
  26.6 1.9 %shard_map.136 = (f32[240,1024]{1,0:T(8,128)S(1)}, bf16[1152,128]{1,0:T(8,128)(2,1)S(1)}, bf16[240,256]{1,0:T(8,128)(2,1)S(1)}) custom-call(bf16[1920,128]{1,0:T(8,128)(2,1)S(1)} %get-tuple-element.64.refs_0_, s32[24,128]{1,0:T(8,128)S(1)} %copy-done.8, s32[24,128]{1,0:T(8,128)S(1)} %copy-done.9, bf16[8,240,240]{2,1,0:T(8,128)(2,1)S(1)} %copy-done.1, ...), custom_call_target="tpu_custom_call" | custom-call | flops 1260000000 | bytes 3000000 | tf_op jit(solution)/shard_map/pallas_call | solution.py:315
  29.7 1.9 %shard_map.137 = (f32[240,1024]{1,0:T(8,128)S(1)}, bf16[1152,128]{1,0:T(8,128)(2,1)S(1)}, bf16[240,256]{1,0:T(8,128)(2,1)S(1)}) custom-call(bf16[1920,128]{1,0:T(8,128)(2,1)S(1)} %get-tuple-element.66.refs_0_, s32[24,128]{1,0:T(8,128)S(1)} %copy-done.8, s32[24,128]{1,0:T(8,128)S(1)} %copy-done.9, bf16[8,240,240]{2,1,0:T(8,128)(2,1)S(1)} %copy-done.1, ...), custom_call_target="tpu_custom_call" | custom-call | flops 1260000000 | bytes 3000000 | tf_op jit(solution)/shard_map/pallas_call | solution.py:315
  31.6 2.5 %collective-permute-done.7 = f32[4,32,128]{2,1,0:T(8,128)S(1)} collective-permute-done((f32[4,32,128]{2,1,0:T(8,128)S(1)}, f32[4,32,128]{2,1,0:T(8,128)S(1)}, u32[]{:S(2)}, u32[]{:S(2)}) %collective-permute-start.7) | collective-permute-done | bytes 65568 | tf_op jit(solution)/shard_map/ppermute | solution.py:25
  34.4 1.9 %shard_map.139 = (f32[240,1024]{1,0:T(8,128)S(1)}, bf16[1152,128]{1,0:T(8,128)(2,1)S(1)}, bf16[240,256]{1,0:T(8,128)(2,1)S(1)}) custom-call(bf16[1920,128]{1,0:T(8,128)(2,1)S(1)} %get-tuple-element.70.refs_0_, s32[24,128]{1,0:T(8,128)S(1)} %copy-done.8, s32[24,128]{1,0:T(8,128)S(1)} %copy-done.9, bf16[8,240,240]{2,1,0:T(8,128)(2,1)S(1)} %copy-done.1, ...), custom_call_target="tpu_custom_call" | custom-call | flops 1260000000 | bytes 3000000 | tf_op jit(solution)/shard_map/pallas_call | solution.py:315
  36.3 5.4 %collective-permute-done.8 = f32[2,32,128]{2,1,0:T(8,128)S(1)} collective-permute-done((f32[2,32,128]{2,1,0:T(8,128)S(1)}, f32[2,32,128]{2,1,0:T(8,128)S(1)}, u32[]{:S(2)}, u32[]{:S(2)}) %collective-permute-start.8) | collective-permute-done | bytes 32800 | tf_op jit(solution)/shard_map/ppermute | solution.py:25
  42.1 1.9 %shard_map.140 = (f32[240,1024]{1,0:T(8,128)S(1)}, bf16[1152,128]{1,0:T(8,128)(2,1)S(1)}, bf16[240,256]{1,0:T(8,128)(2,1)S(1)}) custom-call(bf16[1920,128]{1,0:T(8,128)(2,1)S(1)} %get-tuple-element.72.refs_0_, s32[24,128]{1,0:T(8,128)S(1)} %copy-done.8, s32[24,128]{1,0:T(8,128)S(1)} %copy-done.9, bf16[8,240,240]{2,1,0:T(8,128)(2,1)S(1)} %copy-done.1, ...), custom_call_target="tpu_custom_call" | custom-call | flops 1260000000 | bytes 3000000 | tf_op jit(solution)/shard_map/pallas_call | solution.py:315
  44.0 5.1 %collective-permute-done.9 = f32[1,32,128]{2,1,0:T(8,128)S(1)} collective-permute-done((f32[1,32,128]{2,1,0:T(8,128)S(1)}, f32[1,32,128]{2,1,0:T(8,128)S(1)}, u32[]{:S(2)}, u32[]{:S(2)}) %collective-permute-start.9) | collective-permute-done | bytes 16416 | tf_op jit(solution)/shard_map/ppermute | solution.py:25
  49.1 3.0 %collective-permute-start.5 = (bf16[960,128]{1,0:T(8,128)(2,1)S(1)}, bf16[960,128]{1,0:T(8,128)(2,1)S(1)}, u32[]{:S(2)}, u32[]{:S(2)}) collective-permute-start(bf16[960,128]{1,0:T(8,128)(2,1)S(1)} %get-tuple-element.50), channel_id=1, source_target_pairs={{0,112},{16,0},{32,16},{48,32},{64,48},{80,64},{96,80},{112,96},{1... | collective-permute-start | bytes 737288 | tf_op jit(solution)/shard_map/ppermute | solution.py:25
  54.3 1.6 %collective-permute-done.4.first = bf16[960,128]{1,0:T(8,128)(2,1)S(1)} collective-permute-done((bf16[960,128]{1,0:T(8,128)(2,1)S(1)}, bf16[960,128]{1,0:T(8,128)(2,1)S(1)}, u32[]{:S(2)}, u32[]{:S(2)}) %collective-permute-start.4) | collective-permute-done | bytes 245792 | tf_op jit(solution)/shard_map/ppermute | solution.py:25
  61.9 3.3 %collective-permute-done.11 = f32[2,32,128]{2,1,0:T(8,128)S(1)} collective-permute-done((f32[2,32,128]{2,1,0:T(8,128)S(1)}, f32[2,32,128]{2,1,0:T(8,128)S(1)}, u32[]{:S(2)}, u32[]{:S(2)}) %collective-permute-start.11) | collective-permute-done | bytes 32800 | tf_op jit(solution)/shard_map/ppermute | solution.py:25
  67.5 3.5 %collective-permute-done.12 = f32[4,32,128]{2,1,0:T(8,128)S(1)} collective-permute-done((f32[4,32,128]{2,1,0:T(8,128)S(1)}, f32[4,32,128]{2,1,0:T(8,128)S(1)}, u32[]{:S(2)}, u32[]{:S(2)}) %collective-permute-start.12) | collective-permute-done | bytes 65568 | tf_op jit(solution)/shard_map/ppermute | solution.py:25
  72.1 7.0 %collective-permute-done.13 = bf16[1,32,128]{2,1,0:T(8,128)(2,1)S(1)} collective-permute-done((bf16[1,32,128]{2,1,0:T(8,128)(2,1)S(1)}, bf16[1,32,128]{2,1,0:T(8,128)(2,1)S(1)}, u32[]{:S(2)}, u32[]{:S(2)}) %collective-permute-start.13) | collective-permute-done | bytes 8224 | tf_op jit(solution)/shard_map/ppermute | solution.py:25
  79.0 7.3 %collective-permute-done.14 = bf16[2,32,128]{2,1,0:T(8,128)(2,1)S(1)} collective-permute-done((bf16[2,32,128]{2,1,0:T(8,128)(2,1)S(1)}, bf16[2,32,128]{2,1,0:T(8,128)(2,1)S(1)}, u32[]{:S(2)}, u32[]{:S(2)}) %collective-permute-start.14) | collective-permute-done | bytes 16416 | tf_op jit(solution)/shard_map/ppermute | solution.py:25
  86.4 5.5 %collective-permute-done.15 = bf16[4,32,128]{2,1,0:T(8,128)(2,1)S(1)} collective-permute-done((bf16[4,32,128]{2,1,0:T(8,128)(2,1)S(1)}, bf16[4,32,128]{2,1,0:T(8,128)(2,1)S(1)}, u32[]{:S(2)}, u32[]{:S(2)}) %collective-permute-start.15) | collective-permute-done | bytes 32800 | tf_op jit(solution)/shard_map/ppermute | solution.py:25
  92.0 5.7 %collective-permute-done.16 = bf16[8,32,128]{2,1,0:T(8,128)(2,1)S(1)} collective-permute-done((bf16[8,32,128]{2,1,0:T(8,128)(2,1)S(1)}, bf16[8,32,128]{2,1,0:T(8,128)(2,1)S(1)}, u32[]{:S(2)}, u32[]{:S(2)}) %collective-permute-start.16) | collective-permute-done | bytes 65568 | tf_op jit(solution)/shard_map/ppermute | solution.py:25
  97.9 3.2 %final.1 = f32[8,240,128]{2,1,0:T(8,128)} custom-call(f32[2,240,1024]{2,1,0:T(8,128)S(1)} %shard_map.132.refs_0_, f32[2,240,1024]{2,1,0:T(8,128)S(1)} %shard_map.135.refs_1_, f32[2,240,1024]{2,1,0:T(8,128)S(1)} %shard_map.138.refs_2_, f32[2,240,1024]{2,1,0:T(8,128)S(1)} %shard_map.141.refs_3_, bf16[240,256]{1,0:T(8,128)(2,1)S(1)} %get-tuple-element.76.refs_4_, ...), custom_call_target="tpu_custom_call" | custom-call | tf_op jit(solution)/shard_map/final/pallas_call | solution.py:355
  (67 shorter events, 14.1 us)
Async XLA Ops:
  0.0 18.8 %copy-start.8 = (s32[24,128]{1,0:T(8,128)S(1)}, s32[24,128]{1,0:T(8,128)}, u32[]{:S(2)}) copy-start(s32[24,128]{1,0:T(8,128)} %refs_1_.17) | copy-start | bytes 36868
  0.0 18.8 %copy-start.9 = (s32[24,128]{1,0:T(8,128)S(1)}, s32[24,128]{1,0:T(8,128)}, u32[]{:S(2)}) copy-start(s32[24,128]{1,0:T(8,128)} %refs_2_.17) | copy-start | bytes 36868
  5.9 43.2 %collective-permute-start = (bf16[960,128]{1,0:T(8,128)(2,1)S(1)}, bf16[960,128]{1,0:T(8,128)(2,1)S(1)}, u32[]{:S(2)}, u32[]{:S(2)}) collective-permute-start(bf16[960,128]{1,0:T(8,128)(2,1)S(1)} %get-tuple-element.45), channel_id=1, source_target_pairs={{0,1},{1,2},{2,3},{3,4},{4,5},{5,6},{6,7},{7,8},{8,9},{9,10},{10,1... | collective-permute-start | bytes 737288 | tf_op jit(solution)/shard_map/ppermute | solution.py:25
  7.6 44.5 %collective-permute-start.1 = (bf16[960,128]{1,0:T(8,128)(2,1)S(1)}, bf16[960,128]{1,0:T(8,128)(2,1)S(1)}, u32[]{:S(2)}, u32[]{:S(2)}) collective-permute-start(bf16[960,128]{1,0:T(8,128)(2,1)S(1)} %get-tuple-element.46), channel_id=1, source_target_pairs={{0,15},{1,0},{2,1},{3,2},{4,3},{5,4},{6,5},{7,6},{8,7},{9,8},{10,9... | collective-permute-start | bytes 737288 | tf_op jit(solution)/shard_map/ppermute | solution.py:25
  12.4 40.8 %collective-permute-start.2 = (bf16[960,128]{1,0:T(8,128)(2,1)S(1)}, bf16[960,128]{1,0:T(8,128)(2,1)S(1)}, u32[]{:S(2)}, u32[]{:S(2)}) collective-permute-start(bf16[960,128]{1,0:T(8,128)(2,1)S(1)} %get-tuple-element.47), channel_id=1, source_target_pairs={{0,2},{1,3},{2,4},{3,5},{4,6},{5,7},{6,8},{7,9},{8,10},{9,11},{10,... | collective-permute-start | bytes 737288 | tf_op jit(solution)/shard_map/ppermute | solution.py:25
  12.4 40.8 %collective-permute-start.3 = (bf16[960,128]{1,0:T(8,128)(2,1)S(1)}, bf16[960,128]{1,0:T(8,128)(2,1)S(1)}, u32[]{:S(2)}, u32[]{:S(2)}) collective-permute-start(bf16[960,128]{1,0:T(8,128)(2,1)S(1)} %get-tuple-element.48), channel_id=1, source_target_pairs={{0,14},{1,15},{2,0},{3,1},{4,2},{5,3},{6,4},{7,5},{8,6},{9,7},{10,... | collective-permute-start | bytes 737288 | tf_op jit(solution)/shard_map/ppermute | solution.py:25
  18.1 10.4 %collective-permute-start.6 = (f32[8,32,128]{2,1,0:T(8,128)S(1)}, f32[8,32,128]{2,1,0:T(8,128)S(1)}, u32[]{:S(2)}, u32[]{:S(2)}) collective-permute-start(f32[8,32,128]{2,1,0:T(8,128)S(1)} %slice.25), channel_id=1, source_target_pairs={{0,8},{1,9},{2,10},{3,11},{4,12},{5,13},{6,14},{7,15},{8,0},{9,1},... | collective-permute-start | bytes 393224 | tf_op jit(solution)/shard_map/ppermute | solution.py:25
  28.6 5.5 %collective-permute-start.7 = (f32[4,32,128]{2,1,0:T(8,128)S(1)}, f32[4,32,128]{2,1,0:T(8,128)S(1)}, u32[]{:S(2)}, u32[]{:S(2)}) collective-permute-start(f32[4,32,128]{2,1,0:T(8,128)S(1)} %slice.33), channel_id=1, source_target_pairs={{0,4},{1,5},{2,6},{3,7},{4,8},{5,9},{6,10},{7,11},{8,12},{9,13},{1... | collective-permute-start | bytes 196616 | tf_op jit(solution)/shard_map/ppermute | solution.py:25
  34.1 7.6 %collective-permute-start.8 = (f32[2,32,128]{2,1,0:T(8,128)S(1)}, f32[2,32,128]{2,1,0:T(8,128)S(1)}, u32[]{:S(2)}, u32[]{:S(2)}) collective-permute-start(f32[2,32,128]{2,1,0:T(8,128)S(1)} %slice.35), channel_id=1, source_target_pairs={{0,2},{1,3},{2,4},{3,5},{4,6},{5,7},{6,8},{7,9},{8,10},{9,11},{10,... | collective-permute-start | bytes 98312 | tf_op jit(solution)/shard_map/ppermute | solution.py:25
  41.8 7.3 %collective-permute-start.9 = (f32[1,32,128]{2,1,0:T(8,128)S(1)}, f32[1,32,128]{2,1,0:T(8,128)S(1)}, u32[]{:S(2)}, u32[]{:S(2)}) collective-permute-start(f32[1,32,128]{2,1,0:T(8,128)S(1)} %slice.37), channel_id=1, source_target_pairs={{0,1},{1,2},{2,3},{3,4},{4,5},{5,6},{6,7},{7,8},{8,9},{9,10},{10,1... | collective-permute-start | bytes 49160 | tf_op jit(solution)/shard_map/ppermute | solution.py:25
  49.1 6.8 %collective-permute-start.4 = (bf16[960,128]{1,0:T(8,128)(2,1)S(1)}, bf16[960,128]{1,0:T(8,128)(2,1)S(1)}, u32[]{:S(2)}, u32[]{:S(2)}) collective-permute-start(bf16[960,128]{1,0:T(8,128)(2,1)S(1)} %get-tuple-element.49), channel_id=1, source_target_pairs={{0,16},{16,32},{32,48},{48,64},{64,80},{80,96},{96,112},{112,0},{1... | collective-permute-start | bytes 737288 | tf_op jit(solution)/shard_map/ppermute | solution.py:25
  49.1 6.8 %collective-permute-start.5 = (bf16[960,128]{1,0:T(8,128)(2,1)S(1)}, bf16[960,128]{1,0:T(8,128)(2,1)S(1)}, u32[]{:S(2)}, u32[]{:S(2)}) collective-permute-start(bf16[960,128]{1,0:T(8,128)(2,1)S(1)} %get-tuple-element.50), channel_id=1, source_target_pairs={{0,112},{16,0},{32,16},{48,32},{64,48},{80,64},{96,80},{112,96},{1... | collective-permute-start | bytes 737288 | tf_op jit(solution)/shard_map/ppermute | solution.py:25
  52.1 7.9 %collective-permute-start.10 = (f32[1,32,128]{2,1,0:T(8,128)S(1)}, f32[1,32,128]{2,1,0:T(8,128)S(1)}, u32[]{:S(2)}, u32[]{:S(2)}) collective-permute-start(f32[1,32,128]{2,1,0:T(8,128)S(1)} %slice_add_fusion.3), channel_id=1, source_target_pairs={{0,16},{16,32},{32,48},{48,64},{64,80},{80,96},{96,112},{112,0},{1... | collective-permute-start | bytes 49160 | tf_op jit(solution)/shard_map/ppermute | solution.py:25
  60.0 5.2 %collective-permute-start.11 = (f32[2,32,128]{2,1,0:T(8,128)S(1)}, f32[2,32,128]{2,1,0:T(8,128)S(1)}, u32[]{:S(2)}, u32[]{:S(2)}) collective-permute-start(f32[2,32,128]{2,1,0:T(8,128)S(1)} %pad_maximum_fusion.3), channel_id=1, source_target_pairs={{0,32},{16,48},{32,64},{48,80},{64,96},{80,112},{96,0},{112,16},{1... | collective-permute-start | bytes 98312 | tf_op jit(solution)/shard_map/ppermute | solution.py:25
  65.2 5.8 %collective-permute-start.12 = (f32[4,32,128]{2,1,0:T(8,128)S(1)}, f32[4,32,128]{2,1,0:T(8,128)S(1)}, u32[]{:S(2)}, u32[]{:S(2)}) collective-permute-start(f32[4,32,128]{2,1,0:T(8,128)S(1)} %pad_maximum_fusion.1), channel_id=1, source_target_pairs={{0,64},{16,80},{32,96},{48,112},{64,0},{80,16},{96,32},{112,48},{1... | collective-permute-start | bytes 196616 | tf_op jit(solution)/shard_map/ppermute | solution.py:25
  66.0 31.8 %copy-start.2 = (f32[8,240,128]{2,1,0:T(8,128)S(1)}, f32[8,240,128]{2,1,0:T(8,128)}, u32[]{:S(2)}) copy-start(f32[8,240,128]{2,1,0:T(8,128)} %refs_16_.1) | copy-start | bytes 2949124
  66.0 31.8 %copy-start.4 = (bf16[2,240,240]{2,1,0:T(8,128)(2,1)S(1)}, bf16[2,240,240]{2,1,0:T(8,128)(2,1)}, u32[]{:S(2)}) copy-start(bf16[2,240,240]{2,1,0:T(8,128)(2,1)} %refs_13_.1) | copy-start | bytes 691204
  66.0 31.8 %copy-start.5 = (f32[2,240]{1,0:T(2,128)S(1)}, f32[2,240]{1,0:T(2,128)}, u32[]{:S(2)}) copy-start(f32[2,240]{1,0:T(2,128)} %refs_17_.1) | copy-start | bytes 5764
  66.0 31.8 %copy-start.6 = (s32[128]{0:T(128)S(1)}, s32[128]{0:T(128)}, u32[]{:S(2)}) copy-start(s32[128]{0:T(128)} %param.22) | copy-start | bytes 1540
  66.0 31.8 %copy-start.7 = (s32[128]{0:T(128)S(1)}, s32[128]{0:T(128)}, u32[]{:S(2)}) copy-start(s32[128]{0:T(128)} %param.21) | copy-start | bytes 1540
  72.0 7.0 %collective-permute-start.13 = (bf16[1,32,128]{2,1,0:T(8,128)(2,1)S(1)}, bf16[1,32,128]{2,1,0:T(8,128)(2,1)S(1)}, u32[]{:S(2)}, u32[]{:S(2)}) collective-permute-start(bf16[1,32,128]{2,1,0:T(8,128)(2,1)S(1)} %bitcast.4), channel_id=1, source_target_pairs={{0,1},{1,2},{2,3},{3,4},{4,5},{5,6},{6,7},{7,8},{8,9},{9,10},{10,1... | collective-permute-start | bytes 24584 | tf_op jit(solution)/shard_map/ppermute | solution.py:25
  79.0 7.4 %collective-permute-start.14 = (bf16[2,32,128]{2,1,0:T(8,128)(2,1)S(1)}, bf16[2,32,128]{2,1,0:T(8,128)(2,1)S(1)}, u32[]{:S(2)}, u32[]{:S(2)}) collective-permute-start(bf16[2,32,128]{2,1,0:T(8,128)(2,1)S(1)} %pad_maximum_fusion.5), channel_id=1, source_target_pairs={{0,2},{1,3},{2,4},{3,5},{4,6},{5,7},{6,8},{7,9},{8,10},{9,11},{10,... | collective-permute-start | bytes 49160 | tf_op jit(solution)/shard_map/ppermute | solution.py:25
  86.4 5.5 %collective-permute-start.15 = (bf16[4,32,128]{2,1,0:T(8,128)(2,1)S(1)}, bf16[4,32,128]{2,1,0:T(8,128)(2,1)S(1)}, u32[]{:S(2)}, u32[]{:S(2)}) collective-permute-start(bf16[4,32,128]{2,1,0:T(8,128)(2,1)S(1)} %pad_maximum_fusion.4), channel_id=1, source_target_pairs={{0,4},{1,5},{2,6},{3,7},{4,8},{5,9},{6,10},{7,11},{8,12},{9,13},{1... | collective-permute-start | bytes 98312 | tf_op jit(solution)/shard_map/ppermute | solution.py:25
  91.9 5.8 %collective-permute-start.16 = (bf16[8,32,128]{2,1,0:T(8,128)(2,1)S(1)}, bf16[8,32,128]{2,1,0:T(8,128)(2,1)S(1)}, u32[]{:S(2)}, u32[]{:S(2)}) collective-permute-start(bf16[8,32,128]{2,1,0:T(8,128)(2,1)S(1)} %pad_maximum_fusion.2), channel_id=1, source_target_pairs={{0,8},{1,9},{2,10},{3,11},{4,12},{5,13},{6,14},{7,15},{8,0},{9,1},... | collective-permute-start | bytes 196616 | tf_op jit(solution)/shard_map/ppermute | solution.py:25
  (3 other events, 42.7 us)

commit v2 on v1

--- a/solution.py
+++ b/solution.py
@@ -20,9 +20,14 @@
     return lax.broadcasted_iota(I32, shape, dim)
 
 
+def moved_by(value, axis, target):
+    length = lax.axis_size(axis)
+    return lax.ppermute(value, axis, [(i, target(i)) for i in range(length)])
+
+
 def shifted(value, axis, by):
     length = lax.axis_size(axis)
-    return lax.ppermute(value, axis, [(i, (i + by) % length) for i in range(length)])
+    return moved_by(value, axis, lambda i: (i + by) % length)
 
 
 def packed_complex(mat, cols):
@@ -32,10 +37,11 @@
     return both[:k] + pltpu.roll(both[k:], 64, 1) * sign
 
 
-def send_kernel(n_mem, coef_h, rot_h, send_h, crot_h, cid_h, up_h, *rest):
+def send_kernel(coef_h, rot_h, send_h, crot_h, cid_h, up_h, *rest):
     pools = rest[:8]
     outs = rest[8:14]
-    far, coef, rot, send, crot, cid, up, xs, sel, sems = rest[14:]
+    fars = rest[14:18]
+    coef, rot, send, crot, cid, up, xs, sel, whole, sems = rest[18:]
     pairs = ((coef_h, coef), (rot_h, rot), (send_h, send), (crot_h, crot), (cid_h, cid), (up_h, up))
     copies = [pltpu.make_async_copy(src, dst, sems.at[i]) for i, (src, dst) in enumerate(pairs)]
     for copy in copies:
@@ -72,11 +78,7 @@
         im = imag[:, q * 128 : (q + 1) * 128]
         outs[2 * q][...] = jnp.where(low, re, pltpu.roll(im, 64, 1)).astype(BF)
         outs[2 * q + 1][...] = jnp.where(low, pltpu.roll(re, 64, 1), im).astype(BF)
-    me = lax.axis_index("mem")
-    chunk = 32
-    far[lax.rem(2 * n_mem - 1 - me, n_mem)] = jnp.zeros((chunk, 128), F32)
     mat = up[...].reshape(2 * n_k, n_k)
-    packed = []
     for xh in range(2):
         total = None
         for q in range(4):
@@ -89,12 +91,14 @@
         rem = total - hi.astype(F32)
         mid = rem.astype(BF)
         lo = (rem - mid.astype(F32)).astype(BF)
-        packed.append(
+        whole[xh * n_k : (xh + 1) * n_k, :] = (
             packed_complex(mat, lo) + packed_complex(mat, mid) + packed_complex(mat, hi)
         )
-    whole = jnp.concatenate(packed, axis=0)
-    for c in range(2 * n_k // chunk):
-        far[lax.rem(n_mem + c - me, n_mem)] = whole[c * chunk : (c + 1) * chunk]
+    whole[2 * n_k :, :] = jnp.zeros((512 - 2 * n_k, 128), F32)
+    z = lax.axis_index("mem") // 4
+    for k in range(4):
+        at = pl.multiple_of(lax.rem(z + k, 4) * 128, 128)
+        fars[k][...] = whole[pl.ds(at, 128), :]
 
 
 def own_kernel(r, *refs):
@@ -173,42 +177,48 @@
             )
 
 
-def reach_kernel(blocks, coupling, out):
+def reach_kernel(*refs):
+    blocks = refs[:4]
+    coupling, own, other = refs[4:]
     me = lax.axis_index("grp")
-    n_g = blocks.shape[0]
-    rows = coupling[pl.ds(pl.multiple_of(me * 32, 32), 32), :]
-    diag = iota((32, 256), 1) == iota((32, 256), 0) + me * 32
-    rows = jnp.where(diag, 0.0, rows)
     lanes = iota((32, 128), 1)
-    total = jnp.zeros((32, 128), F32)
-    for gs in range(n_g):
-        window = rows[:, gs // 4 * 128 : gs // 4 * 128 + 128]
-        parts = []
-        for q in range(4):
-            by = (q * 32 - gs % 4 * 32) % 128
-            moved = pltpu.roll(window, by, 1) if by else window
-            parts.append(jnp.where((lanes >= q * 32) & (lanes < q * 32 + 32), moved, 0.0))
-        mat = jnp.concatenate(parts, axis=0)
-        block = blocks[lax.rem(n_g + me - gs, n_g)]
-        total = total + lax.dot_general(
-            block,
-            mat,
-            (((1,), (1,)), ((), ())),
-            preferred_element_type=F32,
-            precision=lax.Precision.HIGHEST,
-        )
-    out[...] = total.astype(BF)
+    outs = []
+    for target in (me, me + 1 - 2 * lax.rem(me, 2)):
+        row_at = pl.multiple_of(target * 32, 32)
+        total = jnp.zeros((128, 128), F32)
+        for k in range(4):
+            gs = lax.rem(me + 8 - 2 * k, 8)
+            col_at = pl.multiple_of(gs // 4 * 128, 128)
+            window = coupling[pl.ds(row_at, 32), pl.ds(col_at, 128)]
+            same = lanes + col_at == iota((32, 128), 0) + row_at
+            window = jnp.where(same, 0.0, window)
+            parts = []
+            for q in range(4):
+                by = lax.rem(q * 32 + 128 - lax.rem(gs, 4) * 32, 128)
+                turned = pltpu.roll(window, by, 1)
+                parts.append(jnp.where((lanes >= q * 32) & (lanes < q * 32 + 32), turned, 0.0))
+            total = total + lax.dot_general(
+                blocks[k][...],
+                jnp.concatenate(parts, axis=0),
+                (((1,), (1,)), ((), ())),
+                preferred_element_type=F32,
+                precision=lax.Precision.HIGHEST,
+            )
+        outs.append(total)
+    own[...] = outs[0]
+    other[...] = outs[1]
 
 
 def final_kernel(*refs):
     gs = refs[:4]
     rts = refs[4:12]
-    far_in, far_axial, cid, crot, incident, mie, out, gb, fin, fsum = refs[12:]
+    fars = refs[12:16]
+    far_axial, cid, crot, incident, mie, out, gb, fin, fsum = refs[16:]
     n_k = 240
-    n_mem = far_in.shape[0]
-    me = lax.axis_index("mem")
-    for c in range(n_mem):
-        fin[c * 32 : (c + 1) * 32, :] = far_in[lax.rem(n_mem + me - c, n_mem)]
+    z = lax.axis_index("mem") // 4
+    for k in range(4):
+        at = pl.multiple_of(lax.rem(z + 4 - k, 4) * 128, 128)
+        fin[pl.ds(at, 128), :] = fars[k][...]
     mat = far_axial[...].reshape(2 * n_k, n_k)
     ids = jnp.broadcast_to(cid[...], (n_k, 128))
     for xh in range(2):
@@ -257,14 +267,13 @@
     send_col,
 ):
     sds = jax.ShapeDtypeStruct
-    n_mem = lax.axis_size("mem")
     cid = cluster_ids.reshape(1, 128)
     crot = center_rot.reshape(1, 128)
     first = pl.pallas_call(
-        lambda *refs: send_kernel(n_mem, *refs),
-        out_shape=[sds((1920, 128), BF)] * 8 + [sds((960, 128), BF)] * 6 + [sds((n_mem, 32, 128), F32)],
+        send_kernel,
+        out_shape=[sds((1920, 128), BF)] * 8 + [sds((960, 128), BF)] * 6 + [sds((128, 128), F32)] * 4,
         in_specs=[pl.BlockSpec(memory_space=pltpu.MemorySpace.HBM)] * 6,
-        out_specs=[VM] * 15,
+        out_specs=[VM] * 18,
         scratch_shapes=[
             pltpu.VMEM((8, 240, 128), F32),
             pltpu.VMEM((8, 240, 240), BF),
@@ -274,6 +283,7 @@
             pltpu.VMEM((2, 240, 240), BF),
             pltpu.VMEM((240, 1024), BF),
             pltpu.VMEM((1024, 512), BF),
+            pltpu.VMEM((512, 128), F32),
             pltpu.SemaphoreType.DMA((6,)),
         ],
         compiler_params=params(24),
@@ -281,34 +291,34 @@
     )(*[pltpu.with_memory_space_constraint(v, pltpu.HBM) for v in (coefficients, rot_table, send_col, crot, cid, up_axial)])
     pools = first[:8]
     sends = first[8:14]
-    acc = first[14]
+    fars = first[14:18]
     moves = (("mem", 1), ("mem", -1), ("mem", 2), ("mem", -2), ("grp", 1), ("grp", -1))
     got = []
     for p in range(6):
         got.append(shifted(sends[p], *moves[p]))
-    size = n_mem // 2
-    while size:
-        come = shifted(acc[size:], "mem", size)
-        acc = acc[:size] + come
-        size //= 2
-    step = 1
-    while step < lax.axis_size("grp"):
-        come = shifted(acc, "grp", step)
-        acc = jnp.concatenate([acc, come], axis=0)
-        step *= 2
-    reached = pl.pallas_call(
+    acc = fars[0]
+    for k in (2, 1, 3):
+        come = shifted(fars[k], "mem", 4 * k)
+        acc = acc + come
+    blocks = [acc]
+    for k in (1, 2, 3):
+        blocks.append(shifted(acc, "grp", 2 * k))
+    mine, theirs = pl.pallas_call(
         reach_kernel,
-        out_shape=sds((32, 128), BF),
-        in_specs=[VM] * 2,
-        out_specs=VM,
+        out_shape=[sds((128, 128), F32)] * 2,
+        in_specs=[VM] * 5,
+        out_specs=[VM] * 2,
         compiler_params=params(2),
         name="reach",
-    )(acc, coupling)[None]
-    step = 1
-    while step < n_mem:
-        come = shifted(reached, "mem", step)
-        reached = jnp.concatenate([reached, come], axis=0)
-        step *= 2
+    )(*blocks, coupling)
+    come = moved_by(theirs, "grp", lambda i: i ^ 1)
+    part = mine + come
+    total = part
+    for k in (2, 1, 3):
+        total = total + moved_by(part, "mem", lambda i: i // 4 * 4 + (i + k) % 4)
+    reached = [total.astype(BF)]
+    for k in (1, 2, 3):
+        reached.append(shifted(reached[0], "mem", 4 * k))
     g_own, sels, rts = [], [], []
     mats = None
     for r in range(8):
@@ -355,7 +365,7 @@
     return pl.pallas_call(
         final_kernel,
         out_shape=sds((8, 240, 128), F32),
-        in_specs=[VM] * 18,
+        in_specs=[VM] * 21,
         out_specs=VM,
         scratch_shapes=[
             pltpu.VMEM((2048, 1024), BF),
@@ -364,7 +374,7 @@
         ],
         compiler_params=params(20),
         name="final",
-    )(*totals, *rts, reached, far_axial, cid, crot, incident, mie_coeffs)
+    )(*totals, *rts, *reached, far_axial, cid, crot, incident, mie_coeffs)
 
 
 def solution(mesh):

time: 101 us -> 68.4 us (0.68)
  waiting for transfers between devices: 47 us -> 1.17 us
  starting transfers between devices: 18.8 us -> 31.1 us
    ppermute x17 -> x19, waiting for transfers between devices: 47 us -> 1.17 us  [moved_by(): return lax.ppermute(value, axis, [(i, target(i)) for i in range(length)])]
    ppermute x17 -> x19, starting transfers between devices: 18.8 us -> 31.1 us  [moved_by(): return lax.ppermute(value, axis, [(i, target(i)) for i in range(length)])]
  transfers between devices with their start and end apart: 17 -> 19, of which waited for: 10 -> 1; matrix products, arithmetic and copies ran while one was open for 0% -> 0% of each run, Pallas kernels for 24% -> 38%
where the time goes in v2:
time: 68.4 us; the launch traced here: 67.8 us
  Pallas kernels  35.1 us (51%)
  starting transfers between devices  31.1 us (45%)
  waiting for transfers between devices  1.17 us (2%)
    ppermute x19, starting transfers between devices, moved_by(): return lax.ppermute(value, axis, [(i, target(i)) for i in range(length)])  31.1 us
    pallas_call x8, Pallas kernels, on_device(): pl.pallas_call(lambda *refs, r=r: own_kernel(r, *refs), out_shape=[sds((2...  15.4 us
    pallas_call x1, Pallas kernels, on_device(): pl.pallas_call(send_kernel, out_shape=[sds((1920, 128), BF)] * 8 + [sds((...  5.94 us
    pallas_call x4, Pallas kernels, on_device(): pl.pallas_call(recv_kernel, out_shape=sds((2, 240, 1024), F32), in_specs=...  5.89 us
    pallas_call x3, Pallas kernels, on_device(): pl.pallas_call(lift_kernel, out_shape=sds((1920, 384), BF), in_specs=[VM]...  3.31 us
    pallas_call x1, Pallas kernels, on_device(): pl.pallas_call(final_kernel, out_shape=sds((8, 240, 128), F32), in_specs=...  3.23 us
  transfers between devices with their start and end apart: 19, of which 1 were waited for; matrix products, arithmetic and copies ran while one was open for 0% of the time, Pallas kernels for 38%

profile of v2, /device:TPU:0, one launch (start us, length us, event | category | flops | bytes accessed | tf_op | source)
XLA Modules:
  0.0 67.8 jit_solution(13521661973968996199)
XLA Ops:
  0.0 5.9 %send.1 = (bf16[1920,128]{1,0:T(8,128)(2,1)S(1)}, bf16[1920,128]{1,0:T(8,128)(2,1)S(1)}, bf16[1920,128]{1,0:T(8,128)(2,1)S(1)}, bf16[1920,128]{1,0:T(8,128)(2,1)...) custom-call(f32[8,240,128]{2,1,0:T(8,128)} %coef_h.1, ...), custom_call_target="tpu_custom_call" | custom-call | tf_op jit(solution)/shard_map/send/pallas_call | solution.py:272
  6.0 1.7 %collective-permute-start = (bf16[960,128]{1,0:T(8,128)(2,1)S(1)}, bf16[960,128]{1,0:T(8,128)(2,1)S(1)}, u32[]{:S(2)}, u32[]{:S(2)}) collective-permute-start(bf16[960,128]{1,0:T(8,128)(2,1)S(1)} %get-tuple-element.50), channel_id=1, source_target_pairs={{0,1},{1,2},{2,3},{3,4},{4,5},{5,6},{6,7},{7,8},{8,9},{9,10},{10,1... | collective-permute-start | bytes 737288 | tf_op jit(solution)/shard_map/ppermute | solution.py:25
  7.6 4.8 %collective-permute-start.1 = (bf16[960,128]{1,0:T(8,128)(2,1)S(1)}, bf16[960,128]{1,0:T(8,128)(2,1)S(1)}, u32[]{:S(2)}, u32[]{:S(2)}) collective-permute-start(bf16[960,128]{1,0:T(8,128)(2,1)S(1)} %get-tuple-element.51), channel_id=1, source_target_pairs={{0,15},{1,0},{2,1},{3,2},{4,3},{5,4},{6,5},{7,6},{8,7},{9,8},{10,9... | collective-permute-start | bytes 737288 | tf_op jit(solution)/shard_map/ppermute | solution.py:25
  12.5 1.9 %collective-permute-start.8 = (f32[128,128]{1,0:T(8,128)S(1)}, f32[128,128]{1,0:T(8,128)S(1)}, u32[]{:S(2)}, u32[]{:S(2)}) collective-permute-start(f32[128,128]{1,0:T(8,128)S(1)} %get-tuple-element.92), channel_id=1, source_target_pairs={{0,12},{1,13},{2,14},{3,15},{4,0},{5,1},{6,2},{7,3},{8,4},{9,5},{1... | collective-permute-start | bytes 196616 | tf_op jit(solution)/shard_map/ppermute | solution.py:25
  14.5 1.7 %collective-permute-start.6 = (f32[128,128]{1,0:T(8,128)S(1)}, f32[128,128]{1,0:T(8,128)S(1)}, u32[]{:S(2)}, u32[]{:S(2)}) collective-permute-start(f32[128,128]{1,0:T(8,128)S(1)} %get-tuple-element.90), channel_id=1, source_target_pairs={{0,8},{1,9},{2,10},{3,11},{4,12},{5,13},{6,14},{7,15},{8,0},{9,1},... | collective-permute-start | bytes 196616 | tf_op jit(solution)/shard_map/ppermute | solution.py:25
  16.2 2.0 %shard_map.130 = (f32[240,1024]{1,0:T(8,128)S(1)}, bf16[1152,128]{1,0:T(8,128)(2,1)S(1)}, bf16[240,256]{1,0:T(8,128)(2,1)S(1)}, bf16[480,768]{1,0:T(8,128)(2,1)S(1)}) custom-call(bf16[1920,128]{1,0:T(8,128)(2,1)S(1)} %get-tuple-element.56.refs_0_, s32[24,128]{1,0:T(8,128)S(1)} %copy-done.8, s32[24,128]{1,0:T(8,128)S(1)} %copy-done.9, ...), custom_call_target="tpu_custom_call" | custom-call | flops 1260000000 | bytes 3000000 | tf_op jit(solution)/shard_map/pallas_call | solution.py:325
  18.2 1.9 %shard_map.131 = (f32[240,1024]{1,0:T(8,128)S(1)}, bf16[1152,128]{1,0:T(8,128)(2,1)S(1)}, bf16[240,256]{1,0:T(8,128)(2,1)S(1)}) custom-call(bf16[1920,128]{1,0:T(8,128)(2,1)S(1)} %get-tuple-element.58.refs_0_, s32[24,128]{1,0:T(8,128)S(1)} %copy-done.8, s32[24,128]{1,0:T(8,128)S(1)} %copy-done.9, bf16[8,240,240]{2,1,0:T(8,128)(2,1)S(1)} %copy-done.1, ...), custom_call_target="tpu_custom_call" | custom-call | flops 1260000000 | bytes 3000000 | tf_op jit(solution)/shard_map/pallas_call | solution.py:325
  20.1 1.9 %shard_map.133 = (f32[240,1024]{1,0:T(8,128)S(1)}, bf16[1152,128]{1,0:T(8,128)(2,1)S(1)}, bf16[240,256]{1,0:T(8,128)(2,1)S(1)}) custom-call(bf16[1920,128]{1,0:T(8,128)(2,1)S(1)} %get-tuple-element.63.refs_0_, s32[24,128]{1,0:T(8,128)S(1)} %copy-done.8, s32[24,128]{1,0:T(8,128)S(1)} %copy-done.9, bf16[8,240,240]{2,1,0:T(8,128)(2,1)S(1)} %copy-done.1, ...), custom_call_target="tpu_custom_call" | custom-call | flops 1260000000 | bytes 3000000 | tf_op jit(solution)/shard_map/pallas_call | solution.py:325
  22.0 1.9 %shard_map.134 = (f32[240,1024]{1,0:T(8,128)S(1)}, bf16[1152,128]{1,0:T(8,128)(2,1)S(1)}, bf16[240,256]{1,0:T(8,128)(2,1)S(1)}) custom-call(bf16[1920,128]{1,0:T(8,128)(2,1)S(1)} %get-tuple-element.65.refs_0_, s32[24,128]{1,0:T(8,128)S(1)} %copy-done.8, s32[24,128]{1,0:T(8,128)S(1)} %copy-done.9, bf16[8,240,240]{2,1,0:T(8,128)(2,1)S(1)} %copy-done.1, ...), custom_call_target="tpu_custom_call" | custom-call | flops 1260000000 | bytes 3000000 | tf_op jit(solution)/shard_map/pallas_call | solution.py:325
  24.0 1.9 %shard_map.136 = (f32[240,1024]{1,0:T(8,128)S(1)}, bf16[1152,128]{1,0:T(8,128)(2,1)S(1)}, bf16[240,256]{1,0:T(8,128)(2,1)S(1)}) custom-call(bf16[1920,128]{1,0:T(8,128)(2,1)S(1)} %get-tuple-element.69.refs_0_, s32[24,128]{1,0:T(8,128)S(1)} %copy-done.8, s32[24,128]{1,0:T(8,128)S(1)} %copy-done.9, bf16[8,240,240]{2,1,0:T(8,128)(2,1)S(1)} %copy-done.1, ...), custom_call_target="tpu_custom_call" | custom-call | flops 1260000000 | bytes 3000000 | tf_op jit(solution)/shard_map/pallas_call | solution.py:325
  26.0 1.6 %collective-permute-start.9 = (f32[128,128]{1,0:T(8,128)S(1)}, f32[128,128]{1,0:T(8,128)S(1)}, u32[]{:S(2)}, u32[]{:S(2)}) collective-permute-start(f32[128,128]{1,0:T(8,128)S(1)} %add_add_fusion.refs_0_), channel_id=1, source_target_pairs={{0,32},{16,48},{32,64},{48,80},{64,96},{80,112},{96,0},{112,16},{1... | collective-permute-start | bytes 196616 | tf_op jit(solution)/shard_map/ppermute | solution.py:25
  27.6 2.9 %collective-permute-start.10 = (f32[128,128]{1,0:T(8,128)S(1)}, f32[128,128]{1,0:T(8,128)S(1)}, u32[]{:S(2)}, u32[]{:S(2)}) collective-permute-start(f32[128,128]{1,0:T(8,128)S(1)} %add_add_fusion.refs_0_), channel_id=1, source_target_pairs={{0,64},{16,80},{32,96},{48,112},{64,0},{80,16},{96,32},{112,48},{1... | collective-permute-start | bytes 196616 | tf_op jit(solution)/shard_map/ppermute | solution.py:25
  31.8 1.9 %shard_map.137 = (f32[240,1024]{1,0:T(8,128)S(1)}, bf16[1152,128]{1,0:T(8,128)(2,1)S(1)}, bf16[240,256]{1,0:T(8,128)(2,1)S(1)}) custom-call(bf16[1920,128]{1,0:T(8,128)(2,1)S(1)} %get-tuple-element.71.refs_0_, s32[24,128]{1,0:T(8,128)S(1)} %copy-done.8, s32[24,128]{1,0:T(8,128)S(1)} %copy-done.9, bf16[8,240,240]{2,1,0:T(8,128)(2,1)S(1)} %copy-done.1, ...), custom_call_target="tpu_custom_call" | custom-call | flops 1260000000 | bytes 3000000 | tf_op jit(solution)/shard_map/pallas_call | solution.py:325
  34.8 4.7 %collective-permute-start.3 = (bf16[960,128]{1,0:T(8,128)(2,1)S(1)}, bf16[960,128]{1,0:T(8,128)(2,1)S(1)}, u32[]{:S(2)}, u32[]{:S(2)}) collective-permute-start(bf16[960,128]{1,0:T(8,128)(2,1)S(1)} %get-tuple-element.53), channel_id=1, source_target_pairs={{0,14},{1,15},{2,0},{3,1},{4,2},{5,3},{6,4},{7,5},{8,6},{9,7},{10,... | collective-permute-start | bytes 737288 | tf_op jit(solution)/shard_map/ppermute | solution.py:25
  41.1 1.9 %shard_map.139 = (f32[240,1024]{1,0:T(8,128)S(1)}, bf16[1152,128]{1,0:T(8,128)(2,1)S(1)}, bf16[240,256]{1,0:T(8,128)(2,1)S(1)}) custom-call(bf16[1920,128]{1,0:T(8,128)(2,1)S(1)} %get-tuple-element.75.refs_0_, s32[24,128]{1,0:T(8,128)S(1)} %copy-done.8, s32[24,128]{1,0:T(8,128)S(1)} %copy-done.9, bf16[8,240,240]{2,1,0:T(8,128)(2,1)S(1)} %copy-done.1, ...), custom_call_target="tpu_custom_call" | custom-call | flops 1260000000 | bytes 3000000 | tf_op jit(solution)/shard_map/pallas_call | solution.py:325
  43.6 2.5 %collective-permute-start.5 = (bf16[960,128]{1,0:T(8,128)(2,1)S(1)}, bf16[960,128]{1,0:T(8,128)(2,1)S(1)}, u32[]{:S(2)}, u32[]{:S(2)}) collective-permute-start(bf16[960,128]{1,0:T(8,128)(2,1)S(1)} %get-tuple-element.55), channel_id=1, source_target_pairs={{0,112},{16,0},{32,16},{48,32},{64,48},{80,64},{96,80},{112,96},{1... | collective-permute-start | bytes 737288 | tf_op jit(solution)/shard_map/ppermute | solution.py:25
  46.0 1.9 %shard_map.140 = (f32[240,1024]{1,0:T(8,128)S(1)}, bf16[1152,128]{1,0:T(8,128)(2,1)S(1)}, bf16[240,256]{1,0:T(8,128)(2,1)S(1)}) custom-call(bf16[1920,128]{1,0:T(8,128)(2,1)S(1)} %get-tuple-element.77.refs_0_, s32[24,128]{1,0:T(8,128)S(1)} %copy-done.8, s32[24,128]{1,0:T(8,128)S(1)} %copy-done.9, bf16[8,240,240]{2,1,0:T(8,128)(2,1)S(1)} %copy-done.1, ...), custom_call_target="tpu_custom_call" | custom-call | flops 1260000000 | bytes 3000000 | tf_op jit(solution)/shard_map/pallas_call | solution.py:325
  49.2 2.1 %collective-permute-start.14 = (f32[128,128]{1,0:T(8,128)S(1)}, f32[128,128]{1,0:T(8,128)S(1)}, u32[]{:S(2)}, u32[]{:S(2)}) collective-permute-start(f32[128,128]{1,0:T(8,128)S(1)} %add.24), channel_id=1, source_target_pairs={{0,1},{1,2},{2,3},{3,0},{4,5},{5,6},{6,7},{7,4},{8,9},{9,10},{10,1... | collective-permute-start | bytes 196616 | tf_op jit(solution)/shard_map/ppermute | solution.py:25
  53.5 1.4 %shard_map.132.refs_0_ = f32[2,240,1024]{2,1,0:T(8,128)S(1)} custom-call(bf16[1920,384]{1,0:T(8,128)(2,1)S(1)} %shard_map.127.m0, bf16[1920,384]{1,0:T(8,128)(2,1)S(1)} %shard_map.128.m1, bf16[1920,384]{1,0:T(8,128)(2,1)S(1)} %shard_map.129.m2, bf16[1152,128]{1,0:T(8,128)(2,1)S(1)} %get-tuple-element.57.sel_a, ...), custom_call_target="tpu_custom_call" | custom-call | flops 1200000000 | bytes 8000000 | tf_op jit(solution)/shard_map/pallas_call | solution.py:356
  55.0 1.5 %shard_map.135.refs_1_ = f32[2,240,1024]{2,1,0:T(8,128)S(1)} custom-call(bf16[1920,384]{1,0:T(8,128)(2,1)S(1)} %shard_map.127.m0, bf16[1920,384]{1,0:T(8,128)(2,1)S(1)} %shard_map.128.m1, bf16[1920,384]{1,0:T(8,128)(2,1)S(1)} %shard_map.129.m2, bf16[1152,128]{1,0:T(8,128)(2,1)S(1)} %get-tuple-element.64.sel_a, ...), custom_call_target="tpu_custom_call" | custom-call | flops 1200000000 | bytes 8000000 | tf_op jit(solution)/shard_map/pallas_call | solution.py:356
  56.5 1.5 %shard_map.138.refs_2_ = f32[2,240,1024]{2,1,0:T(8,128)S(1)} custom-call(bf16[1920,384]{1,0:T(8,128)(2,1)S(1)} %shard_map.127.m0, bf16[1920,384]{1,0:T(8,128)(2,1)S(1)} %shard_map.128.m1, bf16[1920,384]{1,0:T(8,128)(2,1)S(1)} %shard_map.129.m2, bf16[1152,128]{1,0:T(8,128)(2,1)S(1)} %get-tuple-element.70.sel_a, ...), custom_call_target="tpu_custom_call" | custom-call | flops 1200000000 | bytes 8000000 | tf_op jit(solution)/shard_map/pallas_call | solution.py:356
  60.1 1.8 %collective-permute-start.18 = (bf16[128,128]{1,0:T(8,128)(2,1)S(1)}, bf16[128,128]{1,0:T(8,128)(2,1)S(1)}, u32[]{:S(2)}, u32[]{:S(2)}) collective-permute-start(bf16[128,128]{1,0:T(8,128)(2,1)S(1)} %add_convert_fusion.refs_12_), channel_id=1, source_target_pairs={{0,12},{1,13},{2,14},{3,15},{4,0},{5,1},{6,2},{7,3},{8,4},{9,5},{1... | collective-permute-start | bytes 98312 | tf_op jit(solution)/shard_map/ppermute | solution.py:25
  61.9 1.5 %shard_map.141.refs_3_ = f32[2,240,1024]{2,1,0:T(8,128)S(1)} custom-call(bf16[1920,384]{1,0:T(8,128)(2,1)S(1)} %shard_map.127.m0, bf16[1920,384]{1,0:T(8,128)(2,1)S(1)} %shard_map.128.m1, bf16[1920,384]{1,0:T(8,128)(2,1)S(1)} %shard_map.129.m2, bf16[1152,128]{1,0:T(8,128)(2,1)S(1)} %get-tuple-element.76.sel_a, ...), custom_call_target="tpu_custom_call" | custom-call | flops 1200000000 | bytes 8000000 | tf_op jit(solution)/shard_map/pallas_call | solution.py:356
  64.6 3.2 %final.1 = f32[8,240,128]{2,1,0:T(8,128)} custom-call(f32[2,240,1024]{2,1,0:T(8,128)S(1)} %shard_map.132.refs_0_, f32[2,240,1024]{2,1,0:T(8,128)S(1)} %shard_map.135.refs_1_, f32[2,240,1024]{2,1,0:T(8,128)S(1)} %shard_map.138.refs_2_, f32[2,240,1024]{2,1,0:T(8,128)S(1)} %shard_map.141.refs_3_, bf16[240,256]{1,0:T(8,128)(2,1)S(1)} %get-tuple-element.81.refs_4_, ...), custom_call_target="tpu_custom_call" | custom-call | tf_op jit(solution)/shard_map/final/pallas_call | solution.py:365
  (55 shorter events, 11.4 us)
Async XLA Ops:
  0.0 16.2 %copy-start.1 = (bf16[8,240,240]{2,1,0:T(8,128)(2,1)S(1)}, bf16[8,240,240]{2,1,0:T(8,128)(2,1)}, u32[]{:S(2)}) copy-start(bf16[8,240,240]{2,1,0:T(8,128)(2,1)} %refs_3_.15) | copy-start | bytes 2764804
  0.0 16.2 %copy-start = (bf16[3,2,240,240]{3,2,1,0:T(8,128)(2,1)S(1)}, bf16[3,2,240,240]{3,2,1,0:T(8,128)(2,1)}, u32[]{:S(2)}) copy-start(bf16[3,2,240,240]{3,2,1,0:T(8,128)(2,1)} %refs_4_.2) | copy-start | bytes 2073604
  0.0 16.2 %copy-start.8 = (s32[24,128]{1,0:T(8,128)S(1)}, s32[24,128]{1,0:T(8,128)}, u32[]{:S(2)}) copy-start(s32[24,128]{1,0:T(8,128)} %refs_1_.15) | copy-start | bytes 36868
  0.0 16.2 %copy-start.9 = (s32[24,128]{1,0:T(8,128)S(1)}, s32[24,128]{1,0:T(8,128)}, u32[]{:S(2)}) copy-start(s32[24,128]{1,0:T(8,128)} %refs_2_.15) | copy-start | bytes 36868
  6.0 37.6 %collective-permute-start = (bf16[960,128]{1,0:T(8,128)(2,1)S(1)}, bf16[960,128]{1,0:T(8,128)(2,1)S(1)}, u32[]{:S(2)}, u32[]{:S(2)}) collective-permute-start(bf16[960,128]{1,0:T(8,128)(2,1)S(1)} %get-tuple-element.50), channel_id=1, source_target_pairs={{0,1},{1,2},{2,3},{3,4},{4,5},{5,6},{6,7},{7,8},{8,9},{9,10},{10,1... | collective-permute-start | bytes 737288 | tf_op jit(solution)/shard_map/ppermute | solution.py:25
  7.6 40.3 %collective-permute-start.1 = (bf16[960,128]{1,0:T(8,128)(2,1)S(1)}, bf16[960,128]{1,0:T(8,128)(2,1)S(1)}, u32[]{:S(2)}, u32[]{:S(2)}) collective-permute-start(bf16[960,128]{1,0:T(8,128)(2,1)S(1)} %get-tuple-element.51), channel_id=1, source_target_pairs={{0,15},{1,0},{2,1},{3,2},{4,3},{5,4},{6,5},{7,6},{8,7},{9,8},{10,9... | collective-permute-start | bytes 737288 | tf_op jit(solution)/shard_map/ppermute | solution.py:25
  12.5 13.4 %collective-permute-start.8 = (f32[128,128]{1,0:T(8,128)S(1)}, f32[128,128]{1,0:T(8,128)S(1)}, u32[]{:S(2)}, u32[]{:S(2)}) collective-permute-start(f32[128,128]{1,0:T(8,128)S(1)} %get-tuple-element.92), channel_id=1, source_target_pairs={{0,12},{1,13},{2,14},{3,15},{4,0},{5,1},{6,2},{7,3},{8,4},{9,5},{1... | collective-permute-start | bytes 196616 | tf_op jit(solution)/shard_map/ppermute | solution.py:25
  14.3 11.6 %collective-permute-start.7 = (f32[128,128]{1,0:T(8,128)S(1)}, f32[128,128]{1,0:T(8,128)S(1)}, u32[]{:S(2)}, u32[]{:S(2)}) collective-permute-start(f32[128,128]{1,0:T(8,128)S(1)} %get-tuple-element.91), channel_id=1, source_target_pairs={{0,4},{1,5},{2,6},{3,7},{4,8},{5,9},{6,10},{7,11},{8,12},{9,13},{1... | collective-permute-start | bytes 196616 | tf_op jit(solution)/shard_map/ppermute | solution.py:25
  14.5 11.4 %collective-permute-start.6 = (f32[128,128]{1,0:T(8,128)S(1)}, f32[128,128]{1,0:T(8,128)S(1)}, u32[]{:S(2)}, u32[]{:S(2)}) collective-permute-start(f32[128,128]{1,0:T(8,128)S(1)} %get-tuple-element.90), channel_id=1, source_target_pairs={{0,8},{1,9},{2,10},{3,11},{4,12},{5,13},{6,14},{7,15},{8,0},{9,1},... | collective-permute-start | bytes 196616 | tf_op jit(solution)/shard_map/ppermute | solution.py:25
  26.0 7.8 %collective-permute-start.9 = (f32[128,128]{1,0:T(8,128)S(1)}, f32[128,128]{1,0:T(8,128)S(1)}, u32[]{:S(2)}, u32[]{:S(2)}) collective-permute-start(f32[128,128]{1,0:T(8,128)S(1)} %add_add_fusion.refs_0_), channel_id=1, source_target_pairs={{0,32},{16,48},{32,64},{48,80},{64,96},{80,112},{96,0},{112,16},{1... | collective-permute-start | bytes 196616 | tf_op jit(solution)/shard_map/ppermute | solution.py:25
  27.6 7.2 %collective-permute-start.10 = (f32[128,128]{1,0:T(8,128)S(1)}, f32[128,128]{1,0:T(8,128)S(1)}, u32[]{:S(2)}, u32[]{:S(2)}) collective-permute-start(f32[128,128]{1,0:T(8,128)S(1)} %add_add_fusion.refs_0_), channel_id=1, source_target_pairs={{0,64},{16,80},{32,96},{48,112},{64,0},{80,16},{96,32},{112,48},{1... | collective-permute-start | bytes 196616 | tf_op jit(solution)/shard_map/ppermute | solution.py:25
  30.5 9.0 %collective-permute-start.11 = (f32[128,128]{1,0:T(8,128)S(1)}, f32[128,128]{1,0:T(8,128)S(1)}, u32[]{:S(2)}, u32[]{:S(2)}) collective-permute-start(f32[128,128]{1,0:T(8,128)S(1)} %add_add_fusion.refs_0_), channel_id=1, source_target_pairs={{0,96},{16,112},{32,0},{48,16},{64,32},{80,48},{96,64},{112,80},{1... | collective-permute-start | bytes 196616 | tf_op jit(solution)/shard_map/ppermute | solution.py:25
  31.8 7.7 %copy-start.3 = (f32[256,256]{1,0:T(8,128)S(1)}, f32[256,256]{1,0:T(8,128)}, u32[]{:S(2)}) copy-start(f32[256,256]{1,0:T(8,128)} %refs_4_.3) | copy-start | bytes 786436
  33.8 15.4 %collective-permute-start.2 = (bf16[960,128]{1,0:T(8,128)(2,1)S(1)}, bf16[960,128]{1,0:T(8,128)(2,1)S(1)}, u32[]{:S(2)}, u32[]{:S(2)}) collective-permute-start(bf16[960,128]{1,0:T(8,128)(2,1)S(1)} %get-tuple-element.52), channel_id=1, source_target_pairs={{0,2},{1,3},{2,4},{3,5},{4,6},{5,7},{6,8},{7,9},{8,10},{9,11},{10,... | collective-permute-start | bytes 737288 | tf_op jit(solution)/shard_map/ppermute | solution.py:25
  34.8 16.5 %collective-permute-start.3 = (bf16[960,128]{1,0:T(8,128)(2,1)S(1)}, bf16[960,128]{1,0:T(8,128)(2,1)S(1)}, u32[]{:S(2)}, u32[]{:S(2)}) collective-permute-start(bf16[960,128]{1,0:T(8,128)(2,1)S(1)} %get-tuple-element.53), channel_id=1, source_target_pairs={{0,14},{1,15},{2,0},{3,1},{4,2},{5,3},{6,4},{7,5},{8,6},{9,7},{10,... | collective-permute-start | bytes 737288 | tf_op jit(solution)/shard_map/ppermute | solution.py:25
  40.8 2.2 %collective-permute-start.12 = (f32[128,128]{1,0:T(8,128)S(1)}, f32[128,128]{1,0:T(8,128)S(1)}, u32[]{:S(2)}, u32[]{:S(2)}) collective-permute-start(f32[128,128]{1,0:T(8,128)S(1)} %get-tuple-element.94), channel_id=1, source_target_pairs={{0,16},{16,0},{32,48},{48,32},{64,80},{80,64},{96,112},{112,96},{1... | collective-permute-start | bytes 196616 | tf_op jit(solution)/shard_map/ppermute | solution.py:25
  43.1 9.3 %collective-permute-start.4 = (bf16[960,128]{1,0:T(8,128)(2,1)S(1)}, bf16[960,128]{1,0:T(8,128)(2,1)S(1)}, u32[]{:S(2)}, u32[]{:S(2)}) collective-permute-start(bf16[960,128]{1,0:T(8,128)(2,1)S(1)} %get-tuple-element.54), channel_id=1, source_target_pairs={{0,16},{16,32},{32,48},{48,64},{64,80},{80,96},{96,112},{112,0},{1... | collective-permute-start | bytes 737288 | tf_op jit(solution)/shard_map/ppermute | solution.py:25
  43.6 8.8 %collective-permute-start.5 = (bf16[960,128]{1,0:T(8,128)(2,1)S(1)}, bf16[960,128]{1,0:T(8,128)(2,1)S(1)}, u32[]{:S(2)}, u32[]{:S(2)}) collective-permute-start(bf16[960,128]{1,0:T(8,128)(2,1)S(1)} %get-tuple-element.55), channel_id=1, source_target_pairs={{0,112},{16,0},{32,16},{48,32},{64,48},{80,64},{96,80},{112,96},{1... | collective-permute-start | bytes 737288 | tf_op jit(solution)/shard_map/ppermute | solution.py:25
  48.0 10.0 %collective-permute-start.15 = (f32[128,128]{1,0:T(8,128)S(1)}, f32[128,128]{1,0:T(8,128)S(1)}, u32[]{:S(2)}, u32[]{:S(2)}) collective-permute-start(f32[128,128]{1,0:T(8,128)S(1)} %add.24), channel_id=1, source_target_pairs={{0,3},{1,0},{2,1},{3,2},{4,7},{5,4},{6,5},{7,6},{8,11},{9,8},{10,9... | collective-permute-start | bytes 196616 | tf_op jit(solution)/shard_map/ppermute | solution.py:25
  49.2 8.8 %collective-permute-start.14 = (f32[128,128]{1,0:T(8,128)S(1)}, f32[128,128]{1,0:T(8,128)S(1)}, u32[]{:S(2)}, u32[]{:S(2)}) collective-permute-start(f32[128,128]{1,0:T(8,128)S(1)} %add.24), channel_id=1, source_target_pairs={{0,1},{1,2},{2,3},{3,0},{4,5},{5,6},{6,7},{7,4},{8,9},{9,10},{10,1... | collective-permute-start | bytes 196616 | tf_op jit(solution)/shard_map/ppermute | solution.py:25
  51.3 6.7 %collective-permute-start.13 = (f32[128,128]{1,0:T(8,128)S(1)}, f32[128,128]{1,0:T(8,128)S(1)}, u32[]{:S(2)}, u32[]{:S(2)}) collective-permute-start(f32[128,128]{1,0:T(8,128)S(1)} %add.24), channel_id=1, source_target_pairs={{0,2},{1,3},{2,0},{3,1},{4,6},{5,7},{6,4},{7,5},{8,10},{9,11},{10,... | collective-permute-start | bytes 196616 | tf_op jit(solution)/shard_map/ppermute | solution.py:25
  58.0 5.4 %collective-permute-start.16 = (bf16[128,128]{1,0:T(8,128)(2,1)S(1)}, bf16[128,128]{1,0:T(8,128)(2,1)S(1)}, u32[]{:S(2)}, u32[]{:S(2)}) collective-permute-start(bf16[128,128]{1,0:T(8,128)(2,1)S(1)} %add_convert_fusion.refs_12_), channel_id=1, source_target_pairs={{0,4},{1,5},{2,6},{3,7},{4,8},{5,9},{6,10},{7,11},{8,12},{9,13},{1... | collective-permute-start | bytes 98312 | tf_op jit(solution)/shard_map/ppermute | solution.py:25
  59.1 5.4 %collective-permute-start.17 = (bf16[128,128]{1,0:T(8,128)(2,1)S(1)}, bf16[128,128]{1,0:T(8,128)(2,1)S(1)}, u32[]{:S(2)}, u32[]{:S(2)}) collective-permute-start(bf16[128,128]{1,0:T(8,128)(2,1)S(1)} %add_convert_fusion.refs_12_), channel_id=1, source_target_pairs={{0,8},{1,9},{2,10},{3,11},{4,12},{5,13},{6,14},{7,15},{8,0},{9,1},... | collective-permute-start | bytes 98312 | tf_op jit(solution)/shard_map/ppermute | solution.py:25
  60.1 4.4 %collective-permute-start.18 = (bf16[128,128]{1,0:T(8,128)(2,1)S(1)}, bf16[128,128]{1,0:T(8,128)(2,1)S(1)}, u32[]{:S(2)}, u32[]{:S(2)}) collective-permute-start(bf16[128,128]{1,0:T(8,128)(2,1)S(1)} %add_convert_fusion.refs_12_), channel_id=1, source_target_pairs={{0,12},{1,13},{2,14},{3,15},{4,0},{5,1},{6,2},{7,3},{8,4},{9,5},{1... | collective-permute-start | bytes 98312 | tf_op jit(solution)/shard_map/ppermute | solution.py:25
  (5 other events, 13.3 us)

commit v3 on v2

--- a/solution.py
+++ b/solution.py
@@ -25,9 +25,14 @@
     return lax.ppermute(value, axis, [(i, target(i)) for i in range(length)])
 
 
-def shifted(value, axis, by):
-    length = lax.axis_size(axis)
-    return moved_by(value, axis, lambda i: (i + by) % length)
+def flipped(value, axis, bits):
+    return moved_by(value, axis, lambda i: i ^ bits)
+
+
+def upper_sides():
+    m = lax.axis_index("mem")
+    g = lax.axis_index("grp")
+    return lax.rem(m, 2), lax.rem(m // 2, 2), lax.rem(g, 2)
 
 
 def packed_complex(mat, cols):
@@ -40,8 +45,8 @@
 def send_kernel(coef_h, rot_h, send_h, crot_h, cid_h, up_h, *rest):
     pools = rest[:8]
     outs = rest[8:14]
-    fars = rest[14:18]
-    coef, rot, send, crot, cid, up, xs, sel, whole, sems = rest[18:]
+    fars = rest[14:16]
+    coef, rot, send, crot, cid, up, xs, sel, whole, sems = rest[16:]
     pairs = ((coef_h, coef), (rot_h, rot), (send_h, send), (crot_h, crot), (cid_h, cid), (up_h, up))
     copies = [pltpu.make_async_copy(src, dst, sems.at[i]) for i, (src, dst) in enumerate(pairs)]
     for copy in copies:
@@ -51,8 +56,13 @@
     for i in (2, 3, 4):
         copies[i].wait()
     rows = iota((n_r * n_i, 128), 0)
-    for q in range(3):
-        ids = jnp.concatenate([send[2 * q : 2 * q + 1, :], send[2 * q + 1 : 2 * q + 2, :]], axis=1)
+    for q, upper in enumerate(upper_sides()):
+        up_row, down_row = send[2 * q : 2 * q + 1, :], send[2 * q + 1 : 2 * q + 2, :]
+        ids = jnp.where(
+            upper == 1,
+            jnp.concatenate([down_row, up_row], axis=1),
+            jnp.concatenate([up_row, down_row], axis=1),
+        )
         sel[:, q * 128 : (q + 1) * 128] = jnp.where(rows == ids, 1.0, 0.0).astype(BF)
     key = (crot[...] * 32 + cid[...]).astype(F32)
     key_t = jnp.transpose(jnp.broadcast_to(key, (n_i, n_i)))
@@ -95,10 +105,10 @@
             packed_complex(mat, lo) + packed_complex(mat, mid) + packed_complex(mat, hi)
         )
     whole[2 * n_k :, :] = jnp.zeros((512 - 2 * n_k, 128), F32)
-    z = lax.axis_index("mem") // 4
-    for k in range(4):
-        at = pl.multiple_of(lax.rem(z + k, 4) * 128, 128)
-        fars[k][...] = whole[pl.ds(at, 128), :]
+    place = lax.rem(lax.axis_index("mem"), 4)
+    for k, flip in enumerate((0, 1, 3, 2)):
+        at = pl.multiple_of(lax.bitwise_xor(place, flip) * 128, 128)
+        fars[k // 2][k % 2 * 128 : k % 2 * 128 + 128, :] = whole[pl.ds(at, 128), :]
 
 
 def own_kernel(r, *refs):
@@ -135,12 +145,13 @@
     g_out[:, :half] = both[:n_k, :half] - both[n_k:, half:]
     g_out[:, half:] = both[n_k:, :half] + both[:n_k, half:]
     keys = jnp.where(pcol[...] >= 1024, pcol[...] - 1024 + prot[...] * 384, -1)
-    for pair in range(3):
+    for pair, upper in enumerate(upper_sides()):
+        cols = lax.bitwise_xor(js, 64 - 64 * upper) + pair * 128 + r * 384
         for s in range(3):
             total = jnp.zeros((n_i, n_i), F32)
             for t in range(8):
                 row = keys[s * 8 + t : s * 8 + t + 1, :]
-                total = total + jnp.where(row == js + pair * 128 + r * 384, 1.0, 0.0)
+                total = total + jnp.where(row == cols, 1.0, 0.0)
             at = (pair * 3 + s) * 128
             sel_out[at : at + 128, :] = total.astype(BF)
 
@@ -178,16 +189,16 @@
 
 
 def reach_kernel(*refs):
-    blocks = refs[:4]
-    coupling, own, other = refs[4:]
+    halves = refs[:2]
+    coupling, own, other = refs[2:]
     me = lax.axis_index("grp")
     lanes = iota((32, 128), 1)
     outs = []
-    for target in (me, me + 1 - 2 * lax.rem(me, 2)):
+    for target in (me, lax.bitwise_xor(me, 1)):
         row_at = pl.multiple_of(target * 32, 32)
         total = jnp.zeros((128, 128), F32)
-        for k in range(4):
-            gs = lax.rem(me + 8 - 2 * k, 8)
+        for k, flip in enumerate((0, 2, 6, 4)):
+            gs = lax.bitwise_xor(me, flip)
             col_at = pl.multiple_of(gs // 4 * 128, 128)
             window = coupling[pl.ds(row_at, 32), pl.ds(col_at, 128)]
             same = lanes + col_at == iota((32, 128), 0) + row_at
@@ -198,7 +209,7 @@
                 turned = pltpu.roll(window, by, 1)
                 parts.append(jnp.where((lanes >= q * 32) & (lanes < q * 32 + 32), turned, 0.0))
             total = total + lax.dot_general(
-                blocks[k][...],
+                halves[k // 2][k % 2 * 128 : k % 2 * 128 + 128, :],
                 jnp.concatenate(parts, axis=0),
                 (((1,), (1,)), ((), ())),
                 preferred_element_type=F32,
@@ -212,13 +223,13 @@
 def final_kernel(*refs):
     gs = refs[:4]
     rts = refs[4:12]
-    fars = refs[12:16]
-    far_axial, cid, crot, incident, mie, out, gb, fin, fsum = refs[16:]
+    fars = refs[12:14]
+    far_axial, cid, crot, incident, mie, out, gb, fin, fsum = refs[14:]
     n_k = 240
-    z = lax.axis_index("mem") // 4
-    for k in range(4):
-        at = pl.multiple_of(lax.rem(z + 4 - k, 4) * 128, 128)
-        fin[pl.ds(at, 128), :] = fars[k][...]
+    place = lax.rem(lax.axis_index("mem"), 4)
+    for k, flip in enumerate((0, 1, 3, 2)):
+        at = pl.multiple_of(lax.bitwise_xor(place, flip) * 128, 128)
+        fin[pl.ds(at, 128), :] = fars[k // 2][k % 2 * 128 : k % 2 * 128 + 128, :]
     mat = far_axial[...].reshape(2 * n_k, n_k)
     ids = jnp.broadcast_to(cid[...], (n_k, 128))
     for xh in range(2):
@@ -271,9 +282,9 @@
     crot = center_rot.reshape(1, 128)
     first = pl.pallas_call(
         send_kernel,
-        out_shape=[sds((1920, 128), BF)] * 8 + [sds((960, 128), BF)] * 6 + [sds((128, 128), F32)] * 4,
+        out_shape=[sds((1920, 128), BF)] * 8 + [sds((960, 128), BF)] * 6 + [sds((256, 128), F32)] * 2,
         in_specs=[pl.BlockSpec(memory_space=pltpu.MemorySpace.HBM)] * 6,
-        out_specs=[VM] * 18,
+        out_specs=[VM] * 16,
         scratch_shapes=[
             pltpu.VMEM((8, 240, 128), F32),
             pltpu.VMEM((8, 240, 240), BF),
@@ -291,34 +302,37 @@
     )(*[pltpu.with_memory_space_constraint(v, pltpu.HBM) for v in (coefficients, rot_table, send_col, crot, cid, up_axial)])
     pools = first[:8]
     sends = first[8:14]
-    fars = first[14:18]
-    moves = (("mem", 1), ("mem", -1), ("mem", 2), ("mem", -2), ("grp", 1), ("grp", -1))
+    near_blocks, far_blocks = first[14:]
     got = []
-    for p in range(6):
-        got.append(shifted(sends[p], *moves[p]))
-    acc = fars[0]
-    for k in (2, 1, 3):
-        come = shifted(fars[k], "mem", 4 * k)
-        acc = acc + come
-    blocks = [acc]
-    for k in (1, 2, 3):
-        blocks.append(shifted(acc, "grp", 2 * k))
+    for q, (axis, bit) in enumerate((("mem", 1), ("mem", 2), ("grp", 1))):
+        got.append(flipped(sends[2 * q], axis, bit))
+        size = lax.axis_size(axis)
+        got.append(
+            moved_by(sends[2 * q + 1], axis, lambda i: (i + (bit if i & bit else -bit)) % size)
+        )
+    come = flipped(far_blocks, "mem", 3)
+    come_next = flipped(near_blocks[128:] + come[128:], "mem", 1)
+    acc = near_blocks[:128] + come[:128] + come_next
+    come = flipped(acc, "grp", 2)
+    pair = jnp.concatenate([acc, come], axis=0)
+    come = flipped(pair, "grp", 6)
     mine, theirs = pl.pallas_call(
         reach_kernel,
         out_shape=[sds((128, 128), F32)] * 2,
-        in_specs=[VM] * 5,
+        in_specs=[VM] * 3,
         out_specs=[VM] * 2,
         compiler_params=params(2),
         name="reach",
-    )(*blocks, coupling)
-    come = moved_by(theirs, "grp", lambda i: i ^ 1)
-    part = mine + come
-    total = part
-    for k in (2, 1, 3):
-        total = total + moved_by(part, "mem", lambda i: i // 4 * 4 + (i + k) % 4)
-    reached = [total.astype(BF)]
-    for k in (1, 2, 3):
-        reached.append(shifted(reached[0], "mem", 4 * k))
+    )(pair, come, coupling)
+    come = flipped(theirs, "grp", 1)
+    total = mine + come
+    for flip in (4, 12):
+        come = flipped(total, "mem", flip)
+        total = total + come
+    total = total.astype(BF)
+    come = flipped(total, "mem", 1)
+    reached = [jnp.concatenate([total, come], axis=0)]
+    reached.append(flipped(reached[0], "mem", 3))
     g_own, sels, rts = [], [], []
     mats = None
     for r in range(8):
@@ -365,7 +379,7 @@
     return pl.pallas_call(
         final_kernel,
         out_shape=sds((8, 240, 128), F32),
-        in_specs=[VM] * 21,
+        in_specs=[VM] * 19,
         out_specs=VM,
         scratch_shapes=[
             pltpu.VMEM((2048, 1024), BF),

time: 68.4 us -> 75.6 us (1.11)
  waiting for transfers between devices: 1.17 us -> 15.2 us
  starting transfers between devices: 31.1 us -> 24.4 us
    ppermute x19 -> x15, waiting for transfers between devices: 1.17 us -> 15.2 us  [moved_by(): return lax.ppermute(value, axis, [(i, target(i)) for i in range(length)])]
    ppermute x19 -> x15, starting transfers between devices: 31.1 us -> 24.4 us  [moved_by(): return lax.ppermute(value, axis, [(i, target(i)) for i in range(length)])]
  transfers between devices with their start and end apart: 19 -> 15, of which waited for: 1 -> 8; matrix products, arithmetic and copies ran while one was open for 0% -> 0% of each run, Pallas kernels for 38% -> 35%
where the time goes in v3:
time: 75.6 us; the launch traced here: 75.1 us
  Pallas kernels  35.1 us (46%)
  starting transfers between devices  24.4 us (32%)
  waiting for transfers between devices  15.2 us (20%)
    ppermute x15, starting transfers between devices, moved_by(): return lax.ppermute(value, axis, [(i, target(i)) for i in range(length)])  24.4 us
    pallas_call x8, Pallas kernels, on_device(): pl.pallas_call(lambda *refs, r=r: own_kernel(r, *refs), out_shape=[sds((2...  15.5 us
    ppermute x15, waiting for transfers between devices, moved_by(): return lax.ppermute(value, axis, [(i, target(i)) for i in range(length)])  15.2 us
    pallas_call x1, Pallas kernels, on_device(): pl.pallas_call(send_kernel, out_shape=[sds((1920, 128), BF)] * 8 + [sds((...  5.93 us
    pallas_call x4, Pallas kernels, on_device(): pl.pallas_call(recv_kernel, out_shape=sds((2, 240, 1024), F32), in_specs=...  5.88 us
    pallas_call x3, Pallas kernels, on_device(): pl.pallas_call(lift_kernel, out_shape=sds((1920, 384), BF), in_specs=[VM]...  3.32 us
    pallas_call x1, Pallas kernels, on_device(): pl.pallas_call(final_kernel, out_shape=sds((8, 240, 128), F32), in_specs=...  3.22 us
  transfers between devices with their start and end apart: 15, of which 8 were waited for; matrix products, arithmetic and copies ran while one was open for 0% of the time, Pallas kernels for 35%

profile of v3, /device:TPU:0, one launch (start us, length us, event | category | flops | bytes accessed | tf_op | source)
XLA Modules:
  0.0 75.1 jit_solution(2092877122193282891)
XLA Ops:
  0.0 5.9 %send.1 = (bf16[1920,128]{1,0:T(8,128)(2,1)S(1)}, bf16[1920,128]{1,0:T(8,128)(2,1)S(1)}, bf16[1920,128]{1,0:T(8,128)(2,1)S(1)}, bf16[1920,128]{1,0:T(8,128)(2,1)...) custom-call(f32[8,240,128]{2,1,0:T(8,128)} %coef_h.1, ...), custom_call_target="tpu_custom_call" | custom-call | tf_op jit(solution)/shard_map/send/pallas_call | solution.py:283
  5.9 1.7 %collective-permute-start = (bf16[960,128]{1,0:T(8,128)(2,1)S(1)}, bf16[960,128]{1,0:T(8,128)(2,1)S(1)}, u32[]{:S(2)}, u32[]{:S(2)}) collective-permute-start(bf16[960,128]{1,0:T(8,128)(2,1)S(1)} %get-tuple-element.48), channel_id=1, source_target_pairs={{0,1},{1,0},{2,3},{3,2},{4,5},{5,4},{6,7},{7,6},{8,9},{9,8},{10,11... | collective-permute-start | bytes 737288 | tf_op jit(solution)/shard_map/ppermute | solution.py:25
  7.6 5.6 %collective-permute-start.1 = (bf16[960,128]{1,0:T(8,128)(2,1)S(1)}, bf16[960,128]{1,0:T(8,128)(2,1)S(1)}, u32[]{:S(2)}, u32[]{:S(2)}) collective-permute-start(bf16[960,128]{1,0:T(8,128)(2,1)S(1)} %get-tuple-element.49), channel_id=1, source_target_pairs={{0,15},{1,2},{2,1},{3,4},{4,3},{5,6},{6,5},{7,8},{8,7},{9,10},{10,... | collective-permute-start | bytes 737288 | tf_op jit(solution)/shard_map/ppermute | solution.py:25
  13.2 3.4 %collective-permute-start.3 = (bf16[960,128]{1,0:T(8,128)(2,1)S(1)}, bf16[960,128]{1,0:T(8,128)(2,1)S(1)}, u32[]{:S(2)}, u32[]{:S(2)}) collective-permute-start(bf16[960,128]{1,0:T(8,128)(2,1)S(1)} %get-tuple-element.51), channel_id=1, source_target_pairs={{0,14},{1,15},{2,4},{3,5},{4,2},{5,3},{6,8},{7,9},{8,6},{9,7},{10,... | collective-permute-start | bytes 737288 | tf_op jit(solution)/shard_map/ppermute | solution.py:25
  17.1 2.0 %shard_map.130 = (f32[240,1024]{1,0:T(8,128)S(1)}, bf16[1152,128]{1,0:T(8,128)(2,1)S(1)}, bf16[240,256]{1,0:T(8,128)(2,1)S(1)}, bf16[480,768]{1,0:T(8,128)(2,1)S(1)}) custom-call(bf16[1920,128]{1,0:T(8,128)(2,1)S(1)} %get-tuple-element.54.refs_0_, s32[24,128]{1,0:T(8,128)S(1)} %copy-done.8, s32[24,128]{1,0:T(8,128)S(1)} %copy-done.9, ...), custom_call_target="tpu_custom_call" | custom-call | flops 1260000000 | bytes 3000000 | tf_op jit(solution)/shard_map/pallas_call | solution.py:339
  19.1 1.9 %shard_map.131 = (f32[240,1024]{1,0:T(8,128)S(1)}, bf16[1152,128]{1,0:T(8,128)(2,1)S(1)}, bf16[240,256]{1,0:T(8,128)(2,1)S(1)}) custom-call(bf16[1920,128]{1,0:T(8,128)(2,1)S(1)} %get-tuple-element.56.refs_0_, s32[24,128]{1,0:T(8,128)S(1)} %copy-done.8, s32[24,128]{1,0:T(8,128)S(1)} %copy-done.9, bf16[8,240,240]{2,1,0:T(8,128)(2,1)S(1)} %copy-done.1, ...), custom_call_target="tpu_custom_call" | custom-call | flops 1260000000 | bytes 3000000 | tf_op jit(solution)/shard_map/pallas_call | solution.py:339
  21.0 1.9 %shard_map.133 = (f32[240,1024]{1,0:T(8,128)S(1)}, bf16[1152,128]{1,0:T(8,128)(2,1)S(1)}, bf16[240,256]{1,0:T(8,128)(2,1)S(1)}) custom-call(bf16[1920,128]{1,0:T(8,128)(2,1)S(1)} %get-tuple-element.61.refs_0_, s32[24,128]{1,0:T(8,128)S(1)} %copy-done.8, s32[24,128]{1,0:T(8,128)S(1)} %copy-done.9, bf16[8,240,240]{2,1,0:T(8,128)(2,1)S(1)} %copy-done.1, ...), custom_call_target="tpu_custom_call" | custom-call | flops 1260000000 | bytes 3000000 | tf_op jit(solution)/shard_map/pallas_call | solution.py:339
  23.0 1.9 %shard_map.134 = (f32[240,1024]{1,0:T(8,128)S(1)}, bf16[1152,128]{1,0:T(8,128)(2,1)S(1)}, bf16[240,256]{1,0:T(8,128)(2,1)S(1)}) custom-call(bf16[1920,128]{1,0:T(8,128)(2,1)S(1)} %get-tuple-element.63.refs_0_, s32[24,128]{1,0:T(8,128)S(1)} %copy-done.8, s32[24,128]{1,0:T(8,128)S(1)} %copy-done.9, bf16[8,240,240]{2,1,0:T(8,128)(2,1)S(1)} %copy-done.1, ...), custom_call_target="tpu_custom_call" | custom-call | flops 1260000000 | bytes 3000000 | tf_op jit(solution)/shard_map/pallas_call | solution.py:339
  24.9 1.9 %shard_map.136 = (f32[240,1024]{1,0:T(8,128)S(1)}, bf16[1152,128]{1,0:T(8,128)(2,1)S(1)}, bf16[240,256]{1,0:T(8,128)(2,1)S(1)}) custom-call(bf16[1920,128]{1,0:T(8,128)(2,1)S(1)} %get-tuple-element.67.refs_0_, s32[24,128]{1,0:T(8,128)S(1)} %copy-done.8, s32[24,128]{1,0:T(8,128)S(1)} %copy-done.9, bf16[8,240,240]{2,1,0:T(8,128)(2,1)S(1)} %copy-done.1, ...), custom_call_target="tpu_custom_call" | custom-call | flops 1260000000 | bytes 3000000 | tf_op jit(solution)/shard_map/pallas_call | solution.py:339
  26.9 1.9 %shard_map.137 = (f32[240,1024]{1,0:T(8,128)S(1)}, bf16[1152,128]{1,0:T(8,128)(2,1)S(1)}, bf16[240,256]{1,0:T(8,128)(2,1)S(1)}) custom-call(bf16[1920,128]{1,0:T(8,128)(2,1)S(1)} %get-tuple-element.69.refs_0_, s32[24,128]{1,0:T(8,128)S(1)} %copy-done.8, s32[24,128]{1,0:T(8,128)S(1)} %copy-done.9, bf16[8,240,240]{2,1,0:T(8,128)(2,1)S(1)} %copy-done.1, ...), custom_call_target="tpu_custom_call" | custom-call | flops 1260000000 | bytes 3000000 | tf_op jit(solution)/shard_map/pallas_call | solution.py:339
  28.8 2.2 %collective-permute-done.6 = f32[256,128]{1,0:T(8,128)S(1)} collective-permute-done((f32[256,128]{1,0:T(8,128)S(1)}, f32[256,128]{1,0:T(8,128)S(1)}, u32[]{:S(2)}, u32[]{:S(2)}) %collective-permute-start.6) | collective-permute-done | bytes 131104 | tf_op jit(solution)/shard_map/ppermute | solution.py:25
  31.1 1.9 %shard_map.139 = (f32[240,1024]{1,0:T(8,128)S(1)}, bf16[1152,128]{1,0:T(8,128)(2,1)S(1)}, bf16[240,256]{1,0:T(8,128)(2,1)S(1)}) custom-call(bf16[1920,128]{1,0:T(8,128)(2,1)S(1)} %get-tuple-element.73.refs_0_, s32[24,128]{1,0:T(8,128)S(1)} %copy-done.8, s32[24,128]{1,0:T(8,128)S(1)} %copy-done.9, bf16[8,240,240]{2,1,0:T(8,128)(2,1)S(1)} %copy-done.1, ...), custom_call_target="tpu_custom_call" | custom-call | flops 1260000000 | bytes 3000000 | tf_op jit(solution)/shard_map/pallas_call | solution.py:339
  33.0 2.3 %collective-permute-done.7 = f32[128,128]{1,0:T(8,128)S(1)} collective-permute-done((f32[128,128]{1,0:T(8,128)S(1)}, f32[128,128]{1,0:T(8,128)S(1)}, u32[]{:S(2)}, u32[]{:S(2)}) %collective-permute-start.7) | collective-permute-done | bytes 65568 | tf_op jit(solution)/shard_map/ppermute | solution.py:25
  35.4 1.9 %collective-permute-start.8 = (f32[128,128]{1,0:T(8,128)S(1)}, f32[128,128]{1,0:T(8,128)S(1)}, u32[]{:S(2)}, u32[]{:S(2)}) collective-permute-start(f32[128,128]{1,0:T(8,128)S(1)} %fusion), channel_id=1, source_target_pairs={{0,32},{16,48},{32,0},{48,16},{64,96},{80,112},{96,64},{112,80},{1... | collective-permute-start | bytes 196616 | tf_op jit(solution)/shard_map/ppermute | solution.py:25
  37.3 1.9 %shard_map.140 = (f32[240,1024]{1,0:T(8,128)S(1)}, bf16[1152,128]{1,0:T(8,128)(2,1)S(1)}, bf16[240,256]{1,0:T(8,128)(2,1)S(1)}) custom-call(bf16[1920,128]{1,0:T(8,128)(2,1)S(1)} %get-tuple-element.75.refs_0_, s32[24,128]{1,0:T(8,128)S(1)} %copy-done.8, s32[24,128]{1,0:T(8,128)S(1)} %copy-done.9, bf16[8,240,240]{2,1,0:T(8,128)(2,1)S(1)} %copy-done.1, ...), custom_call_target="tpu_custom_call" | custom-call | flops 1260000000 | bytes 3000000 | tf_op jit(solution)/shard_map/pallas_call | solution.py:339
  39.9 1.6 %collective-permute-start.5 = (bf16[960,128]{1,0:T(8,128)(2,1)S(1)}, bf16[960,128]{1,0:T(8,128)(2,1)S(1)}, u32[]{:S(2)}, u32[]{:S(2)}) collective-permute-start(bf16[960,128]{1,0:T(8,128)(2,1)S(1)} %get-tuple-element.53), channel_id=1, source_target_pairs={{0,112},{16,32},{32,16},{48,64},{64,48},{80,96},{96,80},{112,0},{1... | collective-permute-start | bytes 737288 | tf_op jit(solution)/shard_map/ppermute | solution.py:25
  45.3 3.9 %collective-permute-done.9.refs_1_ = f32[256,128]{1,0:T(8,128)S(1)} collective-permute-done((f32[256,128]{1,0:T(8,128)S(1)}, f32[256,128]{1,0:T(8,128)S(1)}, u32[]{:S(2)}, u32[]{:S(2)}) %collective-permute-start.9) | collective-permute-done | bytes 131104 | tf_op jit(solution)/shard_map/ppermute | solution.py:25
  51.9 2.0 %collective-permute-start.11 = (f32[128,128]{1,0:T(8,128)S(1)}, f32[128,128]{1,0:T(8,128)S(1)}, u32[]{:S(2)}, u32[]{:S(2)}) collective-permute-start(f32[128,128]{1,0:T(8,128)S(1)} %add.21), channel_id=1, source_target_pairs={{0,4},{1,5},{2,6},{3,7},{4,0},{5,1},{6,2},{7,3},{8,12},{9,13},{10,... | collective-permute-start | bytes 196616 | tf_op jit(solution)/shard_map/ppermute | solution.py:25
  56.5 2.3 %collective-permute-start.12 = (f32[128,128]{1,0:T(8,128)S(1)}, f32[128,128]{1,0:T(8,128)S(1)}, u32[]{:S(2)}, u32[]{:S(2)}) collective-permute-start(f32[128,128]{1,0:T(8,128)S(1)} %add.22), channel_id=1, source_target_pairs={{0,12},{1,13},{2,14},{3,15},{4,8},{5,9},{6,10},{7,11},{8,4},{9,5},... | collective-permute-start | bytes 196616 | tf_op jit(solution)/shard_map/ppermute | solution.py:25
  60.3 1.8 %collective-permute-done.12 = f32[128,128]{1,0:T(8,128)S(1)} collective-permute-done((f32[128,128]{1,0:T(8,128)S(1)}, f32[128,128]{1,0:T(8,128)S(1)}, u32[]{:S(2)}, u32[]{:S(2)}) %collective-permute-start.12) | collective-permute-done | bytes 65568 | tf_op jit(solution)/shard_map/ppermute | solution.py:25
  63.7 2.4 %collective-permute-done.13 = bf16[128,128]{1,0:T(8,128)(2,1)S(1)} collective-permute-done((bf16[128,128]{1,0:T(8,128)(2,1)S(1)}, bf16[128,128]{1,0:T(8,128)(2,1)S(1)}, u32[]{:S(2)}, u32[]{:S(2)}) %collective-permute-start.13) | collective-permute-done | bytes 32800 | tf_op jit(solution)/shard_map/ppermute | solution.py:25
  66.1 3.6 %collective-permute-start.14 = (bf16[256,128]{1,0:T(8,128)(2,1)S(1)}, bf16[256,128]{1,0:T(8,128)(2,1)S(1)}, u32[]{:S(2)}, u32[]{:S(2)}) collective-permute-start(bf16[256,128]{1,0:T(8,128)(2,1)S(1)} %pad_maximum_fusion.1.refs_12_), channel_id=1, source_target_pairs={{0,3},{1,2},{2,1},{3,0},{4,7},{5,6},{6,5},{7,4},{8,11},{9,10},{10,... | collective-permute-start | bytes 196616 | tf_op jit(solution)/shard_map/ppermute | solution.py:25
  69.7 1.5 %shard_map.141.refs_3_ = f32[2,240,1024]{2,1,0:T(8,128)S(1)} custom-call(bf16[1920,384]{1,0:T(8,128)(2,1)S(1)} %shard_map.127.m0, bf16[1920,384]{1,0:T(8,128)(2,1)S(1)} %shard_map.128.m1, bf16[1920,384]{1,0:T(8,128)(2,1)S(1)} %shard_map.129.m2, bf16[1152,128]{1,0:T(8,128)(2,1)S(1)} %get-tuple-element.74.sel_a, ...), custom_call_target="tpu_custom_call" | custom-call | flops 1200000000 | bytes 8000000 | tf_op jit(solution)/shard_map/pallas_call | solution.py:370
  71.9 3.2 %final.1 = f32[8,240,128]{2,1,0:T(8,128)} custom-call(f32[2,240,1024]{2,1,0:T(8,128)S(1)} %shard_map.132.refs_0_, f32[2,240,1024]{2,1,0:T(8,128)S(1)} %shard_map.135.refs_1_, f32[2,240,1024]{2,1,0:T(8,128)S(1)} %shard_map.138.refs_2_, f32[2,240,1024]{2,1,0:T(8,128)S(1)} %shard_map.141.refs_3_, bf16[240,256]{1,0:T(8,128)(2,1)S(1)} %get-tuple-element.79.refs_4_, ...), custom_call_target="tpu_custom_call" | custom-call | tf_op jit(solution)/shard_map/final/pallas_call | solution.py:379
  (51 shorter events, 14.1 us)
Async XLA Ops:
  0.0 17.1 %copy-start.1 = (bf16[8,240,240]{2,1,0:T(8,128)(2,1)S(1)}, bf16[8,240,240]{2,1,0:T(8,128)(2,1)}, u32[]{:S(2)}) copy-start(bf16[8,240,240]{2,1,0:T(8,128)(2,1)} %refs_3_.15) | copy-start | bytes 2764804
  0.0 17.1 %copy-start = (bf16[3,2,240,240]{3,2,1,0:T(8,128)(2,1)S(1)}, bf16[3,2,240,240]{3,2,1,0:T(8,128)(2,1)}, u32[]{:S(2)}) copy-start(bf16[3,2,240,240]{3,2,1,0:T(8,128)(2,1)} %refs_4_.1) | copy-start | bytes 2073604
  0.0 17.1 %copy-start.8 = (s32[24,128]{1,0:T(8,128)S(1)}, s32[24,128]{1,0:T(8,128)}, u32[]{:S(2)}) copy-start(s32[24,128]{1,0:T(8,128)} %refs_1_.15) | copy-start | bytes 36868
  0.0 17.1 %copy-start.9 = (s32[24,128]{1,0:T(8,128)S(1)}, s32[24,128]{1,0:T(8,128)}, u32[]{:S(2)}) copy-start(s32[24,128]{1,0:T(8,128)} %refs_2_.16) | copy-start | bytes 36868
  5.9 33.3 %collective-permute-start = (bf16[960,128]{1,0:T(8,128)(2,1)S(1)}, bf16[960,128]{1,0:T(8,128)(2,1)S(1)}, u32[]{:S(2)}, u32[]{:S(2)}) collective-permute-start(bf16[960,128]{1,0:T(8,128)(2,1)S(1)} %get-tuple-element.48), channel_id=1, source_target_pairs={{0,1},{1,0},{2,3},{3,2},{4,5},{5,4},{6,7},{7,6},{8,9},{9,8},{10,11... | collective-permute-start | bytes 737288 | tf_op jit(solution)/shard_map/ppermute | solution.py:25
  7.6 34.0 %collective-permute-start.1 = (bf16[960,128]{1,0:T(8,128)(2,1)S(1)}, bf16[960,128]{1,0:T(8,128)(2,1)S(1)}, u32[]{:S(2)}, u32[]{:S(2)}) collective-permute-start(bf16[960,128]{1,0:T(8,128)(2,1)S(1)} %get-tuple-element.49), channel_id=1, source_target_pairs={{0,15},{1,2},{2,1},{3,4},{4,3},{5,6},{6,5},{7,8},{8,7},{9,10},{10,... | collective-permute-start | bytes 737288 | tf_op jit(solution)/shard_map/ppermute | solution.py:25
  13.2 31.0 %collective-permute-start.2 = (bf16[960,128]{1,0:T(8,128)(2,1)S(1)}, bf16[960,128]{1,0:T(8,128)(2,1)S(1)}, u32[]{:S(2)}, u32[]{:S(2)}) collective-permute-start(bf16[960,128]{1,0:T(8,128)(2,1)S(1)} %get-tuple-element.50), channel_id=1, source_target_pairs={{0,2},{1,3},{2,0},{3,1},{4,6},{5,7},{6,4},{7,5},{8,10},{9,11},{10,... | collective-permute-start | bytes 737288 | tf_op jit(solution)/shard_map/ppermute | solution.py:25
  13.2 31.0 %collective-permute-start.3 = (bf16[960,128]{1,0:T(8,128)(2,1)S(1)}, bf16[960,128]{1,0:T(8,128)(2,1)S(1)}, u32[]{:S(2)}, u32[]{:S(2)}) collective-permute-start(bf16[960,128]{1,0:T(8,128)(2,1)S(1)} %get-tuple-element.51), channel_id=1, source_target_pairs={{0,14},{1,15},{2,4},{3,5},{4,2},{5,3},{6,8},{7,9},{8,6},{9,7},{10,... | collective-permute-start | bytes 737288 | tf_op jit(solution)/shard_map/ppermute | solution.py:25
  16.6 14.4 %collective-permute-start.6 = (f32[256,128]{1,0:T(8,128)S(1)}, f32[256,128]{1,0:T(8,128)S(1)}, u32[]{:S(2)}, u32[]{:S(2)}) collective-permute-start(f32[256,128]{1,0:T(8,128)S(1)} %get-tuple-element.88), channel_id=1, source_target_pairs={{0,3},{1,2},{2,1},{3,0},{4,7},{5,6},{6,5},{7,4},{8,11},{9,10},{10,... | collective-permute-start | bytes 393224 | tf_op jit(solution)/shard_map/ppermute | solution.py:25
  31.0 4.3 %collective-permute-start.7 = (f32[128,128]{1,0:T(8,128)S(1)}, f32[128,128]{1,0:T(8,128)S(1)}, u32[]{:S(2)}, u32[]{:S(2)}) collective-permute-start(f32[128,128]{1,0:T(8,128)S(1)} %slice_add_fusion), channel_id=1, source_target_pairs={{0,1},{1,0},{2,3},{3,2},{4,5},{5,4},{6,7},{7,6},{8,9},{9,8},{10,11... | collective-permute-start | bytes 196616 | tf_op jit(solution)/shard_map/ppermute | solution.py:25
  35.4 4.6 %collective-permute-start.8 = (f32[128,128]{1,0:T(8,128)S(1)}, f32[128,128]{1,0:T(8,128)S(1)}, u32[]{:S(2)}, u32[]{:S(2)}) collective-permute-start(f32[128,128]{1,0:T(8,128)S(1)} %fusion), channel_id=1, source_target_pairs={{0,32},{16,48},{32,0},{48,16},{64,96},{80,112},{96,64},{112,80},{1... | collective-permute-start | bytes 196616 | tf_op jit(solution)/shard_map/ppermute | solution.py:25
  39.2 11.6 %collective-permute-start.4 = (bf16[960,128]{1,0:T(8,128)(2,1)S(1)}, bf16[960,128]{1,0:T(8,128)(2,1)S(1)}, u32[]{:S(2)}, u32[]{:S(2)}) collective-permute-start(bf16[960,128]{1,0:T(8,128)(2,1)S(1)} %get-tuple-element.52), channel_id=1, source_target_pairs={{0,16},{16,0},{32,48},{48,32},{64,80},{80,64},{96,112},{112,96},{1... | collective-permute-start | bytes 737288 | tf_op jit(solution)/shard_map/ppermute | solution.py:25
  39.9 10.8 %collective-permute-start.5 = (bf16[960,128]{1,0:T(8,128)(2,1)S(1)}, bf16[960,128]{1,0:T(8,128)(2,1)S(1)}, u32[]{:S(2)}, u32[]{:S(2)}) collective-permute-start(bf16[960,128]{1,0:T(8,128)(2,1)S(1)} %get-tuple-element.53), channel_id=1, source_target_pairs={{0,112},{16,32},{32,16},{48,64},{64,48},{80,96},{96,80},{112,0},{1... | collective-permute-start | bytes 737288 | tf_op jit(solution)/shard_map/ppermute | solution.py:25
  41.6 7.7 %collective-permute-start.9 = (f32[256,128]{1,0:T(8,128)S(1)}, f32[256,128]{1,0:T(8,128)S(1)}, u32[]{:S(2)}, u32[]{:S(2)}) collective-permute-start(f32[256,128]{1,0:T(8,128)S(1)} %pad_maximum_fusion.refs_0_), channel_id=1, source_target_pairs={{0,96},{16,112},{32,64},{48,80},{64,32},{80,48},{96,0},{112,16},{1... | collective-permute-start | bytes 393224 | tf_op jit(solution)/shard_map/ppermute | solution.py:25
  44.2 5.1 %copy-start.3 = (f32[256,256]{1,0:T(8,128)S(1)}, f32[256,256]{1,0:T(8,128)}, u32[]{:S(2)}) copy-start(f32[256,256]{1,0:T(8,128)} %refs_2_.17) | copy-start | bytes 786436
  50.6 1.3 %collective-permute-start.10 = (f32[128,128]{1,0:T(8,128)S(1)}, f32[128,128]{1,0:T(8,128)S(1)}, u32[]{:S(2)}, u32[]{:S(2)}) collective-permute-start(f32[128,128]{1,0:T(8,128)S(1)} %get-tuple-element.90), channel_id=1, source_target_pairs={{0,16},{16,0},{32,48},{48,32},{64,80},{80,64},{96,112},{112,96},{1... | collective-permute-start | bytes 196616 | tf_op jit(solution)/shard_map/ppermute | solution.py:25
  51.9 4.6 %collective-permute-start.11 = (f32[128,128]{1,0:T(8,128)S(1)}, f32[128,128]{1,0:T(8,128)S(1)}, u32[]{:S(2)}, u32[]{:S(2)}) collective-permute-start(f32[128,128]{1,0:T(8,128)S(1)} %add.21), channel_id=1, source_target_pairs={{0,4},{1,5},{2,6},{3,7},{4,0},{5,1},{6,2},{7,3},{8,12},{9,13},{10,... | collective-permute-start | bytes 196616 | tf_op jit(solution)/shard_map/ppermute | solution.py:25
  56.5 5.6 %collective-permute-start.12 = (f32[128,128]{1,0:T(8,128)S(1)}, f32[128,128]{1,0:T(8,128)S(1)}, u32[]{:S(2)}, u32[]{:S(2)}) collective-permute-start(f32[128,128]{1,0:T(8,128)S(1)} %add.22), channel_id=1, source_target_pairs={{0,12},{1,13},{2,14},{3,15},{4,8},{5,9},{6,10},{7,11},{8,4},{9,5},... | collective-permute-start | bytes 196616 | tf_op jit(solution)/shard_map/ppermute | solution.py:25
  62.1 4.0 %collective-permute-start.13 = (bf16[128,128]{1,0:T(8,128)(2,1)S(1)}, bf16[128,128]{1,0:T(8,128)(2,1)S(1)}, u32[]{:S(2)}, u32[]{:S(2)}) collective-permute-start(bf16[128,128]{1,0:T(8,128)(2,1)S(1)} %add_convert_fusion), channel_id=1, source_target_pairs={{0,1},{1,0},{2,3},{3,2},{4,5},{5,4},{6,7},{7,6},{8,9},{9,8},{10,11... | collective-permute-start | bytes 98312 | tf_op jit(solution)/shard_map/ppermute | solution.py:25
  66.1 5.8 %collective-permute-start.14 = (bf16[256,128]{1,0:T(8,128)(2,1)S(1)}, bf16[256,128]{1,0:T(8,128)(2,1)S(1)}, u32[]{:S(2)}, u32[]{:S(2)}) collective-permute-start(bf16[256,128]{1,0:T(8,128)(2,1)S(1)} %pad_maximum_fusion.1.refs_12_), channel_id=1, source_target_pairs={{0,3},{1,2},{2,1},{3,0},{4,7},{5,6},{6,5},{7,4},{8,11},{9,10},{10,... | collective-permute-start | bytes 196616 | tf_op jit(solution)/shard_map/ppermute | solution.py:25
  69.6 2.2 %copy-start.4 = (bf16[2,240,240]{2,1,0:T(8,128)(2,1)S(1)}, bf16[2,240,240]{2,1,0:T(8,128)(2,1)}, u32[]{:S(2)}) copy-start(bf16[2,240,240]{2,1,0:T(8,128)(2,1)} %refs_14_.1) | copy-start | bytes 691204
  69.7 2.2 %copy-start.5 = (f32[2,240]{1,0:T(2,128)S(1)}, f32[2,240]{1,0:T(2,128)}, u32[]{:S(2)}) copy-start(f32[2,240]{1,0:T(2,128)} %refs_18_.1) | copy-start | bytes 5764
  69.7 2.2 %copy-start.6 = (s32[128]{0:T(128)S(1)}, s32[128]{0:T(128)}, u32[]{:S(2)}) copy-start(s32[128]{0:T(128)} %param.22) | copy-start | bytes 1540
  69.7 2.3 %copy-start.7 = (s32[128]{0:T(128)S(1)}, s32[128]{0:T(128)}, u32[]{:S(2)}) copy-start(s32[128]{0:T(128)} %param.21) | copy-start | bytes 1540
  (1 other events, 2.2 us)

commit v4 on v3

--- a/solution.py
+++ b/solution.py
@@ -49,8 +49,8 @@
     coef, rot, send, crot, cid, up, xs, sel, whole, sems = rest[16:]
     pairs = ((coef_h, coef), (rot_h, rot), (send_h, send), (crot_h, crot), (cid_h, cid), (up_h, up))
     copies = [pltpu.make_async_copy(src, dst, sems.at[i]) for i, (src, dst) in enumerate(pairs)]
-    for copy in copies:
-        copy.start()
+    for i in (2, 3, 4, 0, 1, 5):
+        copies[i].start()
     n_x, n_k, n_i = coef.shape
     n_r = rot.shape[0]
     for i in (2, 3, 4):
@@ -193,31 +193,31 @@
     coupling, own, other = refs[2:]
     me = lax.axis_index("grp")
     lanes = iota((32, 128), 1)
-    outs = []
+    rows = []
     for target in (me, lax.bitwise_xor(me, 1)):
         row_at = pl.multiple_of(target * 32, 32)
-        total = jnp.zeros((128, 128), F32)
-        for k, flip in enumerate((0, 2, 6, 4)):
+        lines = [[] for _ in range(4)]
+        for flip in (0, 2, 6, 4):
             gs = lax.bitwise_xor(me, flip)
             col_at = pl.multiple_of(gs // 4 * 128, 128)
             window = coupling[pl.ds(row_at, 32), pl.ds(col_at, 128)]
             same = lanes + col_at == iota((32, 128), 0) + row_at
             window = jnp.where(same, 0.0, window)
-            parts = []
             for q in range(4):
                 by = lax.rem(q * 32 + 128 - lax.rem(gs, 4) * 32, 128)
                 turned = pltpu.roll(window, by, 1)
-                parts.append(jnp.where((lanes >= q * 32) & (lanes < q * 32 + 32), turned, 0.0))
-            total = total + lax.dot_general(
-                halves[k // 2][k % 2 * 128 : k % 2 * 128 + 128, :],
-                jnp.concatenate(parts, axis=0),
-                (((1,), (1,)), ((), ())),
-                preferred_element_type=F32,
-                precision=lax.Precision.HIGHEST,
-            )
-        outs.append(total)
-    own[...] = outs[0]
-    other[...] = outs[1]
+                lines[q].append(jnp.where((lanes >= q * 32) & (lanes < q * 32 + 32), turned, 0.0))
+        rows += [jnp.concatenate(line, axis=1) for line in lines]
+    blocks = [half[at : at + 128, :] for half in halves for at in (0, 128)]
+    both = lax.dot_general(
+        jnp.concatenate(blocks, axis=1),
+        jnp.concatenate(rows, axis=0),
+        (((1,), (1,)), ((), ())),
+        preferred_element_type=F32,
+        precision=lax.Precision.HIGHEST,
+    )
+    own[...] = both[:, :128]
+    other[...] = both[:, 128:]
 
 
 def final_kernel(*refs):

time: 75.6 us -> 74.9 us (level)
  transfers between devices with their start and end apart: 15 -> 15, of which waited for: 8 -> 8; matrix products, arithmetic and copies ran while one was open for 0% -> 0% of each run, Pallas kernels for 35% -> 34%
where the time goes in v4:
time: 74.9 us; the launch traced here: 74.5 us
  Pallas kernels  34.5 us (46%)
  starting transfers between devices  24.4 us (33%)
  waiting for transfers between devices  15.2 us (20%)
    ppermute x15, starting transfers between devices, moved_by(): return lax.ppermute(value, axis, [(i, target(i)) for i in range(length)])  24.4 us
    pallas_call x8, Pallas kernels, on_device(): pl.pallas_call(lambda *refs, r=r: own_kernel(r, *refs), out_shape=[sds((2...  15.5 us
    ppermute x15, waiting for transfers between devices, moved_by(): return lax.ppermute(value, axis, [(i, target(i)) for i in range(length)])  15.2 us
    pallas_call x4, Pallas kernels, on_device(): pl.pallas_call(recv_kernel, out_shape=sds((2, 240, 1024), F32), in_specs=...  5.89 us
    pallas_call x1, Pallas kernels, on_device(): pl.pallas_call(send_kernel, out_shape=[sds((1920, 128), BF)] * 8 + [sds((...  5.74 us
    pallas_call x3, Pallas kernels, on_device(): pl.pallas_call(lift_kernel, out_shape=sds((1920, 384), BF), in_specs=[VM]...  3.31 us
    pallas_call x1, Pallas kernels, on_device(): pl.pallas_call(final_kernel, out_shape=sds((8, 240, 128), F32), in_specs=...  3.22 us
  transfers between devices with their start and end apart: 15, of which 8 were waited for; matrix products, arithmetic and copies ran while one was open for 0% of the time, Pallas kernels for 34%

profile of v4, /device:TPU:0, one launch (start us, length us, event | category | flops | bytes accessed | tf_op | source)
XLA Modules:
  0.0 74.5 jit_solution(11020585304494594267)
XLA Ops:
  0.0 5.7 %send.1 = (bf16[1920,128]{1,0:T(8,128)(2,1)S(1)}, bf16[1920,128]{1,0:T(8,128)(2,1)S(1)}, bf16[1920,128]{1,0:T(8,128)(2,1)S(1)}, bf16[1920,128]{1,0:T(8,128)(2,1)...) custom-call(f32[8,240,128]{2,1,0:T(8,128)} %coef_h.1, ...), custom_call_target="tpu_custom_call" | custom-call | tf_op jit(solution)/shard_map/send/pallas_call | solution.py:283
  5.8 1.7 %collective-permute-start = (bf16[960,128]{1,0:T(8,128)(2,1)S(1)}, bf16[960,128]{1,0:T(8,128)(2,1)S(1)}, u32[]{:S(2)}, u32[]{:S(2)}) collective-permute-start(bf16[960,128]{1,0:T(8,128)(2,1)S(1)} %get-tuple-element.48), channel_id=1, source_target_pairs={{0,1},{1,0},{2,3},{3,2},{4,5},{5,4},{6,7},{7,6},{8,9},{9,8},{10,11... | collective-permute-start | bytes 737288 | tf_op jit(solution)/shard_map/ppermute | solution.py:25
  7.5 5.6 %collective-permute-start.1 = (bf16[960,128]{1,0:T(8,128)(2,1)S(1)}, bf16[960,128]{1,0:T(8,128)(2,1)S(1)}, u32[]{:S(2)}, u32[]{:S(2)}) collective-permute-start(bf16[960,128]{1,0:T(8,128)(2,1)S(1)} %get-tuple-element.49), channel_id=1, source_target_pairs={{0,15},{1,2},{2,1},{3,4},{4,3},{5,6},{6,5},{7,8},{8,7},{9,10},{10,... | collective-permute-start | bytes 737288 | tf_op jit(solution)/shard_map/ppermute | solution.py:25
  13.0 3.4 %collective-permute-start.3 = (bf16[960,128]{1,0:T(8,128)(2,1)S(1)}, bf16[960,128]{1,0:T(8,128)(2,1)S(1)}, u32[]{:S(2)}, u32[]{:S(2)}) collective-permute-start(bf16[960,128]{1,0:T(8,128)(2,1)S(1)} %get-tuple-element.51), channel_id=1, source_target_pairs={{0,14},{1,15},{2,4},{3,5},{4,2},{5,3},{6,8},{7,9},{8,6},{9,7},{10,... | collective-permute-start | bytes 737288 | tf_op jit(solution)/shard_map/ppermute | solution.py:25
  16.9 2.0 %shard_map.130 = (f32[240,1024]{1,0:T(8,128)S(1)}, bf16[1152,128]{1,0:T(8,128)(2,1)S(1)}, bf16[240,256]{1,0:T(8,128)(2,1)S(1)}, bf16[480,768]{1,0:T(8,128)(2,1)S(1)}) custom-call(bf16[1920,128]{1,0:T(8,128)(2,1)S(1)} %get-tuple-element.54.refs_0_, s32[24,128]{1,0:T(8,128)S(1)} %copy-done.8, s32[24,128]{1,0:T(8,128)S(1)} %copy-done.9, ...), custom_call_target="tpu_custom_call" | custom-call | flops 1260000000 | bytes 3000000 | tf_op jit(solution)/shard_map/pallas_call | solution.py:339
  18.9 1.9 %shard_map.131 = (f32[240,1024]{1,0:T(8,128)S(1)}, bf16[1152,128]{1,0:T(8,128)(2,1)S(1)}, bf16[240,256]{1,0:T(8,128)(2,1)S(1)}) custom-call(bf16[1920,128]{1,0:T(8,128)(2,1)S(1)} %get-tuple-element.56.refs_0_, s32[24,128]{1,0:T(8,128)S(1)} %copy-done.8, s32[24,128]{1,0:T(8,128)S(1)} %copy-done.9, bf16[8,240,240]{2,1,0:T(8,128)(2,1)S(1)} %copy-done.1, ...), custom_call_target="tpu_custom_call" | custom-call | flops 1260000000 | bytes 3000000 | tf_op jit(solution)/shard_map/pallas_call | solution.py:339
  20.9 1.9 %shard_map.133 = (f32[240,1024]{1,0:T(8,128)S(1)}, bf16[1152,128]{1,0:T(8,128)(2,1)S(1)}, bf16[240,256]{1,0:T(8,128)(2,1)S(1)}) custom-call(bf16[1920,128]{1,0:T(8,128)(2,1)S(1)} %get-tuple-element.61.refs_0_, s32[24,128]{1,0:T(8,128)S(1)} %copy-done.8, s32[24,128]{1,0:T(8,128)S(1)} %copy-done.9, bf16[8,240,240]{2,1,0:T(8,128)(2,1)S(1)} %copy-done.1, ...), custom_call_target="tpu_custom_call" | custom-call | flops 1260000000 | bytes 3000000 | tf_op jit(solution)/shard_map/pallas_call | solution.py:339
  22.8 1.9 %shard_map.134 = (f32[240,1024]{1,0:T(8,128)S(1)}, bf16[1152,128]{1,0:T(8,128)(2,1)S(1)}, bf16[240,256]{1,0:T(8,128)(2,1)S(1)}) custom-call(bf16[1920,128]{1,0:T(8,128)(2,1)S(1)} %get-tuple-element.63.refs_0_, s32[24,128]{1,0:T(8,128)S(1)} %copy-done.8, s32[24,128]{1,0:T(8,128)S(1)} %copy-done.9, bf16[8,240,240]{2,1,0:T(8,128)(2,1)S(1)} %copy-done.1, ...), custom_call_target="tpu_custom_call" | custom-call | flops 1260000000 | bytes 3000000 | tf_op jit(solution)/shard_map/pallas_call | solution.py:339
  24.7 1.9 %shard_map.136 = (f32[240,1024]{1,0:T(8,128)S(1)}, bf16[1152,128]{1,0:T(8,128)(2,1)S(1)}, bf16[240,256]{1,0:T(8,128)(2,1)S(1)}) custom-call(bf16[1920,128]{1,0:T(8,128)(2,1)S(1)} %get-tuple-element.67.refs_0_, s32[24,128]{1,0:T(8,128)S(1)} %copy-done.8, s32[24,128]{1,0:T(8,128)S(1)} %copy-done.9, bf16[8,240,240]{2,1,0:T(8,128)(2,1)S(1)} %copy-done.1, ...), custom_call_target="tpu_custom_call" | custom-call | flops 1260000000 | bytes 3000000 | tf_op jit(solution)/shard_map/pallas_call | solution.py:339
  26.7 1.9 %shard_map.137 = (f32[240,1024]{1,0:T(8,128)S(1)}, bf16[1152,128]{1,0:T(8,128)(2,1)S(1)}, bf16[240,256]{1,0:T(8,128)(2,1)S(1)}) custom-call(bf16[1920,128]{1,0:T(8,128)(2,1)S(1)} %get-tuple-element.69.refs_0_, s32[24,128]{1,0:T(8,128)S(1)} %copy-done.8, s32[24,128]{1,0:T(8,128)S(1)} %copy-done.9, bf16[8,240,240]{2,1,0:T(8,128)(2,1)S(1)} %copy-done.1, ...), custom_call_target="tpu_custom_call" | custom-call | flops 1260000000 | bytes 3000000 | tf_op jit(solution)/shard_map/pallas_call | solution.py:339
  28.6 2.2 %collective-permute-done.6 = f32[256,128]{1,0:T(8,128)S(1)} collective-permute-done((f32[256,128]{1,0:T(8,128)S(1)}, f32[256,128]{1,0:T(8,128)S(1)}, u32[]{:S(2)}, u32[]{:S(2)}) %collective-permute-start.6) | collective-permute-done | bytes 131104 | tf_op jit(solution)/shard_map/ppermute | solution.py:25
  30.9 1.9 %shard_map.139 = (f32[240,1024]{1,0:T(8,128)S(1)}, bf16[1152,128]{1,0:T(8,128)(2,1)S(1)}, bf16[240,256]{1,0:T(8,128)(2,1)S(1)}) custom-call(bf16[1920,128]{1,0:T(8,128)(2,1)S(1)} %get-tuple-element.73.refs_0_, s32[24,128]{1,0:T(8,128)S(1)} %copy-done.8, s32[24,128]{1,0:T(8,128)S(1)} %copy-done.9, bf16[8,240,240]{2,1,0:T(8,128)(2,1)S(1)} %copy-done.1, ...), custom_call_target="tpu_custom_call" | custom-call | flops 1260000000 | bytes 3000000 | tf_op jit(solution)/shard_map/pallas_call | solution.py:339
  32.9 2.3 %collective-permute-done.7 = f32[128,128]{1,0:T(8,128)S(1)} collective-permute-done((f32[128,128]{1,0:T(8,128)S(1)}, f32[128,128]{1,0:T(8,128)S(1)}, u32[]{:S(2)}, u32[]{:S(2)}) %collective-permute-start.7) | collective-permute-done | bytes 65568 | tf_op jit(solution)/shard_map/ppermute | solution.py:25
  35.2 1.9 %collective-permute-start.8 = (f32[128,128]{1,0:T(8,128)S(1)}, f32[128,128]{1,0:T(8,128)S(1)}, u32[]{:S(2)}, u32[]{:S(2)}) collective-permute-start(f32[128,128]{1,0:T(8,128)S(1)} %fusion), channel_id=1, source_target_pairs={{0,32},{16,48},{32,0},{48,16},{64,96},{80,112},{96,64},{112,80},{1... | collective-permute-start | bytes 196616 | tf_op jit(solution)/shard_map/ppermute | solution.py:25
  37.1 1.9 %shard_map.140 = (f32[240,1024]{1,0:T(8,128)S(1)}, bf16[1152,128]{1,0:T(8,128)(2,1)S(1)}, bf16[240,256]{1,0:T(8,128)(2,1)S(1)}) custom-call(bf16[1920,128]{1,0:T(8,128)(2,1)S(1)} %get-tuple-element.75.refs_0_, s32[24,128]{1,0:T(8,128)S(1)} %copy-done.8, s32[24,128]{1,0:T(8,128)S(1)} %copy-done.9, bf16[8,240,240]{2,1,0:T(8,128)(2,1)S(1)} %copy-done.1, ...), custom_call_target="tpu_custom_call" | custom-call | flops 1260000000 | bytes 3000000 | tf_op jit(solution)/shard_map/pallas_call | solution.py:339
  39.8 1.6 %collective-permute-start.5 = (bf16[960,128]{1,0:T(8,128)(2,1)S(1)}, bf16[960,128]{1,0:T(8,128)(2,1)S(1)}, u32[]{:S(2)}, u32[]{:S(2)}) collective-permute-start(bf16[960,128]{1,0:T(8,128)(2,1)S(1)} %get-tuple-element.53), channel_id=1, source_target_pairs={{0,112},{16,32},{32,16},{48,64},{64,48},{80,96},{96,80},{112,0},{1... | collective-permute-start | bytes 737288 | tf_op jit(solution)/shard_map/ppermute | solution.py:25
  45.1 3.9 %collective-permute-done.9.refs_1_ = f32[256,128]{1,0:T(8,128)S(1)} collective-permute-done((f32[256,128]{1,0:T(8,128)S(1)}, f32[256,128]{1,0:T(8,128)S(1)}, u32[]{:S(2)}, u32[]{:S(2)}) %collective-permute-start.9) | collective-permute-done | bytes 131104 | tf_op jit(solution)/shard_map/ppermute | solution.py:25
  51.2 2.0 %collective-permute-start.11 = (f32[128,128]{1,0:T(8,128)S(1)}, f32[128,128]{1,0:T(8,128)S(1)}, u32[]{:S(2)}, u32[]{:S(2)}) collective-permute-start(f32[128,128]{1,0:T(8,128)S(1)} %add.21), channel_id=1, source_target_pairs={{0,4},{1,5},{2,6},{3,7},{4,0},{5,1},{6,2},{7,3},{8,12},{9,13},{10,... | collective-permute-start | bytes 196616 | tf_op jit(solution)/shard_map/ppermute | solution.py:25
  55.9 2.3 %collective-permute-start.12 = (f32[128,128]{1,0:T(8,128)S(1)}, f32[128,128]{1,0:T(8,128)S(1)}, u32[]{:S(2)}, u32[]{:S(2)}) collective-permute-start(f32[128,128]{1,0:T(8,128)S(1)} %add.22), channel_id=1, source_target_pairs={{0,12},{1,13},{2,14},{3,15},{4,8},{5,9},{6,10},{7,11},{8,4},{9,5},... | collective-permute-start | bytes 196616 | tf_op jit(solution)/shard_map/ppermute | solution.py:25
  59.6 1.8 %collective-permute-done.12 = f32[128,128]{1,0:T(8,128)S(1)} collective-permute-done((f32[128,128]{1,0:T(8,128)S(1)}, f32[128,128]{1,0:T(8,128)S(1)}, u32[]{:S(2)}, u32[]{:S(2)}) %collective-permute-start.12) | collective-permute-done | bytes 65568 | tf_op jit(solution)/shard_map/ppermute | solution.py:25
  63.0 2.4 %collective-permute-done.13 = bf16[128,128]{1,0:T(8,128)(2,1)S(1)} collective-permute-done((bf16[128,128]{1,0:T(8,128)(2,1)S(1)}, bf16[128,128]{1,0:T(8,128)(2,1)S(1)}, u32[]{:S(2)}, u32[]{:S(2)}) %collective-permute-start.13) | collective-permute-done | bytes 32800 | tf_op jit(solution)/shard_map/ppermute | solution.py:25
  65.4 3.5 %collective-permute-start.14 = (bf16[256,128]{1,0:T(8,128)(2,1)S(1)}, bf16[256,128]{1,0:T(8,128)(2,1)S(1)}, u32[]{:S(2)}, u32[]{:S(2)}) collective-permute-start(bf16[256,128]{1,0:T(8,128)(2,1)S(1)} %pad_maximum_fusion.1.refs_12_), channel_id=1, source_target_pairs={{0,3},{1,2},{2,1},{3,0},{4,7},{5,6},{6,5},{7,4},{8,11},{9,10},{10,... | collective-permute-start | bytes 196616 | tf_op jit(solution)/shard_map/ppermute | solution.py:25
  69.0 1.5 %shard_map.141.refs_3_ = f32[2,240,1024]{2,1,0:T(8,128)S(1)} custom-call(bf16[1920,384]{1,0:T(8,128)(2,1)S(1)} %shard_map.127.m0, bf16[1920,384]{1,0:T(8,128)(2,1)S(1)} %shard_map.128.m1, bf16[1920,384]{1,0:T(8,128)(2,1)S(1)} %shard_map.129.m2, bf16[1152,128]{1,0:T(8,128)(2,1)S(1)} %get-tuple-element.74.sel_a, ...), custom_call_target="tpu_custom_call" | custom-call | flops 1200000000 | bytes 8000000 | tf_op jit(solution)/shard_map/pallas_call | solution.py:370
  71.2 3.2 %final.1 = f32[8,240,128]{2,1,0:T(8,128)} custom-call(f32[2,240,1024]{2,1,0:T(8,128)S(1)} %shard_map.132.refs_0_, f32[2,240,1024]{2,1,0:T(8,128)S(1)} %shard_map.135.refs_1_, f32[2,240,1024]{2,1,0:T(8,128)S(1)} %shard_map.138.refs_2_, f32[2,240,1024]{2,1,0:T(8,128)S(1)} %shard_map.141.refs_3_, bf16[240,256]{1,0:T(8,128)(2,1)S(1)} %get-tuple-element.79.refs_4_, ...), custom_call_target="tpu_custom_call" | custom-call | tf_op jit(solution)/shard_map/final/pallas_call | solution.py:379
  (51 shorter events, 13.7 us)
Async XLA Ops:
  0.0 16.9 %copy-start.1 = (bf16[8,240,240]{2,1,0:T(8,128)(2,1)S(1)}, bf16[8,240,240]{2,1,0:T(8,128)(2,1)}, u32[]{:S(2)}) copy-start(bf16[8,240,240]{2,1,0:T(8,128)(2,1)} %refs_3_.15) | copy-start | bytes 2764804
  0.0 16.9 %copy-start = (bf16[3,2,240,240]{3,2,1,0:T(8,128)(2,1)S(1)}, bf16[3,2,240,240]{3,2,1,0:T(8,128)(2,1)}, u32[]{:S(2)}) copy-start(bf16[3,2,240,240]{3,2,1,0:T(8,128)(2,1)} %refs_4_.1) | copy-start | bytes 2073604
  0.0 16.9 %copy-start.8 = (s32[24,128]{1,0:T(8,128)S(1)}, s32[24,128]{1,0:T(8,128)}, u32[]{:S(2)}) copy-start(s32[24,128]{1,0:T(8,128)} %refs_1_.15) | copy-start | bytes 36868
  0.0 16.9 %copy-start.9 = (s32[24,128]{1,0:T(8,128)S(1)}, s32[24,128]{1,0:T(8,128)}, u32[]{:S(2)}) copy-start(s32[24,128]{1,0:T(8,128)} %refs_2_.16) | copy-start | bytes 36868
  5.8 33.3 %collective-permute-start = (bf16[960,128]{1,0:T(8,128)(2,1)S(1)}, bf16[960,128]{1,0:T(8,128)(2,1)S(1)}, u32[]{:S(2)}, u32[]{:S(2)}) collective-permute-start(bf16[960,128]{1,0:T(8,128)(2,1)S(1)} %get-tuple-element.48), channel_id=1, source_target_pairs={{0,1},{1,0},{2,3},{3,2},{4,5},{5,4},{6,7},{7,6},{8,9},{9,8},{10,11... | collective-permute-start | bytes 737288 | tf_op jit(solution)/shard_map/ppermute | solution.py:25
  7.5 34.0 %collective-permute-start.1 = (bf16[960,128]{1,0:T(8,128)(2,1)S(1)}, bf16[960,128]{1,0:T(8,128)(2,1)S(1)}, u32[]{:S(2)}, u32[]{:S(2)}) collective-permute-start(bf16[960,128]{1,0:T(8,128)(2,1)S(1)} %get-tuple-element.49), channel_id=1, source_target_pairs={{0,15},{1,2},{2,1},{3,4},{4,3},{5,6},{6,5},{7,8},{8,7},{9,10},{10,... | collective-permute-start | bytes 737288 | tf_op jit(solution)/shard_map/ppermute | solution.py:25
  13.0 31.0 %collective-permute-start.2 = (bf16[960,128]{1,0:T(8,128)(2,1)S(1)}, bf16[960,128]{1,0:T(8,128)(2,1)S(1)}, u32[]{:S(2)}, u32[]{:S(2)}) collective-permute-start(bf16[960,128]{1,0:T(8,128)(2,1)S(1)} %get-tuple-element.50), channel_id=1, source_target_pairs={{0,2},{1,3},{2,0},{3,1},{4,6},{5,7},{6,4},{7,5},{8,10},{9,11},{10,... | collective-permute-start | bytes 737288 | tf_op jit(solution)/shard_map/ppermute | solution.py:25
  13.0 31.0 %collective-permute-start.3 = (bf16[960,128]{1,0:T(8,128)(2,1)S(1)}, bf16[960,128]{1,0:T(8,128)(2,1)S(1)}, u32[]{:S(2)}, u32[]{:S(2)}) collective-permute-start(bf16[960,128]{1,0:T(8,128)(2,1)S(1)} %get-tuple-element.51), channel_id=1, source_target_pairs={{0,14},{1,15},{2,4},{3,5},{4,2},{5,3},{6,8},{7,9},{8,6},{9,7},{10,... | collective-permute-start | bytes 737288 | tf_op jit(solution)/shard_map/ppermute | solution.py:25
  16.4 14.4 %collective-permute-start.6 = (f32[256,128]{1,0:T(8,128)S(1)}, f32[256,128]{1,0:T(8,128)S(1)}, u32[]{:S(2)}, u32[]{:S(2)}) collective-permute-start(f32[256,128]{1,0:T(8,128)S(1)} %get-tuple-element.88), channel_id=1, source_target_pairs={{0,3},{1,2},{2,1},{3,0},{4,7},{5,6},{6,5},{7,4},{8,11},{9,10},{10,... | collective-permute-start | bytes 393224 | tf_op jit(solution)/shard_map/ppermute | solution.py:25
  30.8 4.3 %collective-permute-start.7 = (f32[128,128]{1,0:T(8,128)S(1)}, f32[128,128]{1,0:T(8,128)S(1)}, u32[]{:S(2)}, u32[]{:S(2)}) collective-permute-start(f32[128,128]{1,0:T(8,128)S(1)} %slice_add_fusion), channel_id=1, source_target_pairs={{0,1},{1,0},{2,3},{3,2},{4,5},{5,4},{6,7},{7,6},{8,9},{9,8},{10,11... | collective-permute-start | bytes 196616 | tf_op jit(solution)/shard_map/ppermute | solution.py:25
  35.2 4.6 %collective-permute-start.8 = (f32[128,128]{1,0:T(8,128)S(1)}, f32[128,128]{1,0:T(8,128)S(1)}, u32[]{:S(2)}, u32[]{:S(2)}) collective-permute-start(f32[128,128]{1,0:T(8,128)S(1)} %fusion), channel_id=1, source_target_pairs={{0,32},{16,48},{32,0},{48,16},{64,96},{80,112},{96,64},{112,80},{1... | collective-permute-start | bytes 196616 | tf_op jit(solution)/shard_map/ppermute | solution.py:25
  39.0 11.1 %collective-permute-start.4 = (bf16[960,128]{1,0:T(8,128)(2,1)S(1)}, bf16[960,128]{1,0:T(8,128)(2,1)S(1)}, u32[]{:S(2)}, u32[]{:S(2)}) collective-permute-start(bf16[960,128]{1,0:T(8,128)(2,1)S(1)} %get-tuple-element.52), channel_id=1, source_target_pairs={{0,16},{16,0},{32,48},{48,32},{64,80},{80,64},{96,112},{112,96},{1... | collective-permute-start | bytes 737288 | tf_op jit(solution)/shard_map/ppermute | solution.py:25
  39.8 10.4 %collective-permute-start.5 = (bf16[960,128]{1,0:T(8,128)(2,1)S(1)}, bf16[960,128]{1,0:T(8,128)(2,1)S(1)}, u32[]{:S(2)}, u32[]{:S(2)}) collective-permute-start(bf16[960,128]{1,0:T(8,128)(2,1)S(1)} %get-tuple-element.53), channel_id=1, source_target_pairs={{0,112},{16,32},{32,16},{48,64},{64,48},{80,96},{96,80},{112,0},{1... | collective-permute-start | bytes 737288 | tf_op jit(solution)/shard_map/ppermute | solution.py:25
  41.4 7.7 %collective-permute-start.9 = (f32[256,128]{1,0:T(8,128)S(1)}, f32[256,128]{1,0:T(8,128)S(1)}, u32[]{:S(2)}, u32[]{:S(2)}) collective-permute-start(f32[256,128]{1,0:T(8,128)S(1)} %pad_maximum_fusion.refs_0_), channel_id=1, source_target_pairs={{0,96},{16,112},{32,64},{48,80},{64,32},{80,48},{96,0},{112,16},{1... | collective-permute-start | bytes 393224 | tf_op jit(solution)/shard_map/ppermute | solution.py:25
  44.0 5.1 %copy-start.3 = (f32[256,256]{1,0:T(8,128)S(1)}, f32[256,256]{1,0:T(8,128)}, u32[]{:S(2)}) copy-start(f32[256,256]{1,0:T(8,128)} %refs_2_.17) | copy-start | bytes 786436
  49.9 1.3 %collective-permute-start.10 = (f32[128,128]{1,0:T(8,128)S(1)}, f32[128,128]{1,0:T(8,128)S(1)}, u32[]{:S(2)}, u32[]{:S(2)}) collective-permute-start(f32[128,128]{1,0:T(8,128)S(1)} %get-tuple-element.90), channel_id=1, source_target_pairs={{0,16},{16,0},{32,48},{48,32},{64,80},{80,64},{96,112},{112,96},{1... | collective-permute-start | bytes 196616 | tf_op jit(solution)/shard_map/ppermute | solution.py:25
  51.2 4.6 %collective-permute-start.11 = (f32[128,128]{1,0:T(8,128)S(1)}, f32[128,128]{1,0:T(8,128)S(1)}, u32[]{:S(2)}, u32[]{:S(2)}) collective-permute-start(f32[128,128]{1,0:T(8,128)S(1)} %add.21), channel_id=1, source_target_pairs={{0,4},{1,5},{2,6},{3,7},{4,0},{5,1},{6,2},{7,3},{8,12},{9,13},{10,... | collective-permute-start | bytes 196616 | tf_op jit(solution)/shard_map/ppermute | solution.py:25
  55.9 5.6 %collective-permute-start.12 = (f32[128,128]{1,0:T(8,128)S(1)}, f32[128,128]{1,0:T(8,128)S(1)}, u32[]{:S(2)}, u32[]{:S(2)}) collective-permute-start(f32[128,128]{1,0:T(8,128)S(1)} %add.22), channel_id=1, source_target_pairs={{0,12},{1,13},{2,14},{3,15},{4,8},{5,9},{6,10},{7,11},{8,4},{9,5},... | collective-permute-start | bytes 196616 | tf_op jit(solution)/shard_map/ppermute | solution.py:25
  61.4 4.0 %collective-permute-start.13 = (bf16[128,128]{1,0:T(8,128)(2,1)S(1)}, bf16[128,128]{1,0:T(8,128)(2,1)S(1)}, u32[]{:S(2)}, u32[]{:S(2)}) collective-permute-start(bf16[128,128]{1,0:T(8,128)(2,1)S(1)} %add_convert_fusion), channel_id=1, source_target_pairs={{0,1},{1,0},{2,3},{3,2},{4,5},{5,4},{6,7},{7,6},{8,9},{9,8},{10,11... | collective-permute-start | bytes 98312 | tf_op jit(solution)/shard_map/ppermute | solution.py:25
  65.4 5.8 %collective-permute-start.14 = (bf16[256,128]{1,0:T(8,128)(2,1)S(1)}, bf16[256,128]{1,0:T(8,128)(2,1)S(1)}, u32[]{:S(2)}, u32[]{:S(2)}) collective-permute-start(bf16[256,128]{1,0:T(8,128)(2,1)S(1)} %pad_maximum_fusion.1.refs_12_), channel_id=1, source_target_pairs={{0,3},{1,2},{2,1},{3,0},{4,7},{5,6},{6,5},{7,4},{8,11},{9,10},{10,... | collective-permute-start | bytes 196616 | tf_op jit(solution)/shard_map/ppermute | solution.py:25
  69.0 2.2 %copy-start.4 = (bf16[2,240,240]{2,1,0:T(8,128)(2,1)S(1)}, bf16[2,240,240]{2,1,0:T(8,128)(2,1)}, u32[]{:S(2)}) copy-start(bf16[2,240,240]{2,1,0:T(8,128)(2,1)} %refs_14_.1) | copy-start | bytes 691204
  69.0 2.2 %copy-start.5 = (f32[2,240]{1,0:T(2,128)S(1)}, f32[2,240]{1,0:T(2,128)}, u32[]{:S(2)}) copy-start(f32[2,240]{1,0:T(2,128)} %refs_18_.1) | copy-start | bytes 5764
  69.0 2.2 %copy-start.6 = (s32[128]{0:T(128)S(1)}, s32[128]{0:T(128)}, u32[]{:S(2)}) copy-start(s32[128]{0:T(128)} %param.22) | copy-start | bytes 1540
  69.0 2.3 %copy-start.7 = (s32[128]{0:T(128)S(1)}, s32[128]{0:T(128)}, u32[]{:S(2)}) copy-start(s32[128]{0:T(128)} %param.21) | copy-start | bytes 1540
  (1 other events, 2.2 us)
